TPU v7x, 32 devices: a whole 2x2x4 slice. The times are simulated.
32 devices in a mesh: rep: 4 (over x, core), fsdp: 8 (over z, y).
Axes of the slice: x: 2, y: 2, z: 4, core: 2. Of those that a mesh axis runs over, the one named last changes fastest.
Arguments:
- patches: bfloat16 [96, 167, 768], P(('rep', 'fsdp')), may hold values from -6 to 6
- mask_places: int32 [96, 100], P(('rep', 'fsdp')), may hold values from 0 to 166, as said below
- square_weights: float32 [6, 768, 768], P(None, 'fsdp')
- square_first: float32 [6, 768, 768], P(None, 'fsdp'), may hold values from -5.722046e-06 to 5.722046e-06
- square_second: float32 [6, 768, 768], P(None, 'fsdp'), may hold values from 3.5321272e-15 to 3.532127e-14
- square_teacher: float32 [6, 768, 768], P(None, 'fsdp')
- feed_weights: float32 [1, 2, 768, 3072], P(None, None, 'fsdp')
- feed_first: float32 [1, 2, 768, 3072], P(None, None, 'fsdp'), may hold values from -5.722046e-06 to 5.722046e-06
- feed_second: float32 [1, 2, 768, 3072], P(None, None, 'fsdp'), may hold values from 3.5321272e-15 to 3.532127e-14
- feed_teacher: float32 [1, 2, 768, 3072], P(None, None, 'fsdp')
- vector_weights: float32 [184, 768], P(None, 'fsdp')
- vector_first: float32 [184, 768], P(None, 'fsdp'), may hold values from -5.722046e-06 to 5.722046e-06
- vector_second: float32 [184, 768], P(None, 'fsdp'), may hold values from 3.5321272e-15 to 3.532127e-14
- vector_teacher: float32 [184, 768], P(None, 'fsdp')
Outputs:
- loss: float32 [], replicated
- clip_norm: float32 [], replicated
- square_step: float32 [6, 768, 768], P(None, 'fsdp')
- square_first_new: float32 [6, 768, 768], P(None, 'fsdp')
- square_second_new: float32 [6, 768, 768], P(None, 'fsdp')
- square_teacher_step: float32 [6, 768, 768], P(None, 'fsdp')
- feed_step: float32 [1, 2, 768, 3072], P(None, None, 'fsdp')
- feed_first_new: float32 [1, 2, 768, 3072], P(None, None, 'fsdp')
- feed_second_new: float32 [1, 2, 768, 3072], P(None, None, 'fsdp')
- feed_teacher_step: float32 [1, 2, 768, 3072], P(None, None, 'fsdp')
- vector_step: float32 [184, 768], P(None, 'fsdp')
- vector_first_new: float32 [184, 768], P(None, 'fsdp')
- vector_second_new: float32 [184, 768], P(None, 'fsdp')
- vector_teacher_step: float32 [184, 768], P(None, 'fsdp')
Inputs may be any that keep to these rules, and one draw needn't show every extreme that they name: `mask_places`: each row lists 100 different positions of its sample.
All inputs are finite; a program needn't handle non-finite values.
Results may differ from a plain program's by a relative error of at most 0.0015.
The roundings to bfloat16 on the way count: a program that leaves them out, or rounds other values in their place, can miss the bound.
Values may be sent and summed in bfloat16 or wider, within the bound.
No kernel may reach another device: no remote copies, remote signals or barrier semaphores. Data moves between devices by JAX's collectives and lax.ppermute only.
A program may use at most 320 MiB of HBM per device.

v0:
```python
import math

import jax
import jax.numpy as jnp
from jax import lax
from jax.sharding import PartitionSpec as P

HEADS = 12
ADAM_STEP = 10


ln_eps = 1e-05
beta_one = 0.9
beta_two = 0.999
adam_eps = 1e-08
learn_rate = 0.01
decay_rate = 0.05
ema_keep = 0.999
huber_delta = 1.0
clip_scale = 1.25


def to_low(values):
    return values.astype(jnp.bfloat16)


def matmul(left, right):
    return jnp.dot(left, right, preferred_element_type=jnp.float32)


def matmul_tn(left, right):
    return lax.dot_general(
        left, right, (((0,), (0,)), ((), ())), preferred_element_type=jnp.float32
    )


def matmul_nt(left, right):
    return lax.dot_general(
        left, right, (((1,), (1,)), ((), ())), preferred_element_type=jnp.float32
    )


def layer_norm(values, gain, shift):
    centred = values - jnp.mean(values, axis=-1, keepdims=True)
    variance = jnp.mean(centred * centred, axis=-1, keepdims=True)
    return centred * lax.rsqrt(variance + ln_eps) * gain + shift


def gelu_exact(values):
    return jax.nn.gelu(values, approximate=False)


def instance_norm(values, samples):
    blocks = values.reshape(samples, -1, values.shape[1])
    centred = blocks - jnp.mean(blocks, axis=1, keepdims=True)
    variance = jnp.mean(centred * centred, axis=1, keepdims=True)
    return (centred * lax.rsqrt(variance + ln_eps)).reshape(values.shape)


def split_heads(values, samples, head_count):
    row_count, model_width = values.shape
    return values.reshape(samples, row_count // samples, head_count, model_width // head_count)


def score_block(query_heads, key_heads):
    scaling = query_heads.shape[-1] ** (-0.5)
    return (
        jnp.einsum("sqhe,skhe->shqk", query_heads, key_heads, preferred_element_type=jnp.float32)
        * scaling
    )


def attention_forward(query, key_rows, value_rows, samples, head_count):
    query_heads = split_heads(query, samples, head_count)
    key_heads = split_heads(key_rows, samples, head_count)
    value_heads = split_heads(value_rows, samples, head_count)
    scores = score_block(query_heads, key_heads)
    highest = jnp.max(scores, axis=-1, keepdims=True)
    logsum = highest + jnp.log(jnp.sum(jnp.exp(scores - highest), axis=-1, keepdims=True))
    soft_weights = to_low(jnp.exp(scores - logsum))
    attended = jnp.einsum(
        "shqk,skhe->sqhe", soft_weights, value_heads, preferred_element_type=jnp.float32
    )
    return (to_low(attended.reshape(query.shape)), logsum)


def attention_backward(query, key_rows, value_rows, logsum, grad_attended, samples, head_count):
    query_heads = split_heads(query, samples, head_count)
    key_heads = split_heads(key_rows, samples, head_count)
    value_heads = split_heads(value_rows, samples, head_count)
    grad_heads = split_heads(grad_attended, samples, head_count)
    scaling = query_heads.shape[-1] ** (-0.5)
    soft_float = jnp.exp(score_block(query_heads, key_heads) - logsum)
    soft_weights = to_low(soft_float)
    grad_soft = jnp.einsum(
        "sqhe,skhe->shqk", grad_heads, value_heads, preferred_element_type=jnp.float32
    )
    grad_value = jnp.einsum(
        "shqk,sqhe->skhe", soft_weights, grad_heads, preferred_element_type=jnp.float32
    )
    grad_scores = to_low(
        soft_float * (grad_soft - jnp.sum(grad_soft * soft_float, axis=-1, keepdims=True))
    )
    grad_query = (
        jnp.einsum("shqk,skhe->sqhe", grad_scores, key_heads, preferred_element_type=jnp.float32)
        * scaling
    )
    grad_key = (
        jnp.einsum("shqk,sqhe->skhe", grad_scores, query_heads, preferred_element_type=jnp.float32)
        * scaling
    )
    shape_rows = query.shape
    return (
        to_low(grad_query.reshape(shape_rows)),
        to_low(grad_key.reshape(shape_rows)),
        to_low(grad_value.reshape(shape_rows)),
    )


def layer_forward(hidden, matrices, feed_pair, vector, base, samples, head_count):
    hidden_low = to_low(hidden)
    query = to_low(matmul(hidden_low, matrices[0]) + vector[base])
    key_rows = to_low(matmul(hidden_low, matrices[1]))
    value_rows = to_low(matmul(hidden_low, matrices[2]) + vector[base + 1])
    attended, logsum = attention_forward(query, key_rows, value_rows, samples, head_count)
    branch = matmul(attended, matrices[3]) + vector[base + 2]
    first_sum = hidden + branch
    normed = layer_norm(first_sum, vector[base + 3], vector[base + 4])
    pre_act = matmul(to_low(normed), feed_pair[0]) + vector[base + 8 : base + 12].reshape(-1)
    activation = to_low(gelu_exact(pre_act))
    branch_two = matmul_nt(activation, feed_pair[1]) + vector[base + 5]
    second_sum = normed + branch_two
    result = layer_norm(second_sum, vector[base + 6], vector[base + 7])
    kept_state = (
        hidden,
        query,
        key_rows,
        value_rows,
        attended,
        logsum,
        first_sum,
        pre_act,
        second_sum,
    )
    return (result, branch_two, kept_state)


def layer_backward(grad_result, kept_state, matrices, feed_pair, vector, base, samples, head_count):
    hidden, query, key_rows, value_rows, attended, logsum, first_sum, pre_act, second_sum = (
        kept_state
    )
    normed, first_back = jax.vjp(layer_norm, first_sum, vector[base + 3], vector[base + 4])
    activ_float, gelu_back = jax.vjp(gelu_exact, pre_act)
    activation = to_low(activ_float)
    unused, second_back = jax.vjp(layer_norm, second_sum, vector[base + 6], vector[base + 7])
    grad_second, grad_gain_two, grad_shift_two = second_back(grad_result)
    grad_branch_two = to_low(grad_second)
    grad_down = matmul_tn(grad_branch_two, activation)
    grad_down_bias = jnp.sum(grad_branch_two.astype(jnp.float32), axis=0)
    grad_activ = matmul(grad_branch_two, feed_pair[1])
    (grad_pre,) = gelu_back(grad_activ)
    grad_pre = to_low(grad_pre)
    grad_up = matmul_tn(to_low(normed), grad_pre)
    grad_up_bias = jnp.sum(grad_pre.astype(jnp.float32), axis=0)
    grad_normed = grad_second + matmul_nt(grad_pre, feed_pair[0])
    grad_first, grad_gain_one, grad_shift_one = first_back(grad_normed)
    grad_branch = to_low(grad_first)
    grad_output_proj = matmul_tn(attended, grad_branch)
    grad_output_bias = jnp.sum(grad_branch.astype(jnp.float32), axis=0)
    grad_attended = to_low(matmul_nt(grad_branch, matrices[3]))
    grad_query, grad_key, grad_value = attention_backward(
        query, key_rows, value_rows, logsum, grad_attended, samples, head_count
    )
    hidden_low = to_low(hidden)
    grad_wq = matmul_tn(hidden_low, grad_query)
    grad_wk = matmul_tn(hidden_low, grad_key)
    grad_wv = matmul_tn(hidden_low, grad_value)
    grad_hidden = (
        grad_first
        + matmul_nt(grad_query, matrices[0])
        + matmul_nt(grad_key, matrices[1])
        + matmul_nt(grad_value, matrices[2])
    )
    matrix_grads = jnp.stack([grad_wq, grad_wk, grad_wv, grad_output_proj])
    feed_grads = jnp.stack([grad_up, grad_down])
    small_rows = jnp.stack(
        [
            jnp.sum(grad_query.astype(jnp.float32), axis=0),
            jnp.sum(grad_value.astype(jnp.float32), axis=0),
            grad_output_bias,
            grad_gain_one,
            grad_shift_one,
            grad_down_bias,
            grad_gain_two,
            grad_shift_two,
        ]
    )
    vector_grads = jnp.concatenate([small_rows, grad_up_bias.reshape(4, -1)], axis=0)
    return (grad_hidden, matrix_grads, feed_grads, vector_grads)


def adam_step(master, moment_one, moment_two, gradient, factor):
    clipped = gradient * factor
    one_new = beta_one * moment_one + (1.0 - beta_one) * clipped
    two_new = beta_two * moment_two + (1.0 - beta_two) * clipped * clipped
    one_hat = one_new / (1.0 - beta_one**ADAM_STEP)
    two_hat = two_new / (1.0 - beta_two**ADAM_STEP)
    step_value = -learn_rate * (one_hat / (jnp.sqrt(two_hat) + adam_eps) + decay_rate * master)
    return (step_value, one_new, two_new)


def teacher_move(master, teacher, step_value):
    return (1.0 - ema_keep) * (master - teacher + step_value)


def per_device(
    patches,
    mask_places,
    square_weights,
    square_first,
    square_second,
    square_teacher,
    feed_weights,
    feed_first,
    feed_second,
    feed_teacher,
    vector_weights,
    vector_first,
    vector_second,
    vector_teacher,
):
    samples, seq_len, model_width = patches.shape
    layer_count = feed_weights.shape[0]
    head_count = HEADS
    total_masked = samples * mask_places.shape[1] * lax.axis_size("rep") * lax.axis_size("fsdp")
    row_count = samples * seq_len
    patch_rows = patches.reshape(row_count, model_width)
    places = jnp.arange(seq_len, dtype=jnp.int32)
    mask_rows = jnp.sum(
        (mask_places[:, :, None] == places[None, None, :]).astype(jnp.float32), axis=1
    ).reshape(row_count, 1)
    edge_pair, teacher_embed = (
        lax.all_gather(
            to_low(jnp.stack([square_weights[0], square_weights[-1]])), "fsdp", axis=1, tiled=True
        ),
        lax.all_gather(to_low(square_teacher[0:1]), "fsdp", axis=1, tiled=True),
    )
    vector_all, vector_old = (
        lax.all_gather(vector_weights, "fsdp", axis=1, tiled=True),
        lax.all_gather(vector_teacher, "fsdp", axis=1, tiled=True),
    )
    embed_teacher = matmul(patch_rows, teacher_embed[0]) + vector_old[0]
    hidden_teacher = (
        embed_teacher.reshape(samples, seq_len, model_width) + vector_old[2 : 2 + seq_len]
    ).reshape(row_count, model_width)
    layer_index = 0
    matrices_t = lax.all_gather(
        to_low(square_teacher[1 + 4 * layer_index : 5 + 4 * layer_index]),
        "fsdp",
        axis=1,
        tiled=True,
    )
    feed_t = lax.all_gather(to_low(feed_teacher[layer_index]), "fsdp", axis=1, tiled=True)
    base = 2 + seq_len + 12 * layer_index
    hidden_teacher, branch_two, unused = layer_forward(
        hidden_teacher, matrices_t, feed_t, vector_old, base, samples, head_count
    )
    target = instance_norm(branch_two, samples)
    target = target * (1.0 / layer_count)
    embed_student = matmul(patch_rows, edge_pair[0]) + vector_all[0]
    masked = jnp.where(mask_rows > 0, vector_all[1], embed_student)
    hidden = (masked.reshape(samples, seq_len, model_width) + vector_all[2 : 2 + seq_len]).reshape(
        row_count, model_width
    )
    kept_weights = []
    layer_index = 0
    matrices = lax.all_gather(
        to_low(square_weights[1 + 4 * layer_index : 5 + 4 * layer_index]),
        "fsdp",
        axis=1,
        tiled=True,
    )
    feed_pair = lax.all_gather(to_low(feed_weights[layer_index]), "fsdp", axis=1, tiled=True)
    kept_weights.append((matrices, feed_pair))
    base = 2 + seq_len + 12 * layer_index
    hidden, unused, kept_state = layer_forward(
        hidden, matrices, feed_pair, vector_all, base, samples, head_count
    )
    kept_states = [kept_state]
    final_base = 2 + seq_len + 12 * layer_count
    final, final_back = jax.vjp(
        layer_norm, hidden, vector_all[final_base], vector_all[final_base + 1]
    )
    final_low = to_low(final)
    output = matmul(final_low, edge_pair[1]) + vector_all[final_base + 2]
    residue = output - target
    magnitude = jnp.abs(residue)
    huber_terms = jnp.where(
        magnitude <= huber_delta,
        0.5 * residue * residue,
        huber_delta * (magnitude - 0.5 * huber_delta),
    )
    loss_scale = 1.0 / (total_masked * model_width)
    loss_local = jnp.sum(huber_terms * mask_rows) * loss_scale
    grad_output = to_low(jnp.clip(residue, -huber_delta, huber_delta) * mask_rows * loss_scale)
    grad_head = matmul_tn(final_low, grad_output)
    grad_head_bias = jnp.sum(grad_output.astype(jnp.float32), axis=0)
    grad_final = matmul_nt(grad_output, edge_pair[1])
    grad_hidden, grad_final_gain, grad_final_shift = final_back(grad_final)
    matrix_shares = [None] * layer_count
    feed_shares = [None] * layer_count
    vector_layers = [None] * layer_count
    for layer_index in reversed(range(layer_count)):
        matrices, feed_pair = (
            lax.all_gather(
                to_low(square_weights[1 + 4 * layer_index : 5 + 4 * layer_index]),
                "fsdp",
                axis=1,
                tiled=True,
            ),
            lax.all_gather(to_low(feed_weights[layer_index]), "fsdp", axis=1, tiled=True),
        )
        base = 2 + seq_len + 12 * layer_index
        grad_hidden, matrix_grads, feed_grads, vector_grads = layer_backward(
            grad_hidden,
            kept_states[layer_index],
            matrices,
            feed_pair,
            vector_all,
            base,
            samples,
            head_count,
        )
        matrix_cols, feed_cols = (
            lax.psum_scatter(matrix_grads, "rep", scatter_dimension=2, tiled=True),
            lax.psum_scatter(feed_grads, "rep", scatter_dimension=2, tiled=True),
        )
        matrix_cols, feed_cols = (
            lax.psum_scatter(matrix_cols, "fsdp", scatter_dimension=1, tiled=True),
            lax.psum_scatter(feed_cols, "fsdp", scatter_dimension=1, tiled=True),
        )
        matrix_share, feed_share = (
            lax.all_gather(matrix_cols, "rep", axis=2, tiled=True),
            lax.all_gather(feed_cols, "rep", axis=2, tiled=True),
        )
        matrix_shares[layer_index] = matrix_share
        feed_shares[layer_index] = feed_share
        vector_layers[layer_index] = vector_grads
    grad_start = grad_hidden.reshape(samples, seq_len, model_width)
    grad_position = jnp.sum(grad_start, axis=0)
    grad_mask_vector = jnp.sum(grad_hidden * mask_rows, axis=0)
    grad_embed_out = to_low(grad_hidden * (1.0 - mask_rows))
    grad_embed = matmul_tn(patch_rows, grad_embed_out)
    grad_embed_bias = jnp.sum(grad_embed_out.astype(jnp.float32), axis=0)
    vector_grad = jnp.concatenate(
        [grad_embed_bias[None], grad_mask_vector[None], grad_position]
        + vector_layers
        + [jnp.stack([grad_final_gain, grad_final_shift, grad_head_bias])],
        axis=0,
    )
    end_share, vector_share = (
        lax.psum_scatter(
            jnp.stack([grad_embed, grad_head]), "fsdp", scatter_dimension=1, tiled=True
        ),
        lax.psum_scatter(vector_grad, "fsdp", scatter_dimension=1, tiled=True),
    )
    end_share, vector_share, loss_group = lax.psum((end_share, vector_share, loss_local), "rep")
    matrix_stack = jnp.stack(matrix_shares)
    feed_grad = jnp.stack(feed_shares)
    square_grad = jnp.concatenate(
        [end_share[0:1], matrix_stack.reshape((-1,) + matrix_stack.shape[2:]), end_share[1:2]],
        axis=0,
    )
    local_squares = (
        jnp.sum(square_grad * square_grad)
        + jnp.sum(feed_grad * feed_grad)
        + jnp.sum(vector_share * vector_share)
    )
    norm_squared, loss_value = lax.psum((local_squares, loss_group), "fsdp")
    grad_norm = jnp.sqrt(norm_squared)
    limit = clip_scale / math.sqrt(total_masked)
    factor = limit / jnp.maximum(grad_norm, limit)
    square_step, square_one, square_two = adam_step(
        square_weights, square_first, square_second, square_grad, factor
    )
    feed_step, feed_one, feed_two = adam_step(
        feed_weights, feed_first, feed_second, feed_grad, factor
    )
    vector_step, vector_one, vector_two = adam_step(
        vector_weights, vector_first, vector_second, vector_share, factor
    )
    square_moved = teacher_move(square_weights, square_teacher, square_step)
    feed_moved = teacher_move(feed_weights, feed_teacher, feed_step)
    vector_moved = teacher_move(vector_weights, vector_teacher, vector_step)
    return (
        loss_value,
        grad_norm,
        square_step,
        square_one,
        square_two,
        square_moved,
        feed_step,
        feed_one,
        feed_two,
        feed_moved,
        vector_step,
        vector_one,
        vector_two,
        vector_moved,
    )


def solution(mesh):
    placed = (
        P(("rep", "fsdp"), None, None),
        P(("rep", "fsdp"), None),
        P(None, "fsdp", None),
        P(None, "fsdp", None),
        P(None, "fsdp", None),
        P(None, "fsdp", None),
        P(None, None, "fsdp", None),
        P(None, None, "fsdp", None),
        P(None, None, "fsdp", None),
        P(None, None, "fsdp", None),
        P(None, "fsdp"),
        P(None, "fsdp"),
        P(None, "fsdp"),
        P(None, "fsdp"),
    )
    return jax.shard_map(
        per_device,
        mesh=mesh,
        in_specs=placed,
        out_specs=(
            P(),
            P(),
            P(None, "fsdp", None),
            P(None, "fsdp", None),
            P(None, "fsdp", None),
            P(None, "fsdp", None),
            P(None, None, "fsdp", None),
            P(None, None, "fsdp", None),
            P(None, None, "fsdp", None),
            P(None, None, "fsdp", None),
            P(None, "fsdp"),
            P(None, "fsdp"),
            P(None, "fsdp"),
            P(None, "fsdp"),
        ),
        check_vma=False,
    )
```

profile of v0, /device:TPU:0, one launch (start us, length us, event | category | flops | bytes accessed | tf_op | source)
XLA Modules:
  0.0 1487.0 jit_solution(202334364363828486)
XLA Ops:
  18.7 34.7 %all-gather.2 = f32[8,96,184]{1,2,0:T(8,128)S(1)} all-gather(f32[1,96,184]{1,2,0:T(8,128)S(1)} %bitcast.202), channel_id=1, replica_groups=mesh['rep'=4,'fsdp'=8] {'fsdp'}, dimensions={0}, use_global_device_ids=true | all-gather | bytes 635904 | tf_op jit(solution)/shard_map/all_gather | solution.py:249
  54.3 33.3 %all-gather.3 = f32[8,96,184]{1,2,0:T(8,128)S(1)} all-gather(f32[1,96,184]{1,2,0:T(8,128)S(1)} %bitcast.201), channel_id=1, replica_groups=mesh['rep'=4,'fsdp'=8] {'fsdp'}, dimensions={0}, use_global_device_ids=true | all-gather | bytes 635904 | tf_op jit(solution)/shard_map/all_gather | solution.py:250
  104.9 9.5 all-gather.13.cloned.1.call-done
  117.7 77.4 %all-gather.15.cloned.1.call-done = bf16[4,768,768]{2,1,0:T(8,128)(2,1)} async-done(((bf16[4,96,768]{2,1,0:T(8,128)(2,1)}), bf16[4,768,768]{2,1,0:T(8,128)(2,1)}) %all-gather.15.cloned.1.call-update) | async-done | bytes 4718608 | tf_op jit(solution)/shard_map/all_gather | solution.py:277
  228.6 46.2 %all-gather.19.cloned.1.call-done = bf16[4,768,768]{2,1,0:T(8,128)(2,1)} async-done(((bf16[4,96,768]{2,1,0:T(8,128)(2,1)}), bf16[4,768,768]{2,1,0:T(8,128)(2,1)}) %all-gather.19.cloned.1.call-update) | async-done | bytes 4718608 | tf_op jit(solution)/shard_map/all_gather | solution.py:257
  308.2 104.9 %all-gather.25.cloned.1.call-done = bf16[1,2,768,3072]{3,2,1,0:T(8,128)(2,1)} async-done(((bf16[1,2,96,3072]{3,2,1,0:T(8,128)(2,1)}), bf16[1,2,768,3072]{3,2,1,0:T(8,128)(2,1)}) %all-gather.25.cloned.1.call-update) | async-done | bytes 9437200 | tf_op jit(solution)/shard_map/all_gather | solution.py:283
  413.1 20.0 %multiply_convert_fusion.1 = (bf16[501,3072]{1,0:T(8,128)(2,1)S(1)}, f32[501,3072]{1,0:T(8,128)}, f32[501,3072]{1,0:T(8,128)}) fusion(f32[3072]{0:T(1024)S(1)} %copy-done.84, bf16[1,2,768,3072]{3,2,1,0:T(8,128)(2,1)} %all-gather.25.cloned.1.call-done, f32[501,768]{1,0:T(8,128)S(1)} %get-tuple-element.132, f32[768]{0:T(1024)S(1)} %get-tuple-element.73, ...), kind=kOutput, calls=%fused_computation.27 | convolution fusion | flops 2467517184 | bytes 21670824 | tf_op jit(solution)/shard_map/dot_general | solution.py:28
  438.1 113.0 %all-gather.27.cloned.1.call-done = bf16[1,2,768,3072]{3,2,1,0:T(8,128)(2,1)} async-done(((bf16[1,2,96,3072]{3,2,1,0:T(8,128)(2,1)}), bf16[1,2,768,3072]{3,2,1,0:T(8,128)(2,1)}) %all-gather.27.cloned.1.call-update) | async-done | bytes 9437200 | tf_op jit(solution)/shard_map/all_gather | solution.py:263
  551.2 22.5 %fusion.70 = f32[501,768]{1,0:T(8,128)} fusion(bf16[1,2,768,3072]{3,2,1,0:T(8,128)(2,1)} %all-gather.27.cloned.1.call-done, f32[3072]{0:T(1024)S(1)} %copy-done.85, f32[501,768]{1,0:T(8,128)S(1)} %copy-done.43, f32[768]{0:T(1024)S(1)} %copy-done.95, f32[768]{0:T(1024)S(1)} %copy-done.96, f32[768]{0:T(1024)S(1)} %copy-done.94, f32[501]{0:T(512)S(1)} %add_rsqrt_fusion.1, ...), kind=kOutput, calls=%fused_computation.165 | convolution fusion | flops 4831917056 | bytes 12540840 | tf_op jit(solution)/shard_map/dot_general | solution.py:38
  592.4 7.4 convert_reduce_fusion
  664.2 8.2 copy.243
  682.2 12.1 copy.245
  694.3 25.3 %reduce-scatter.15.cloned.1.call-done = f32[96,184]{1,0:T(8,128)} async-done(((f32[768,184]{1,0:T(8,128)}), f32[96,184]{1,0:T(8,128)}) %reduce-scatter.15.cloned.1.call-update) | async-done | bytes 70672
  721.2 170.6 %all-reduce.7.cloned.1.call-done = f32[2,768,768]{2,0,1:T(2,128)} async-done(((f32[2,768,768]{2,0,1:T(2,128)}), f32[2,768,768]{2,0,1:T(2,128)}) %all-reduce.7.cloned.1.call-update) | async-done | bytes 4718608
  911.4 164.6 %all-reduce.9.cloned.1.call-done = (f32[2,96,768]{2,1,0:T(8,128)}, f32[4,768,768]{1,0,2:T(4,128)}, f32[184,96]{1,0:T(8,128)}) async-done(((f32[2,96,768]{2,1,0:T(8,128)}, f32[4,768,768]{1,0,2:T(4,128)}, f32[184,96]{1,0:T(8,128)}), (f32[2,96,768]{2,1,0:T(8,128)}, f32[4,768,768]{1,0,2:T(4,128)}, f32[184,96]{1,0:T(8,128)})) %all-reduce.9.cloned.1.call-update) | async-done | bytes 10097680 | tf_op jit(solution)/shard_map/psum | solution.py:367
  1078.1 40.3 %copy.259 = f32[4,768,192]{0,2,1:T(8,128)} copy(f32[4,768,192]{1,0,2:T(4,128)S(1)} %constant_dynamic-slice_fusion) | data formatting | bytes 4718592
  1118.4 64.0 %reshape.302 = f32[768,768]{1,0:T(8,128)} reshape(f32[768,192,4]{2,1,0:T(8,128)} %bitcast.39) | data formatting | bytes 4718592
  1182.5 33.7 %reduce-scatter.9.cloned.1.call-done = f32[2,768,768]{2,1,0:T(8,128)} async-done(((f32[2,768,3072]{2,1,0:T(8,128)}), f32[2,768,768]{2,1,0:T(8,128)}) %reduce-scatter.9.cloned.1.call-update) | async-done | bytes 4718608 | tf_op jit(solution)/shard_map/reduce_scatter | solution.py:336
  1216.3 73.6 %reduce-scatter.13.cloned.1.call-done = f32[96,768]{1,0:T(8,128)} async-done(((f32[768,768]{1,0:T(8,128)}), f32[96,768]{1,0:T(8,128)}) %reduce-scatter.13.cloned.1.call-update) | async-done | bytes 294928
  1289.9 12.1 reshape.303
  1308.9 79.4 %reduce-scatter.11.cloned.1.call-done = f32[2,96,768]{2,1,0:T(8,128)} async-done(((f32[2,768,768]{2,1,0:T(8,128)}), f32[2,96,768]{2,1,0:T(8,128)}) %reduce-scatter.11.cloned.1.call-update) | async-done | bytes 589840 | tf_op jit(solution)/shard_map/reduce_scatter | solution.py:340
  1396.6 13.1 all-gather.21.cloned.1.call-done
  1412.5 22.8 %all-gather.23.cloned.1.call-done = f32[2,96,3072]{2,1,0:T(8,128)} async-done(((f32[2,96,768]{2,1,0:T(8,128)}), f32[2,96,3072]{2,1,0:T(8,128)}) %all-gather.23.cloned.1.call-update) | async-done | bytes 2359312 | tf_op jit(solution)/shard_map/all_gather | solution.py:344
  1440.1 22.0 %all-reduce.2 = (f32[]{:T(128)}, f32[]{:T(128)}) all-reduce(f32[]{:T(128)} %psum.35, f32[]{:T(128)S(6)} %add.441), channel_id=1, replica_groups=mesh['rep'=4,'fsdp'=8] {'fsdp'}, use_global_device_ids=true, to_apply=%region_17.18 | all-reduce | flops 2 | bytes 16 | tf_op jit(solution)/shard_map/psum | solution.py:379
  (433 shorter events, 254.4 us)
Async XLA Ops:
  7.2 94.0 %all-gather.17.cloned.1.call-start = ((), (), s32[]{:S(2)}) async-start(), calls=%async_computation.6 | async-start | bytes 1327104 | tf_op jit(solution)/shard_map/all_gather | solution.py:246
  10.5 103.9 %all-gather.13.cloned.1.call-start = ((), (), s32[]{:S(2)}) async-start(), calls=%async_computation.4 | async-start | bytes 2654208 | tf_op jit(solution)/shard_map/all_gather | solution.py:243
  11.5 183.6 %all-gather.15.cloned.1.call-start = ((), (), s32[]{:S(2)}) async-start(), calls=%async_computation.5 | async-start | bytes 5308416 | tf_op jit(solution)/shard_map/all_gather | solution.py:277
  12.4 262.4 %all-gather.19.cloned.1.call-start = ((), (), s32[]{:S(2)}) async-start(), calls=%async_computation.7 | async-start | bytes 5308416 | tf_op jit(solution)/shard_map/all_gather | solution.py:257
  14.4 398.7 %all-gather.25.cloned.1.call-start = ((), (), s32[]{:S(2)}) async-start(), calls=%async_computation.12 | async-start | bytes 10616832 | tf_op jit(solution)/shard_map/all_gather | solution.py:283
  15.7 535.5 %all-gather.27.cloned.1.call-start = ((), (), s32[]{:S(2)}) async-start(), calls=%async_computation.13 | async-start | bytes 10616832 | tf_op jit(solution)/shard_map/all_gather | solution.py:263
  18.6 701.0 %reduce-scatter.15.cloned.1.call-start = ((), (), s32[]{:S(2)}) async-start(), calls=%async_computation.15 | async-start | bytes 884736
  100.6 312.5 %copy-start.92 = (f32[768]{0:T(1024)}, f32[768]{0:T(1024)S(1)}, u32[]{:S(2)}) copy-start(f32[768]{0:T(1024)S(1)} %get-tuple-element.73) | copy-start | bytes 9220
  100.6 332.5 %copy-start.81 = (f32[768]{0:T(1024)}, f32[768]{0:T(1024)S(1)}, u32[]{:S(2)}) copy-start(f32[768]{0:T(1024)S(1)} %get-tuple-element.74) | copy-start | bytes 9220
  304.0 129.2 %copy-start.19 = (f32[501,768]{1,0:T(8,128)}, f32[501,768]{1,0:T(8,128)S(1)}, u32[]{:S(2)}) copy-start(f32[501,768]{1,0:T(8,128)S(1)} %get-tuple-element.132) | copy-start | bytes 4617220
  304.0 299.6 %copy-start.67 = (f32[501]{0:T(512)}, f32[501]{0:T(512)S(1)}, u32[]{:S(2)}) copy-start(f32[501]{0:T(512)S(1)} %broadcast_multiply_fusion.4) | copy-start | bytes 6016
  308.2 295.4 %copy-start.88 = (f32[501]{0:T(512)}, f32[501]{0:T(512)S(1)}, u32[]{:S(2)}) copy-start(f32[501]{0:T(512)S(1)} %fusion.98) | copy-start | bytes 6016
  436.7 114.4 %copy-start.43 = (f32[501,768]{1,0:T(8,128)S(1)}, f32[501,768]{1,0:T(8,128)}, u32[]{:S(2)}) copy-start(f32[501,768]{1,0:T(8,128)} %copy-done.42) | copy-start | bytes 4617220
  436.7 114.4 %copy-start.85 = (f32[3072]{0:T(1024)S(1)}, f32[3072]{0:T(1024)}, u32[]{:S(2)}) copy-start(f32[3072]{0:T(1024)} %add.428) | copy-start | bytes 36868
  437.1 153.2 %copy-start.56 = (f32[501]{0:T(512)}, f32[501]{0:T(512)S(1)}, u32[]{:S(2)}) copy-start(f32[501]{0:T(512)S(1)} %fusion.99) | copy-start | bytes 6016
  437.6 150.5 %copy-start.62 = (f32[501]{0:T(512)}, f32[501]{0:T(512)S(1)}, u32[]{:S(2)}) copy-start(f32[501]{0:T(512)S(1)} %broadcast_multiply_fusion.2) | copy-start | bytes 6016
  438.1 150.0 %copy-start.71 = (f32[501]{0:T(512)}, f32[501]{0:T(512)S(1)}, u32[]{:S(2)}) copy-start(f32[501]{0:T(512)S(1)} %fusion.100) | copy-start | bytes 6016
  658.1 233.7 %all-reduce.7.cloned.1.call-start = ((), (), s32[]{:S(2)}) async-start(), calls=%async_computation.16 | async-start | bytes 9437184
  672.5 403.6 %all-reduce.9.cloned.1.call-start = ((), (), s32[]{:S(2)}) async-start(), calls=%async_computation.17 | async-start | bytes 20242432 | tf_op jit(solution)/shard_map/psum | solution.py:367
  893.9 322.3 %reduce-scatter.9.cloned.1.call-start = ((), (), s32[]{:S(2)}) async-start(), calls=%async_computation.9 | async-start | bytes 23592960 | tf_op jit(solution)/shard_map/reduce_scatter | solution.py:336
  909.6 380.3 %reduce-scatter.13.cloned.1.call-start = ((), (), s32[]{:S(2)}) async-start(), calls=%async_computation.14 | async-start | bytes 2654208
  1182.5 205.8 %reduce-scatter.11.cloned.1.call-start = ((), (), s32[]{:S(2)}) async-start(), calls=%async_computation.10 | async-start | bytes 5308416 | tf_op jit(solution)/shard_map/reduce_scatter | solution.py:340
  1216.2 193.5 %all-gather.21.cloned.1.call-start = ((), (), s32[]{:S(2)}) async-start(), calls=%async_computation.8 | async-start | bytes 1966080 | tf_op jit(solution)/shard_map/all_gather | solution.py:343
  1308.8 126.4 %all-gather.23.cloned.1.call-start = ((), (), s32[]{:S(2)}) async-start(), calls=%async_computation.11 | async-start | bytes 2949120 | tf_op jit(solution)/shard_map/all_gather | solution.py:344
  (110 other events, 1374.7 us)
Sparse Core Ops, SparseCore 0:
  10.7 48.3 all-gather.16
  61.8 52.5 all-gather.12
  117.2 77.8 all-gather.14
  197.1 77.6 all-gather.18
  277.5 135.5 all-gather.24
  415.7 135.4 all-gather.26
  658.1 61.4 reduce-scatter.14
  723.2 168.5 all-reduce.6
  895.7 180.2 all-reduce.8
  1078.5 137.6 reduce-scatter.8
  1220.3 69.5 reduce-scatter.12
  1293.4 94.8 reduce-scatter.10
  1390.4 19.2 all-gather.20
  1411.2 24.0 all-gather.22
where the time goes:
time: 1490 us
  waiting for transfers between devices  934 us (63%)
  local copies, waits for them, and re-layouts  241 us (16%)
  matrix products  137 us (9%)
  blocking collectives  97 us (7%)
  other arithmetic  54.8 us (4%)
  between operations  21.7 us (1%)
    unnamed x17, waiting for transfers between devices  270 us
    psum x1, waiting for transfers between devices, per_device(): lax.psum((end_share, vector_share, loss_local), 'rep')  165 us
    unnamed x252, local copies, waits for them, and re-layouts  141 us
    all_gather x1, waiting for transfers between devices, per_device(): lax.all_gather(to_low(feed_teacher[layer_index]), 'fsdp', axis=1, tiled=T...  113 us
    all_gather x1, waiting for transfers between devices, per_device(): lax.all_gather(to_low(feed_weights[layer_index]), 'fsdp', axis=1, tiled=T...  105 us
    reduce_scatter x1, waiting for transfers between devices, per_device(): lax.psum_scatter(feed_cols, 'fsdp', scatter_dimension=1, tiled=True)  79.4 us
    all_gather x1, waiting for transfers between devices, per_device(): lax.all_gather(to_low(square_weights[1 + 4 * layer_index:5 + 4 * layer_in...  77.4 us
    dot_general x13, matrix products, matmul(): return jnp.dot(left, right, preferred_element_type=jnp.float32)  61.7 us
  transfers between devices with their start and end apart: 14, of which 13 were waited for; matrix products, arithmetic and copies ran while one was open for 20% of the time, Pallas kernels for 0%

commit v1 on v0

v1 whole, which is shorter than its diff:
```python
import functools
import math

import jax
import jax.numpy as jnp
from jax import lax
from jax.experimental import pallas as pl
from jax.experimental.pallas import tpu as pltpu
from jax.sharding import PartitionSpec as P

HEADS = 12
ADAM_STEP = 10


ln_eps = 1e-05
beta_one = 0.9
beta_two = 0.999
adam_eps = 1e-08
learn_rate = 0.01
decay_rate = 0.05
ema_keep = 0.999
huber_delta = 1.0
clip_scale = 1.25

VMEM_LIMIT = 60 * 1024 * 1024
BF16 = jnp.bfloat16
F32 = jnp.float32


def to_low(values):
    return values.astype(BF16)


def matmul(left, right):
    return jnp.dot(left, right, preferred_element_type=F32)


def matmul_tn(left, right):
    return lax.dot_general(left, right, (((0,), (0,)), ((), ())), preferred_element_type=F32)


def matmul_nt(left, right):
    return lax.dot_general(left, right, (((1,), (1,)), ((), ())), preferred_element_type=F32)


tail_scale = 0.21
tail_terms = (
    0.08371158707086396,
    0.08506867712628283,
    0.06919339848407204,
    0.1248680487092072,
    -0.09391427181816406,
    0.34938494294095396,
    -0.3302388882989717,
    0.2835812219436135,
    -0.07165470896901999,
)


def gelu_exact(values):
    t = 1.0 / (1.0 + tail_scale * jnp.abs(values))
    tail = jnp.full_like(t, tail_terms[-1])
    for term in tail_terms[-2::-1]:
        tail = tail * t + term
    bell = jnp.exp(-0.5 * (values * values))
    tail = tail * t * bell
    normal = jnp.where(values < 0, tail, 1.0 - tail)
    return values * normal, normal + values * bell * (1.0 / math.sqrt(2.0 * math.pi))


def norm_parts(values):
    centred = values - jnp.mean(values, axis=-1, keepdims=True)
    inverse = lax.rsqrt(jnp.mean(centred * centred, axis=-1, keepdims=True) + ln_eps)
    return centred * inverse, inverse


def norm_back(grad, hat, inverse, gain):
    scaled = grad * gain
    return inverse * (
        scaled
        - jnp.mean(scaled, axis=-1, keepdims=True)
        - hat * jnp.mean(scaled * hat, axis=-1, keepdims=True)
    )


def any_spec():
    return pl.BlockSpec(memory_space=pl.ANY)


def vmem_spec():
    return pl.BlockSpec(memory_space=pltpu.VMEM)


def smem_spec():
    return pl.BlockSpec(memory_space=pltpu.SMEM)


def swap(values, stage):
    axis, bit = stage
    return lax.ppermute(values, axis, [(i, i ^ bit) for i in range(lax.axis_size(axis))])


def fsdp_bits():
    count = lax.axis_size("fsdp")
    return [1 << k for k in reversed(range(count.bit_length() - 1))]


def stage_order(kind):
    stages = [("fsdp", bit) for bit in fsdp_bits()]
    place = len(stages) if kind == 0 else len(stages) - 1
    return stages[:place] + [("rep", 2)] + stages[place:]


def gather_unit(mine, kind):
    arrays, labels = [mine], [[(0, 0)]]
    stages = stage_order(kind)
    for number, (axis, bit) in enumerate(stages):
        got = [swap(a, (axis, bit)) for a in arrays]
        moved = [
            [(u ^ bit, e) if axis == "rep" else (u, e ^ bit) for u, e in block] for block in labels
        ]
        if number < len(stages) - 1:
            arrays = [jnp.concatenate([arrays[0], got[0]], axis=0)]
            labels = [labels[0] + moved[0]]
        else:
            arrays, labels = arrays + got, labels + moved
    got = [swap(a, ("rep", 1)) for a in arrays]
    moved = [[(u ^ 1, e) for u, e in block] for block in labels]
    return arrays + got, labels + moved


class Group:
    def __init__(self, mine, kind, wide, where):
        self.arrays, self.labels = gather_unit(mine, kind)
        self.wide = wide
        self.rows, self.width = mine.shape
        count = lax.axis_size("fsdp")
        depth = self.rows * count
        self.shape = (depth, 4 * self.width) if wide else (4, depth, self.width)
        self.blocks = sum(len(block) for block in self.labels)
        if self.rows % 16:
            flat = jnp.concatenate(self.arrays, axis=0).reshape(-1, self.rows, self.width)
            order = [label for block in self.labels for label in block]
            place = {label: number for number, label in enumerate(order)}
            table = jnp.array(
                [[place[(u, e)] for e in range(count)] for u in range(4)], jnp.int32
            )
            units = jnp.arange(4, dtype=jnp.int32)[:, None] ^ where[0]
            owners = jnp.arange(count, dtype=jnp.int32)[None] ^ where[1]
            whole = flat[table[units, owners]].reshape(4, depth, self.width)
            if wide:
                whole = whole.transpose(1, 0, 2).reshape(depth, 4 * self.width)
            self.arrays, self.labels, self.blocks = [whole], None, 1

    def copies(self, where_ref, arrays, out, sems):
        if self.labels is None:
            return [pltpu.make_async_copy(arrays[0], out, sems.at[0])]
        rep, own = where_ref[0], where_ref[1]
        copies = []
        for array, block in zip(arrays, self.labels):
            for number, (u, e) in enumerate(block):
                unit = jnp.bitwise_xor(rep, u)
                rows = pl.ds(pl.multiple_of(jnp.bitwise_xor(own, e) * self.rows, 16), self.rows)
                if self.wide:
                    columns = pl.ds(pl.multiple_of(unit * self.width, 128), self.width)
                    target = out.at[rows, columns]
                else:
                    target = out.at[unit, rows, :]
                source = array.at[pl.ds(number * self.rows, self.rows), :]
                copies.append(pltpu.make_async_copy(source, target, sems.at[len(copies)]))
        return copies


class Loading:
    def __init__(self, copies, ref):
        self.pending, self.ref = copies, ref
        for copy in copies:
            copy.start()

    def __call__(self):
        for copy in self.pending:
            copy.wait()
        self.pending = []
        return self.ref


def call(body, name, where, groups, ins, outs, scratch=(), flops=0):
    sizes = [len(group.arrays) for group in groups]

    def kernel(where_ref, *refs):
        refs = list(refs)
        arrays = [[refs.pop(0) for _ in range(size)] for size in sizes]
        in_refs = [refs.pop(0) for _ in ins]
        out_refs = [refs.pop(0) for _ in outs]
        places = [refs.pop(0) for _ in groups]
        sems = [refs.pop(0) for _ in groups]
        loads = [
            Loading(group.copies(where_ref, given, place, sem), place)
            for group, given, place, sem in zip(groups, arrays, places, sems)
        ]
        body(where_ref, loads, in_refs, out_refs, refs)

    return pl.pallas_call(
        kernel,
        out_shape=tuple(jax.ShapeDtypeStruct(*out) for out in outs),
        in_specs=[smem_spec()] + [any_spec()] * sum(sizes) + [vmem_spec()] * len(ins),
        out_specs=(vmem_spec(),) * len(outs),
        scratch_shapes=[pltpu.VMEM(group.shape, BF16) for group in groups]
        + [pltpu.SemaphoreType.DMA((group.blocks,)) for group in groups]
        + list(scratch),
        compiler_params=pltpu.CompilerParams(vmem_limit_bytes=VMEM_LIMIT),
        cost_estimate=pl.CostEstimate(flops=flops, bytes_accessed=1 << 20, transcendentals=0),
        name=name,
    )(where, *[array for group in groups for array in group.arrays], *ins)


def vector_kernel(where_ref, pieces_ref, out_ref):
    count, width = pieces_ref.shape[0], pieces_ref.shape[3]
    for k in range(count):
        out_ref[:, :, k * width : (k + 1) * width] = pieces_ref[jnp.bitwise_xor(where_ref[1], k)]


def gather_vectors(mine, where):
    pieces = mine[None]
    for bit in reversed(fsdp_bits()):
        pieces = jnp.concatenate([pieces, swap(pieces, ("fsdp", bit))], axis=0)
    count, two, rows, width = pieces.shape
    return pl.pallas_call(
        vector_kernel,
        out_shape=jax.ShapeDtypeStruct((two, rows, count * width), mine.dtype),
        in_specs=[smem_spec(), vmem_spec()],
        out_specs=vmem_spec(),
        compiler_params=pltpu.CompilerParams(vmem_limit_bytes=VMEM_LIMIT),
        name="gather_vectors",
    )(where, pieces)


def reduce_order(kind):
    stages = [("fsdp", bit) for bit in reversed(fsdp_bits())]
    place = 0 if kind == 0 else 1
    return stages[:place] + [("rep", 2)] + stages[place:]


def grad_kernel(unit_of, kind_stages, rows, width, where_ref, *refs):
    count = len(unit_of)
    lefts, rights = refs[:count], refs[count : 2 * count]
    keep, send = refs[2 * count], refs[2 * count + 1]
    rep, own = where_ref[0], where_ref[1]
    owners = lefts[0].shape[1] // rows
    for pair in range(count):
        left = lefts[pair][...]
        for column, unit in unit_of[pair]:
            product = matmul_tn(left, rights[pair][:, column : column + width])
            shifted = jnp.bitwise_xor(rep, unit)
            for other, target in ((0, keep), (1, send)):

                @pl.when(jnp.bitwise_and(shifted, 1) == other)
                def _():
                    for f in range(owners):
                        apart = jnp.bitwise_xor(own, f)
                        position = 0
                        for axis, bit in kind_stages:
                            value = shifted if axis == "rep" else apart
                            position = position * 2 + jnp.where(
                                jnp.bitwise_and(value, bit) != 0, 1, 0
                            )
                        target[pl.ds(pl.multiple_of(position * rows, 8), rows), :] = product[
                            f * rows : (f + 1) * rows, :
                        ]


def unit_grads(pairs, unit_of, kind, width, where):
    depth = pairs[0][0].shape[1]
    rows = depth // lax.axis_size("fsdp")
    shape = jax.ShapeDtypeStruct((2 * depth, width), F32)
    flops = sum(2 * left.shape[0] * depth * width * len(units) for (left, _), units in zip(pairs, unit_of))
    return pl.pallas_call(
        functools.partial(grad_kernel, unit_of, reduce_order(kind), rows, width),
        out_shape=(shape, shape),
        in_specs=[smem_spec()] + [vmem_spec()] * (2 * len(pairs)),
        out_specs=(vmem_spec(), vmem_spec()),
        compiler_params=pltpu.CompilerParams(vmem_limit_bytes=VMEM_LIMIT),
        cost_estimate=pl.CostEstimate(
            flops=flops, bytes_accessed=16 * depth * width, transcendentals=0
        ),
        name="unit_grads",
    )(where, *[left for left, _ in pairs], *[right for _, right in pairs])


def reduce_units(keep, send, kind):
    got = swap(send, ("rep", 1))
    for stage in reduce_order(kind):
        half = keep.shape[0] // 2
        send = keep[half:] + got[half:]
        keep = keep[:half] + got[:half]
        got = swap(send, stage)
    return keep + got


def share_units(own):
    far = swap(own, ("rep", 2))
    near, cross = swap(own, ("rep", 1)), swap(far, ("rep", 1))
    return jnp.stack([own, near, far, cross])


def scores_of(query, key_rows, valid, scaling):
    scores = matmul_nt(query, key_rows) * scaling
    return jnp.where(valid, scores, -1e30)


def attention_kernel(seq_len, head_dim, q_ref, k_ref, v_ref, out_ref, log_ref):
    rows, model_width = q_ref.shape
    scaling = head_dim**-0.5
    valid = lax.broadcasted_iota(jnp.int32, (rows, rows), 1) < seq_len
    lane = lax.broadcasted_iota(jnp.int32, (rows, 2 * head_dim), 1)
    zero = jnp.zeros((rows, 2 * head_dim), BF16)
    for pair in range(model_width // (2 * head_dim)):
        columns = slice(pair * 2 * head_dim, (pair + 1) * 2 * head_dim)
        query, key_rows, values = q_ref[:, columns], k_ref[:, columns], v_ref[:, columns]
        results = []
        for sub in range(2):
            picked = lane >= head_dim if sub else lane < head_dim
            scores = scores_of(jnp.where(picked, query, zero), key_rows, valid, scaling)
            highest = jnp.max(scores, axis=-1, keepdims=True)
            logsum = highest + jnp.log(jnp.sum(jnp.exp(scores - highest), axis=-1, keepdims=True))
            log_ref[:, 2 * pair + sub : 2 * pair + sub + 1] = logsum
            results.append(matmul(to_low(jnp.exp(scores - logsum)), values))
        out_ref[:, columns] = to_low(jnp.where(lane < head_dim, results[0], results[1]))


def attention_forward(query, key_rows, value_rows, samples, seq_len):
    row_count, model_width = query.shape
    rows = row_count // samples
    head_dim = model_width // HEADS
    block = pl.BlockSpec((rows, model_width), lambda i: (i, 0))
    small = pl.BlockSpec((rows, 128), lambda i: (i, 0))
    return pl.pallas_call(
        functools.partial(attention_kernel, seq_len, head_dim),
        grid=(samples,),
        out_shape=(
            jax.ShapeDtypeStruct(query.shape, BF16),
            jax.ShapeDtypeStruct((row_count, 128), F32),
        ),
        in_specs=[block] * 3,
        out_specs=(block, small),
        compiler_params=pltpu.CompilerParams(vmem_limit_bytes=VMEM_LIMIT),
        cost_estimate=pl.CostEstimate(
            flops=4 * row_count * rows * model_width,
            bytes_accessed=8 * row_count * model_width,
            transcendentals=2 * row_count * rows * HEADS,
        ),
        name="attention",
    )(query, key_rows, value_rows)


def attention_back_kernel(
    seq_len, head_dim, q_ref, k_ref, v_ref, da_ref, log_ref, dq_ref, dk_ref, dv_ref
):
    rows, model_width = q_ref.shape
    scaling = head_dim**-0.5
    valid = lax.broadcasted_iota(jnp.int32, (rows, rows), 1) < seq_len
    lane = lax.broadcasted_iota(jnp.int32, (rows, 2 * head_dim), 1)
    zero = jnp.zeros((rows, 2 * head_dim), BF16)
    for pair in range(model_width // (2 * head_dim)):
        columns = slice(pair * 2 * head_dim, (pair + 1) * 2 * head_dim)
        query, key_rows = q_ref[:, columns], k_ref[:, columns]
        values, grad = v_ref[:, columns], da_ref[:, columns]
        results = []
        for sub in range(2):
            picked = lane >= head_dim if sub else lane < head_dim
            scores = scores_of(jnp.where(picked, query, zero), key_rows, valid, scaling)
            soft = jnp.exp(scores - log_ref[:, 2 * pair + sub : 2 * pair + sub + 1])
            grad_soft = matmul_nt(jnp.where(picked, grad, zero), values)
            total = jnp.sum(grad_soft * soft, axis=-1, keepdims=True)
            grad_scores = to_low(soft * (grad_soft - total))
            results.append(
                (
                    matmul(grad_scores, key_rows) * scaling,
                    matmul_tn(grad_scores, query) * scaling,
                    matmul_tn(to_low(soft), grad),
                )
            )
        for target, first, second in zip((dq_ref, dk_ref, dv_ref), *results):
            target[:, columns] = to_low(jnp.where(lane < head_dim, first, second))


def attention_backward(query, key_rows, value_rows, logsum, grad, samples, seq_len):
    row_count, model_width = query.shape
    rows = row_count // samples
    head_dim = model_width // HEADS
    block = pl.BlockSpec((rows, model_width), lambda i: (i, 0))
    small = pl.BlockSpec((rows, 128), lambda i: (i, 0))
    return pl.pallas_call(
        functools.partial(attention_back_kernel, seq_len, head_dim),
        grid=(samples,),
        out_shape=(jax.ShapeDtypeStruct(query.shape, BF16),) * 3,
        in_specs=[block] * 4 + [small],
        out_specs=(block,) * 3,
        compiler_params=pltpu.CompilerParams(vmem_limit_bytes=VMEM_LIMIT),
        cost_estimate=pl.CostEstimate(
            flops=10 * row_count * rows * model_width,
            bytes_accessed=14 * row_count * model_width,
            transcendentals=row_count * rows * HEADS,
        ),
        name="attention_back",
    )(query, key_rows, value_rows, grad, logsum)


TILE = 256


def tiles(width, body):
    def step(number, carry):
        body(pl.ds(pl.multiple_of(number * TILE, TILE), TILE))
        return carry

    lax.fori_loop(0, width // TILE, step, 0)


def embed_body(samples, masked, base, where_ref, loads, ins, outs, scratch):
    patch_ref, vec_ref, pos_ref = ins[:3]
    hid_ref, low_ref, q_ref, k_ref, v_ref = outs
    weights = loads[0]()
    rows = patch_ref.shape[0] // samples
    width = patch_ref.shape[1]

    def embed(columns):
        product = matmul(patch_ref[...], weights[0, :, columns]) + vec_ref[0:1, columns]
        if masked:
            product = jnp.where(ins[3][...] > 0, vec_ref[1:2, columns], product)
        for s in range(samples):
            part = product[s * rows : (s + 1) * rows] + pos_ref[:, columns]
            hid_ref[s * rows : (s + 1) * rows, columns] = part
            low_ref[s * rows : (s + 1) * rows, columns] = to_low(part)

    tiles(width, embed)

    def project(columns):
        low = low_ref[...]
        q_ref[:, columns] = to_low(
            matmul(low, weights[1, :, columns]) + vec_ref[base : base + 1, columns]
        )
        k_ref[:, columns] = to_low(matmul(low, weights[2, :, columns]))
        v_ref[:, columns] = to_low(
            matmul(low, weights[3, :, columns]) + vec_ref[base + 1 : base + 2, columns]
        )

    tiles(width, project)


def feed_forward(samples, base, unit, loads, ins, student, refs):
    att_ref, hid_ref, vec_ref = ins
    sum_ref, low_ref, act_ref = refs[:3]
    rows, width = hid_ref.shape[0] // samples, hid_ref.shape[1]
    squares = loads[0]()

    def project(columns):
        sum_ref[:, columns] = (
            hid_ref[:, columns]
            + matmul(att_ref[...], squares[unit, :, columns])
            + vec_ref[base + 2 : base + 3, columns]
        )

    tiles(width, project)
    for s in range(samples):
        part = slice(s * rows, (s + 1) * rows)
        hat, inverse = norm_parts(sum_ref[part, :])
        if student:
            refs[3][part, :], refs[4][part, :] = hat, inverse
        normed = hat * vec_ref[base + 3 : base + 4, :] + vec_ref[base + 4 : base + 5, :]
        sum_ref[part, :] = normed
        low_ref[part, :] = to_low(normed)
    up = loads[1]()
    hidden_units = up.shape[1]

    def widen(columns, bias):
        pre_act = matmul(low_ref[...], up[:, columns]) + bias
        value, slope = gelu_exact(pre_act)
        act_ref[:, columns] = to_low(value)
        if student:
            refs[5][:, columns] = slope

    for quarter in range(4):
        size = hidden_units // 4

        def step(number, carry, quarter=quarter):
            inner = pl.ds(pl.multiple_of(number * TILE, TILE), TILE)
            outer = pl.ds(pl.multiple_of(quarter * size + number * TILE, TILE), TILE)
            widen(outer, vec_ref[base + 8 + quarter : base + 9 + quarter, inner])
            return carry

        lax.fori_loop(0, size // TILE, step, 0)
    down = loads[2]()

    def narrow(columns, target_ref, residual):
        branch = (
            matmul_nt(act_ref[...], down[columns, :]) + vec_ref[base + 5 : base + 6, columns]
        )
        target_ref[:, columns] = sum_ref[:, columns] + branch if residual else branch

    return narrow


def teacher_body(samples, seq_len, base, where_ref, loads, ins, outs, scratch):
    target_ref = outs[0]
    narrow = feed_forward(samples, base, 0, loads, ins, False, scratch)
    rows, width = target_ref.shape[0] // samples, target_ref.shape[1]
    tiles(width, lambda columns: narrow(columns, target_ref, False))
    valid = lax.broadcasted_iota(jnp.int32, (rows, width), 0) < seq_len
    for s in range(samples):
        part = slice(s * rows, (s + 1) * rows)
        values = target_ref[part, :]
        total = jnp.sum(jnp.where(valid, values, 0.0), axis=0, keepdims=True)
        centred = values - total * (1.0 / seq_len)
        spread = jnp.sum(jnp.where(valid, centred * centred, 0.0), axis=0, keepdims=True)
        target_ref[part, :] = centred * lax.rsqrt(spread * (1.0 / seq_len) + ln_eps)


def student_body(samples, base, loss_scale, where_ref, loads, ins, outs, scratch):
    target_ref, mask_ref = ins[3:]
    final_ref, dy_ref, gb2_ref, g2_ref, act_ref, slope_ref, low_ref, hat_ref, inv_ref = outs[:9]
    rows_ref, loss_ref = outs[9:]
    sum_ref, hat2_ref, hatf_ref, gf_ref, inv2_ref, invf_ref = scratch
    narrow = feed_forward(
        samples, base, 1, loads, ins[:3], True, (sum_ref, low_ref, act_ref, hat_ref, inv_ref, slope_ref)
    )
    vec_ref = ins[2]
    squares = loads[0]()
    width = sum_ref.shape[1]
    rows = sum_ref.shape[0] // samples
    final_base = base + 12
    tiles(width, lambda columns: narrow(columns, gf_ref, True))
    for s in range(samples):
        part = slice(s * rows, (s + 1) * rows)
        hat, inverse = norm_parts(gf_ref[part, :])
        hat2_ref[part, :], inv2_ref[part, :] = hat, inverse
        result = hat * vec_ref[base + 6 : base + 7, :] + vec_ref[base + 7 : base + 8, :]
        hat, inverse = norm_parts(result)
        hatf_ref[part, :], invf_ref[part, :] = hat, inverse
        final_ref[part, :] = to_low(
            hat * vec_ref[final_base : final_base + 1, :]
            + vec_ref[final_base + 1 : final_base + 2, :]
        )
    rows_ref[...] = jnp.zeros_like(rows_ref)
    loss_ref[...] = jnp.zeros_like(loss_ref)

    def head(columns):
        output = matmul(final_ref[...], squares[2, :, columns])
        residue = output + vec_ref[final_base + 2 : final_base + 3, columns] - target_ref[:, columns]
        magnitude = jnp.abs(residue)
        terms = jnp.where(
            magnitude <= huber_delta,
            0.5 * residue * residue,
            huber_delta * (magnitude - 0.5 * huber_delta),
        )
        loss_ref[...] += jnp.sum(
            jnp.sum(terms * mask_ref[...], axis=0, keepdims=True), axis=1, keepdims=True
        )
        grad = to_low(jnp.clip(residue, -huber_delta, huber_delta) * mask_ref[...] * loss_scale)
        dy_ref[:, columns] = grad
        rows_ref[0:1, columns] = jnp.sum(grad.astype(F32), axis=0, keepdims=True)

    tiles(width, head)

    def back(columns):
        gf_ref[:, columns] = matmul_nt(dy_ref[...], squares[2, columns, :])

    tiles(width, back)
    for s in range(samples):
        part = slice(s * rows, (s + 1) * rows)
        grad, hat = gf_ref[part, :], hatf_ref[part, :]
        rows_ref[1:2, :] += jnp.sum(grad * hat, axis=0, keepdims=True)
        rows_ref[2:3, :] += jnp.sum(grad, axis=0, keepdims=True)
        grad = norm_back(grad, hat, invf_ref[part, :], vec_ref[final_base : final_base + 1, :])
        hat = hat2_ref[part, :]
        rows_ref[3:4, :] += jnp.sum(grad * hat, axis=0, keepdims=True)
        rows_ref[4:5, :] += jnp.sum(grad, axis=0, keepdims=True)
        grad = norm_back(grad, hat, inv2_ref[part, :], vec_ref[base + 6 : base + 7, :])
        g2_ref[part, :] = grad
        low = to_low(grad)
        gb2_ref[part, :] = low
        rows_ref[5:6, :] += jnp.sum(low.astype(F32), axis=0, keepdims=True)


def feed_back_body(samples, base, where_ref, loads, ins, outs, scratch):
    gb2_ref, g2_ref, slope_ref, hat_ref, inv_ref, vec_ref = ins
    gpre_ref, gfirst_ref, gbranch_ref, gatt_ref, rows_ref, up_ref = outs
    grad_ref = scratch[0]
    squares, up, down = loads
    down = down()
    width, hidden_units = down.shape
    rows = gb2_ref.shape[0] // samples

    def widen(columns):
        grad = to_low(matmul(gb2_ref[...], down[:, columns]) * slope_ref[:, columns])
        gpre_ref[:, columns] = grad
        up_ref[:, columns] = jnp.sum(grad.astype(F32), axis=0, keepdims=True)

    tiles(hidden_units, widen)
    up = up()

    def narrow(columns):
        grad_ref[:, columns] = g2_ref[:, columns] + matmul_nt(gpre_ref[...], up[columns, :])

    tiles(width, narrow)
    rows_ref[...] = jnp.zeros_like(rows_ref)
    for s in range(samples):
        part = slice(s * rows, (s + 1) * rows)
        grad, hat = grad_ref[part, :], hat_ref[part, :]
        rows_ref[0:1, :] += jnp.sum(grad * hat, axis=0, keepdims=True)
        rows_ref[1:2, :] += jnp.sum(grad, axis=0, keepdims=True)
        grad = norm_back(grad, hat, inv_ref[part, :], vec_ref[base + 3 : base + 4, :])
        gfirst_ref[part, :] = grad
        low = to_low(grad)
        gbranch_ref[part, :] = low
        rows_ref[2:3, :] += jnp.sum(low.astype(F32), axis=0, keepdims=True)
    squares = squares()

    def project(columns):
        gatt_ref[:, columns] = to_low(matmul_nt(gbranch_ref[...], squares[1, columns, :]))

    tiles(width, project)


def embed_back_body(samples, seq_len, base, where_ref, loads, ins, outs, scratch):
    gq_ref, gk_ref, gv_ref, gfirst_ref, mask_ref, after_ref, inner_ref, up_ref = ins
    ge_ref, pieces_ref = outs
    all_ref, pos_ref = scratch
    weights = loads[0]()
    width = gq_ref.shape[1]
    rows = gq_ref.shape[0] // samples

    def project(columns):
        grad = gfirst_ref[:, columns] + matmul_nt(gq_ref[...], weights[1, columns, :])
        grad += matmul_nt(gk_ref[...], weights[2, columns, :])
        grad += matmul_nt(gv_ref[...], weights[3, columns, :])
        hidden = grad * mask_ref[...]
        all_ref[1:2, columns] = jnp.sum(hidden, axis=0, keepdims=True)
        low = to_low(grad * (1.0 - mask_ref[...]))
        ge_ref[:, columns] = low
        all_ref[0:1, columns] = jnp.sum(low.astype(F32), axis=0, keepdims=True)
        total = grad[0:rows]
        for s in range(1, samples):
            total += grad[s * rows : (s + 1) * rows]
        pos_ref[:, columns] = total
        all_ref[base : base + 1, columns] = jnp.sum(
            gq_ref[:, columns].astype(F32), axis=0, keepdims=True
        )
        all_ref[base + 1 : base + 2, columns] = jnp.sum(
            gv_ref[:, columns].astype(F32), axis=0, keepdims=True
        )

    tiles(width, project)
    all_ref[2 : 2 + seq_len, :] = pos_ref[0:seq_len, :]
    all_ref[base + 2 : base + 3, :] = inner_ref[2:3, :]
    all_ref[base + 3 : base + 5, :] = inner_ref[0:2, :]
    all_ref[base + 5 : base + 6, :] = after_ref[5:6, :]
    all_ref[base + 6 : base + 8, :] = after_ref[3:5, :]
    for k in range(4):
        all_ref[base + 8 + k : base + 9 + k, :] = up_ref[:, k * width : (k + 1) * width]
    all_ref[base + 12 : base + 14, :] = after_ref[1:3, :]
    all_ref[base + 14 : base + 15, :] = after_ref[0:1, :]
    count, _, size = pieces_ref.shape
    for k in range(count):
        pieces_ref[jnp.bitwise_xor(where_ref[1], k)] = all_ref[:, k * size : (k + 1) * size]


def adam_step(master, moment_one, moment_two, gradient, factor):
    clipped = gradient * factor
    one_new = beta_one * moment_one + (1.0 - beta_one) * clipped
    two_new = beta_two * moment_two + (1.0 - beta_two) * clipped * clipped
    one_hat = one_new / (1.0 - beta_one**ADAM_STEP)
    two_hat = two_new / (1.0 - beta_two**ADAM_STEP)
    step_value = -learn_rate * (one_hat / (jnp.sqrt(two_hat) + adam_eps) + decay_rate * master)
    return (step_value, one_new, two_new)


def teacher_move(master, teacher, step_value):
    return (1.0 - ema_keep) * (master - teacher + step_value)


def per_device(
    patches,
    mask_places,
    square_weights,
    square_first,
    square_second,
    square_teacher,
    feed_weights,
    feed_first,
    feed_second,
    feed_teacher,
    vector_weights,
    vector_first,
    vector_second,
    vector_teacher,
):
    samples, seq_len, model_width = patches.shape
    total_masked = samples * mask_places.shape[1] * lax.axis_size("rep") * lax.axis_size("fsdp")
    rep, own = lax.axis_index("rep"), lax.axis_index("fsdp")
    where = jnp.stack([rep, own]).astype(jnp.int32)
    pad_len = -(-seq_len // 8) * 8
    row_count = samples * pad_len
    hidden_units = feed_weights.shape[3]
    patch_rows = jnp.pad(patches, ((0, 0), (0, pad_len - seq_len), (0, 0))).reshape(
        row_count, model_width
    )
    places = jnp.arange(pad_len, dtype=jnp.int32)
    mask_rows = jnp.sum(
        (mask_places[:, :, None] == places[None, None, :]).astype(F32), axis=1
    ).reshape(row_count, 1)

    def pick(array, index):
        return to_low(lax.dynamic_index_in_dim(array, index, keepdims=False))

    def columns_of(array, number):
        width = array.shape[3] // 4
        return to_low(lax.dynamic_slice_in_dim(array[0, number], rep * width, width, axis=1))

    vector_old_new = gather_vectors(jnp.stack([vector_weights, vector_teacher]), where)
    vector_all, vector_old = vector_old_new[0], vector_old_new[1]
    entry_t = Group(pick(square_teacher, rep), 0, False, where)
    entry_s = Group(pick(square_weights, rep), 1, False, where)
    others = jnp.where(
        rep == 0, to_low(square_teacher[4]), pick(square_weights, jnp.clip(rep + 3, 4, 5))
    )
    outer = Group(others, 0, False, where)
    up_t = Group(columns_of(feed_teacher, 0), 1, True, where)
    down_t = Group(columns_of(feed_teacher, 1), 0, True, where)
    up_s = Group(columns_of(feed_weights, 0), 1, True, where)
    down_s = Group(columns_of(feed_weights, 1), 0, True, where)
    base = 2 + seq_len
    wide, square = 2 * row_count * model_width * hidden_units, 2 * row_count * model_width**2

    def positions(vector):
        return jnp.pad(vector[2 : 2 + seq_len], ((0, pad_len - seq_len), (0, 0)))

    full, low_full = ((row_count, model_width), F32), ((row_count, model_width), BF16)
    low_wide, full_wide = ((row_count, hidden_units), BF16), ((row_count, hidden_units), F32)
    column = ((row_count, 1), F32)

    def entry(group, vector, masked, name):
        return call(
            functools.partial(embed_body, samples, masked, base),
            name,
            where,
            [group],
            [patch_rows, vector, positions(vector)] + ([mask_rows] if masked else []),
            [full] + [low_full] * 4,
            flops=4 * square,
        )

    hidden_t, _, query, key_rows, value_rows = entry(entry_t, vector_old, False, "embed_t")
    attended, _ = attention_forward(query, key_rows, value_rows, samples, seq_len)
    (target,) = call(
        functools.partial(teacher_body, samples, seq_len, base),
        "layer_t",
        where,
        [outer, up_t, down_t],
        [attended, hidden_t, vector_old],
        [full],
        [pltpu.VMEM(*full), pltpu.VMEM(*low_full), pltpu.VMEM(*low_wide)],
        flops=square + 2 * wide,
    )
    hidden, hidden_low, query, key_rows, value_rows = entry(entry_s, vector_all, True, "embed_s")
    attended, logsum = attention_forward(query, key_rows, value_rows, samples, seq_len)
    loss_scale = 1.0 / (total_masked * model_width)
    (
        final_low,
        grad_output,
        grad_branch_two,
        grad_second,
        activation,
        slope,
        normed_low,
        hat_first,
        inverse_first,
        rows_after,
        loss_sum,
    ) = call(
        functools.partial(student_body, samples, base, loss_scale),
        "layer_s",
        where,
        [outer, up_s, down_s],
        [attended, hidden, vector_all, target, mask_rows],
        [low_full] * 3
        + [full, low_wide, full_wide, low_full, full, column, ((8, model_width), F32), ((1, 1), F32)],
        [pltpu.VMEM(*full)] * 4 + [pltpu.VMEM(*column)] * 2,
        flops=3 * square + 2 * wide,
    )
    loss_local = loss_sum[0, 0] * loss_scale

    unit = model_width
    quarters = [[(k * unit, k) for k in range(4)]]
    down_g = unit_grads([(grad_branch_two, activation)], quarters, 0, unit, where)
    grad_branch_two, *down_g = lax.optimization_barrier((grad_branch_two, *down_g))
    grad_pre, grad_first, grad_branch, grad_attended, rows_inner, rows_up = call(
        functools.partial(feed_back_body, samples, base),
        "feed_back",
        where,
        [outer, up_s, down_s],
        [grad_branch_two, grad_second, slope, hat_first, inverse_first, vector_all],
        [low_wide, full, low_full, low_full, ((8, model_width), F32), ((1, hidden_units), F32)],
        [pltpu.VMEM(*full)],
        flops=square + 2 * wide,
    )
    up_g = unit_grads([(normed_low, grad_pre)], quarters, 1, unit, where)
    halves = [[(0, 0), (unit // 2, 1)], [(0, 2), (unit // 2, 3)]]
    edge_g = unit_grads(
        [(final_low, grad_output), (attended, grad_branch)], halves, 0, unit // 2, where
    )
    grad_attended, *both = lax.optimization_barrier((grad_attended, *up_g, *edge_g))
    up_g, edge_g = both[:2], both[2:]
    grad_query, grad_key, grad_value = attention_backward(
        query, key_rows, value_rows, logsum, grad_attended, samples, seq_len
    )
    vector_count = vector_all.shape[0]
    count = lax.axis_size("fsdp")
    grad_embed, pieces = call(
        functools.partial(embed_back_body, samples, seq_len, base),
        "embed_back",
        where,
        [entry_s],
        [grad_query, grad_key, grad_value, grad_first, mask_rows, rows_after, rows_inner, rows_up],
        [low_full, ((count, vector_count, model_width // count), F32)],
        [pltpu.VMEM((vector_count, model_width), F32), pltpu.VMEM((pad_len, model_width), F32)],
        flops=3 * square,
    )
    singles = [[(0, k)] for k in range(4)]
    qkv_g = unit_grads(
        [(hidden_low, grad_query), (hidden_low, grad_key), (hidden_low, grad_value), (patch_rows, grad_embed)],
        singles,
        1,
        unit,
        where,
    )

    down_own = reduce_units(*down_g, 0)
    up_own = reduce_units(*up_g, 1)
    edge_own = reduce_units(*edge_g, 0)
    qkv_own = reduce_units(*qkv_g, 1)
    for bit in fsdp_bits():
        half = pieces.shape[0] // 2
        pieces = pieces[:half] + swap(pieces[half:], ("fsdp", bit))
    vector_share = pieces[0]
    for bit in (2, 1):
        vector_share = vector_share + swap(vector_share, ("rep", bit))
    squares_own = (
        jnp.sum(down_own * down_own)
        + jnp.sum(up_own * up_own)
        + jnp.sum(edge_own * edge_own)
        + jnp.sum(qkv_own * qkv_own)
        + 0.25 * jnp.sum(vector_share * vector_share)
    )
    totals = jnp.stack([squares_own, loss_local])
    for bit in fsdp_bits():
        totals = totals + swap(totals, ("fsdp", bit))
    for bit in (2, 1):
        totals = totals + swap(totals, ("rep", bit))
    norm_squared, loss_value = totals[0], totals[1]

    def ordered(own_units):
        shared = share_units(own_units)
        return [lax.dynamic_index_in_dim(shared, rep ^ k, keepdims=False) for k in range(4)]

    down_u, up_u, edge_u, qkv_u = ordered(down_own), ordered(up_own), ordered(edge_own), ordered(qkv_own)
    feed_grad = jnp.stack([jnp.concatenate(up_u, axis=1), jnp.concatenate(down_u, axis=1)])[None]
    square_grad = jnp.stack(
        [
            qkv_u[3],
            qkv_u[0],
            qkv_u[1],
            qkv_u[2],
            jnp.concatenate(edge_u[2:], axis=1),
            jnp.concatenate(edge_u[:2], axis=1),
        ]
    )
    grad_norm = jnp.sqrt(norm_squared)
    limit = clip_scale / math.sqrt(total_masked)
    factor = limit / jnp.maximum(grad_norm, limit)
    square_step, square_one, square_two = adam_step(
        square_weights, square_first, square_second, square_grad, factor
    )
    feed_step, feed_one, feed_two = adam_step(
        feed_weights, feed_first, feed_second, feed_grad, factor
    )
    vector_step, vector_one, vector_two = adam_step(
        vector_weights, vector_first, vector_second, vector_share, factor
    )
    square_moved = teacher_move(square_weights, square_teacher, square_step)
    feed_moved = teacher_move(feed_weights, feed_teacher, feed_step)
    vector_moved = teacher_move(vector_weights, vector_teacher, vector_step)
    return (
        loss_value,
        grad_norm,
        square_step,
        square_one,
        square_two,
        square_moved,
        feed_step,
        feed_one,
        feed_two,
        feed_moved,
        vector_step,
        vector_one,
        vector_two,
        vector_moved,
    )


def solution(mesh):
    placed = (
        P(("rep", "fsdp"), None, None),
        P(("rep", "fsdp"), None),
        P(None, "fsdp", None),
        P(None, "fsdp", None),
        P(None, "fsdp", None),
        P(None, "fsdp", None),
        P(None, None, "fsdp", None),
        P(None, None, "fsdp", None),
        P(None, None, "fsdp", None),
        P(None, None, "fsdp", None),
        P(None, "fsdp"),
        P(None, "fsdp"),
        P(None, "fsdp"),
        P(None, "fsdp"),
    )
    return jax.shard_map(
        per_device,
        mesh=mesh,
        in_specs=placed,
        out_specs=(
            P(),
            P(),
            P(None, "fsdp", None),
            P(None, "fsdp", None),
            P(None, "fsdp", None),
            P(None, "fsdp", None),
            P(None, None, "fsdp", None),
            P(None, None, "fsdp", None),
            P(None, None, "fsdp", None),
            P(None, None, "fsdp", None),
            P(None, "fsdp"),
            P(None, "fsdp"),
            P(None, "fsdp"),
            P(None, "fsdp"),
        ),
        check_vma=False,
    )
```

time: 1490 us -> 760 us (0.51)
  waiting for transfers between devices: 934 us -> 399 us
  local copies, waits for them, and re-layouts: 241 us -> 20 us
  Pallas kernels: 0 us -> 179 us
  matrix products: 137 us -> 0 us
  blocking collectives: 97 us -> 0 us
  starting transfers between devices: 0.99 us -> 97.4 us
    ppermute x0 -> x87, waiting for transfers between devices: none -> 399 us  [swap(): lax.ppermute(values, axis, [(i, i ^ bit) for i in range(lax.axis_size(axi...]
    all_gather x8 -> x0, waiting for transfers between devices: 387 us -> none  [the longest x1 113 us: per_device(): lax.all_gather(to_low(feed_teacher[layer_index]), 'fsdp', axis=1, tiled=T...]
    unnamed x17 -> x0, waiting for transfers between devices: 270 us -> none
    pallas_call x0 -> x14, Pallas kernels: none -> 179 us  [the longest x6 106 us: call(): pl.pallas_call(kernel, out_shape=tuple((jax.ShapeDtypeStruct(*out) for ou...]
    psum x1 -> x0, waiting for transfers between devices: 165 us -> none  [per_device(): lax.psum((end_share, vector_share, loss_local), 'rep')]
    dot_general x37 -> x0, matrix products: 137 us -> none  [the longest x13 61.7 us: matmul(): return jnp.dot(left, right, preferred_element_type=jnp.float32)]
    unnamed x252 -> x90, local copies, waits for them, and re-layouts: 141 us -> 6.37 us
    reduce_scatter x2 -> x0, waiting for transfers between devices: 113 us -> none  [the longest x1 79.4 us: per_device(): lax.psum_scatter(feed_cols, 'fsdp', scatter_dimension=1, tiled=True)]
  transfers between devices with their start and end apart: 14 -> 87, of which waited for: 13 -> 37; matrix products, arithmetic and copies ran while one was open for 20% -> 7% of each run, Pallas kernels for 0% -> 8%
where the time goes in v1:
time: 760 us; the launch traced here: 753 us
  waiting for transfers between devices  399 us (52%)
  Pallas kernels  179 us (24%)
  starting transfers between devices  97.4 us (13%)
  other arithmetic  51 us (7%)
  local copies, waits for them, and re-layouts  20 us (3%)
  between operations  7.83 us (1%)
    ppermute x87, waiting for transfers between devices, swap(): lax.ppermute(values, axis, [(i, i ^ bit) for i in range(lax.axis_size(axi...  399 us
    pallas_call x6, Pallas kernels, call(): pl.pallas_call(kernel, out_shape=tuple((jax.ShapeDtypeStruct(*out) for ou...  106 us
    ppermute x87, starting transfers between devices, swap(): lax.ppermute(values, axis, [(i, i ^ bit) for i in range(lax.axis_size(axi...  97.4 us
    pallas_call x4, Pallas kernels, unit_grads(): pl.pallas_call(functools.partial(grad_kernel, unit_of, reduce_order(kind)...  39.1 us
    add x12, other arithmetic, reduce_units(): keep = keep[:half] + got[:half]  22.5 us
    pallas_call x1, Pallas kernels, attention_backward(): pl.pallas_call(functools.partial(attention_back_kernel, seq_len, head_dim...  15.9 us
  transfers between devices with their start and end apart: 87, of which 37 were waited for; matrix products, arithmetic and copies ran while one was open for 7% of the time, Pallas kernels for 8%

profile of v1, /device:TPU:0, one launch (start us, length us, event | category | flops | bytes accessed | tf_op | source)
XLA Modules:
  0.0 753.5 jit_solution(18421286141746336426)
XLA Ops:
  45.9 9.7 %collective-permute-done.1 = bf16[192,768]{1,0:T(8,128)(2,1)S(1)} collective-permute-done((bf16[192,768]{1,0:T(8,128)(2,1)S(1)}, bf16[192,768]{1,0:T(8,128)(2,1)S(1)}, u32[]{:S(2)}, u32[]{:S(2)}) %collective-permute-start.1) | collective-permute-done | bytes 294944 | tf_op jit(solution)/shard_map/ppermute | solution.py:100
  84.2 17.1 %collective-permute-done.28 = bf16[192,768]{1,0:T(8,128)(2,1)S(1)} collective-permute-done((bf16[192,768]{1,0:T(8,128)(2,1)S(1)}, bf16[192,768]{1,0:T(8,128)(2,1)S(1)}, u32[]{:S(2)}, u32[]{:S(2)}) %collective-permute-start.28) | collective-permute-done | bytes 294944 | tf_op jit(solution)/shard_map/ppermute | solution.py:100
  121.0 28.1 %collective-permute-done.20 = bf16[384,768]{1,0:T(8,128)(2,1)S(1)} collective-permute-done((bf16[384,768]{1,0:T(8,128)(2,1)S(1)}, bf16[384,768]{1,0:T(8,128)(2,1)S(1)}, u32[]{:S(2)}, u32[]{:S(2)}) %collective-permute-start.20) | collective-permute-done | bytes 589856 | tf_op jit(solution)/shard_map/ppermute | solution.py:100
  165.3 22.4 %collective-permute-done.9.refs_5_ = bf16[768,768]{1,0:T(8,128)(2,1)} collective-permute-done((bf16[768,768]{1,0:T(8,128)(2,1)S(1)}, bf16[768,768]{1,0:T(8,128)(2,1)}, u32[]{:S(2)}, u32[]{:S(2)}) %collective-permute-start.9) | collective-permute-done | bytes 1179680 | tf_op jit(solution)/shard_map/ppermute | solution.py:100
  189.4 23.7 %collective-permute-done.21.refs_1_ = bf16[768,768]{1,0:T(8,128)(2,1)} collective-permute-done((bf16[768,768]{1,0:T(8,128)(2,1)S(1)}, bf16[768,768]{1,0:T(8,128)(2,1)}, u32[]{:S(2)}, u32[]{:S(2)}) %collective-permute-start.21) | collective-permute-done | bytes 1179680 | tf_op jit(solution)/shard_map/ppermute | solution.py:100
  215.6 18.9 %collective-permute-done.30.refs_5_ = bf16[768,768]{1,0:T(8,128)(2,1)} collective-permute-done((bf16[768,768]{1,0:T(8,128)(2,1)S(1)}, bf16[768,768]{1,0:T(8,128)(2,1)}, u32[]{:S(2)}, u32[]{:S(2)}) %collective-permute-start.30) | collective-permute-done | bytes 1179680 | tf_op jit(solution)/shard_map/ppermute | solution.py:100
  256.4 9.3 %embed_s.1 = (f32[504,768]{1,0:T(8,128)}, bf16[504,768]{1,0:T(8,128)(2,1)}, bf16[504,768]{1,0:T(8,128)(2,1)}, bf16[504,768]{1,0:T(8,128)(2,1)}, bf16[504,768]{1,0:T(8,128)(2,1)}) custom-call(s32[2]{0:T(128)} %pad_add_fusion.where_ref, bf16[768,768]{1,0:T(8,128)(2,1)} %copy-done.4, bf16[768,768]{1,0:T(8,128)(2,1)} %collective-permute-done.21.refs_1_, ...), custom_call_target="tpu_custom_call" | custom-call | flops 2378170368 | bytes 1048576 | tf_op jit(solution)/shard_map/embed_s/pallas_call | solution.py:203
  273.1 9.1 %embed_t.1 = (f32[504,768]{1,0:T(8,128)}, bf16[504,768]{1,0:T(8,128)(2,1)}, bf16[504,768]{1,0:T(8,128)(2,1)}, bf16[504,768]{1,0:T(8,128)(2,1)}, bf16[504,768]{1,0:T(8,128)(2,1)}) custom-call(s32[2]{0:T(128)} %pad_add_fusion.where_ref, bf16[768,768]{1,0:T(8,128)(2,1)} %pad_maximum_fusion.7.refs_0_, bf16[768,768]{1,0:T(8,128)(2,1)} %collective-permute-done.42.refs_1_, ...), custom_call_target="tpu_custom_call" | custom-call | flops 2378170368 | bytes 1048576 | tf_op jit(solution)/shard_map/embed_t/pallas_call | solution.py:203
  289.5 23.5 %layer_t.1.refs_15_ = f32[504,768]{1,0:T(8,128)} custom-call(s32[2]{0:T(128)} %pad_add_fusion.where_ref, bf16[768,768]{1,0:T(8,128)(2,1)} %copy-done.3, bf16[768,768]{1,0:T(8,128)(2,1)} %collective-permute-done.3.refs_1_, bf16[768,768]{1,0:T(8,128)(2,1)} %copy-done.25, bf16[768,768]{1,0:T(8,128)(2,1)} %collective-permute-done.5.refs_3_, ...), custom_call_target="tpu_custom_call" | custom-call | flops 5350883328 | bytes 1048576 | tf_op jit(solution)/shard_map/layer_t/pallas_call | solution.py:203
  313.1 33.0 %layer_s.1 = (bf16[504,768]{1,0:T(8,128)(2,1)}, bf16[504,768]{1,0:T(8,128)(2,1)}, bf16[504,768]{1,0:T(8,128)(2,1)}, f32[504,768]{1,0:T(8,128)}, bf16[504,3072]{1...) custom-call(s32[2]{0:T(128)} %pad_add_fusion.where_ref, ...), custom_call_target="tpu_custom_call" | custom-call | flops 6539968512 | bytes 1048576 | tf_op jit(solution)/shard_map/layer_s/pallas_call | solution.py:203
  346.1 10.5 %unit_grads.4 = (f32[1536,768]{1,0:T(8,128)}, f32[1536,768]{1,0:T(8,128)}) custom-call(s32[2]{0:T(128)} %pad_add_fusion.where_ref, bf16[504,768]{1,0:T(8,128)(2,1)} %get-tuple-element.80.refs_0_.refs_12_, bf16[504,3072]{1,0:T(8,128)(2,1)} %get-tuple-element.75.refs_1_), custom_call_target="tpu_custom_call" | custom-call | flops 2378170368 | bytes 9437184 | tf_op jit(solution)/shard_map/unit_grads/pallas_call | solution.py:277
  356.6 22.4 %feed_back.1 = (bf16[504,3072]{1,0:T(8,128)(2,1)}, f32[504,768]{1,0:T(8,128)}, bf16[504,768]{1,0:T(8,128)(2,1)}, bf16[504,768]{1,0:T(8,128)(2,1)}, f32[8,768]{1,0:T(8,128)}, /*index=5*/f32[1,3072]{1,0:T(1,128)}) custom-call(s32[2]{0:T(128)} %pad_add_fusion.where_ref, bf16[768,768]{1,0:T(8,128)(2,1)} %copy-done.3, ...), custom_call_target="tpu_custom_call" | custom-call | flops 5350883328 | bytes 1048576 | tf_op jit(solution)/shard_map/feed_back/pallas_call | solution.py:203
  379.0 10.3 %unit_grads.5 = (f32[1536,768]{1,0:T(8,128)}, f32[1536,768]{1,0:T(8,128)}) custom-call(s32[2]{0:T(128)} %pad_add_fusion.where_ref, bf16[504,768]{1,0:T(8,128)(2,1)} %get-tuple-element.86.refs_0_, bf16[504,3072]{1,0:T(8,128)(2,1)} %get-tuple-element.87.refs_1_), custom_call_target="tpu_custom_call" | custom-call | flops 2378170368 | bytes 9437184 | tf_op jit(solution)/shard_map/unit_grads/pallas_call | solution.py:277
  396.3 15.9 %attention_back.1 = (bf16[504,768]{1,0:T(8,128)(2,1)}, bf16[504,768]{1,0:T(8,128)(2,1)}, bf16[504,768]{1,0:T(8,128)(2,1)}) custom-call(bf16[504,768]{1,0:T(8,128)(2,1)} %get-tuple-element.64.q_ref, bf16[504,768]{1,0:T(8,128)(2,1)} %get-tuple-element.65.k_ref, bf16[504,768]{1,0:T(8,128)(2,1)} %get-tuple-element.66.v_ref, ...), custom_call_target="tpu_custom_call" | custom-call | flops 650280960 | bytes 5419008 | tf_op jit(solution)/shard_map/attention_back/pallas_call | solution.py:393
  421.1 11.3 %unit_grads.7 = (f32[1536,768]{1,0:T(8,128)}, f32[1536,768]{1,0:T(8,128)}) custom-call(s32[2]{0:T(128)} %pad_add_fusion.where_ref, bf16[504,768]{1,0:T(8,128)(2,1)} %get-tuple-element.99.refs_0_.refs_1_.refs_2_, bf16[504,768]{1,0:T(8,128)(2,1)} %get-tuple-element.99.refs_0_.refs_1_.refs_2_, bf16[504,768]{1,0:T(8,128)(2,1)} %get-tuple-element.99.refs_0_.refs_1_.refs_2_, ...), custom_call_target="tpu_custom_call" | custom-call | flops 2378170368 | bytes 9437184 | tf_op jit(solution)/shard_map/unit_grads/pallas_call | solution.py:277
  433.5 17.2 %collective-permute-done.55 = f32[1536,384]{1,0:T(8,128)S(1)} collective-permute-done((f32[1536,384]{1,0:T(8,128)}, f32[1536,384]{1,0:T(8,128)S(1)}, u32[]{:S(2)}, u32[]{:S(2)}) %collective-permute-start.55) | collective-permute-done | bytes 2359328 | tf_op jit(solution)/shard_map/ppermute | solution.py:100
  454.4 26.5 %collective-permute-done.56 = f32[768,384]{1,0:T(8,128)S(1)} collective-permute-done((f32[768,384]{1,0:T(8,128)S(1)}, f32[768,384]{1,0:T(8,128)S(1)}, u32[]{:S(2)}, u32[]{:S(2)}) %collective-permute-start.56) | collective-permute-done | bytes 1179680 | tf_op jit(solution)/shard_map/ppermute | solution.py:100
  502.3 12.6 %collective-permute-done.65 = f32[4,184,96]{2,1,0:T(8,128)S(1)} collective-permute-done((f32[4,184,96]{2,1,0:T(8,128)S(1)}, f32[4,184,96]{2,1,0:T(8,128)S(1)}, u32[]{:S(2)}, u32[]{:S(2)}) %collective-permute-start.65) | collective-permute-done | bytes 282656 | tf_op jit(solution)/shard_map/ppermute | solution.py:100
  526.5 21.4 %collective-permute-done.61 = f32[768,768]{1,0:T(8,128)} collective-permute-done((f32[768,768]{1,0:T(8,128)}, f32[768,768]{1,0:T(8,128)}, u32[]{:S(2)}, u32[]{:S(2)}) %collective-permute-start.61) | collective-permute-done | bytes 2359328 | tf_op jit(solution)/shard_map/ppermute | solution.py:100
  555.6 42.8 %collective-permute-done.51 = f32[768,768]{1,0:T(8,128)S(1)} collective-permute-done((f32[768,768]{1,0:T(8,128)S(1)}, f32[768,768]{1,0:T(8,128)S(1)}, u32[]{:S(2)}, u32[]{:S(2)}) %collective-permute-start.51) | collective-permute-done | bytes 2359328 | tf_op jit(solution)/shard_map/ppermute | solution.py:100
  602.2 24.7 %collective-permute-done.68 = f32[184,96]{1,0:T(8,128)S(1)} collective-permute-done((f32[184,96]{1,0:T(8,128)S(1)}, f32[184,96]{1,0:T(8,128)S(1)}, u32[]{:S(2)}, u32[]{:S(2)}) %collective-permute-start.68) | collective-permute-done | bytes 70688 | tf_op jit(solution)/shard_map/ppermute | solution.py:100
  641.2 10.3 %collective-permute-done.63 = f32[192,768]{1,0:T(8,128)S(1)} collective-permute-done((f32[192,768]{1,0:T(8,128)S(1)}, f32[192,768]{1,0:T(8,128)S(1)}, u32[]{:S(2)}, u32[]{:S(2)}) %collective-permute-start.63) | collective-permute-done | bytes 589856 | tf_op jit(solution)/shard_map/ppermute | solution.py:100
  655.9 14.6 %collective-permute-done.48 = f32[192,768]{1,0:T(8,128)S(1)} collective-permute-done((f32[192,768]{1,0:T(8,128)S(1)}, f32[192,768]{1,0:T(8,128)S(1)}, u32[]{:S(2)}, u32[]{:S(2)}) %collective-permute-start.48) | collective-permute-done | bytes 589856 | tf_op jit(solution)/shard_map/ppermute | solution.py:100
  674.4 14.2 %collective-permute-done.53 = f32[192,768]{1,0:T(8,128)S(1)} collective-permute-done((f32[192,768]{1,0:T(8,128)S(1)}, f32[192,768]{1,0:T(8,128)S(1)}, u32[]{:S(2)}, u32[]{:S(2)}) %collective-permute-start.53) | collective-permute-done | bytes 589856 | tf_op jit(solution)/shard_map/ppermute | solution.py:100
  (344 shorter events, 296.1 us)
Async XLA Ops:
  76.4 42.0 %collective-permute-start.26 = (f32[4,2,184,96]{3,2,1,0:T(8,128)S(1)}, f32[4,2,184,96]{3,2,1,0:T(8,128)S(1)}, u32[]{:S(2)}, u32[]{:S(2)}) collective-permute-start(f32[4,2,184,96]{3,2,1,0:T(8,128)S(1)} %pad_maximum_fusion.11), channel_id=1, source_target_pairs={{0,4},{1,5},{2,6},{3,7},{4,0},{5,1},{6,2},{7,3},{8,12},{9,13},{10,... | collective-permute-start | bytes 1695752 | tf_op jit(solution)/shard_map/ppermute | solution.py:100
  107.6 54.8 %collective-permute-start.3 = (bf16[768,768]{1,0:T(8,128)(2,1)S(1)}, bf16[768,768]{1,0:T(8,128)(2,1)}, u32[]{:S(2)}, u32[]{:S(2)}) collective-permute-start(bf16[768,768]{1,0:T(8,128)(2,1)S(1)} %pad_maximum_fusion.1.refs_0_), channel_id=1, source_target_pairs={{0,16},{8,24},{16,0},{24,8},{1,17},{9,25},{17,1},{25,9},{2,18},{10... | collective-permute-start | bytes 3538952 | tf_op jit(solution)/shard_map/ppermute | solution.py:100
  119.0 41.4 %collective-permute-start.35 = (bf16[384,768]{1,0:T(8,128)(2,1)S(1)}, bf16[384,768]{1,0:T(8,128)(2,1)S(1)}, u32[]{:S(2)}, u32[]{:S(2)}) collective-permute-start(bf16[384,768]{1,0:T(8,128)(2,1)S(1)} %pad_maximum_fusion.17), channel_id=1, source_target_pairs={{0,1},{1,0},{2,3},{3,2},{4,5},{5,4},{6,7},{7,6},{8,9},{9,8},{10,11... | collective-permute-start | bytes 1769480 | tf_op jit(solution)/shard_map/ppermute | solution.py:100
  161.9 51.2 %collective-permute-start.21 = (bf16[768,768]{1,0:T(8,128)(2,1)S(1)}, bf16[768,768]{1,0:T(8,128)(2,1)}, u32[]{:S(2)}, u32[]{:S(2)}) collective-permute-start(bf16[768,768]{1,0:T(8,128)(2,1)S(1)} %pad_maximum_fusion.4.refs_0_), channel_id=1, source_target_pairs={{0,1},{1,0},{2,3},{3,2},{4,5},{5,4},{6,7},{7,6},{8,9},{9,8},{10,11... | collective-permute-start | bytes 3538952 | tf_op jit(solution)/shard_map/ppermute | solution.py:100
  162.4 50.7 %collective-permute-start.22 = (bf16[768,768]{1,0:T(8,128)(2,1)S(1)}, bf16[768,768]{1,0:T(8,128)(2,1)S(1)}, u32[]{:S(2)}, u32[]{:S(2)}) collective-permute-start(bf16[768,768]{1,0:T(8,128)(2,1)S(1)} %pad_maximum_fusion.4.refs_0_), channel_id=1, source_target_pairs={{0,8},{8,0},{16,24},{24,16},{1,9},{9,1},{17,25},{25,17},{2,10},{10... | collective-permute-start | bytes 3538952 | tf_op jit(solution)/shard_map/ppermute | solution.py:100
  162.5 72.0 %collective-permute-start.30 = (bf16[768,768]{1,0:T(8,128)(2,1)S(1)}, bf16[768,768]{1,0:T(8,128)(2,1)}, u32[]{:S(2)}, u32[]{:S(2)}) collective-permute-start(bf16[768,768]{1,0:T(8,128)(2,1)S(1)} %pad_maximum_fusion.5.refs_4_), channel_id=1, source_target_pairs={{0,1},{1,0},{2,3},{3,2},{4,5},{5,4},{6,7},{7,6},{8,9},{9,8},{10,11... | collective-permute-start | bytes 3538952 | tf_op jit(solution)/shard_map/ppermute | solution.py:100
  187.8 46.8 %collective-permute-start.31 = (bf16[768,768]{1,0:T(8,128)(2,1)S(1)}, bf16[768,768]{1,0:T(8,128)(2,1)S(1)}, u32[]{:S(2)}, u32[]{:S(2)}) collective-permute-start(bf16[768,768]{1,0:T(8,128)(2,1)S(1)} %pad_maximum_fusion.5.refs_4_), channel_id=1, source_target_pairs={{0,8},{8,0},{16,24},{24,16},{1,9},{9,1},{17,25},{25,17},{2,10},{10... | collective-permute-start | bytes 3538952 | tf_op jit(solution)/shard_map/ppermute | solution.py:100
  187.8 47.3 %collective-permute-start.36 = (bf16[768,768]{1,0:T(8,128)(2,1)S(1)}, bf16[768,768]{1,0:T(8,128)(2,1)S(1)}, u32[]{:S(2)}, u32[]{:S(2)}) collective-permute-start(bf16[768,768]{1,0:T(8,128)(2,1)S(1)} %pad_maximum_fusion.6.refs_8_), channel_id=1, source_target_pairs={{0,16},{8,24},{16,0},{24,8},{1,17},{9,25},{17,1},{25,9},{2,18},{10... | collective-permute-start | bytes 3538952 | tf_op jit(solution)/shard_map/ppermute | solution.py:100
  243.0 46.5 %collective-permute-start.38 = (bf16[768,768]{1,0:T(8,128)(2,1)}, bf16[768,768]{1,0:T(8,128)(2,1)}, u32[]{:S(2)}, u32[]{:S(2)}) collective-permute-start(bf16[768,768]{1,0:T(8,128)(2,1)} %copy-done.37), channel_id=1, source_target_pairs={{0,8},{8,0},{16,24},{24,16},{1,9},{9,1},{17,25},{25,17},{2,10},{10... | collective-permute-start | bytes 3538952 | tf_op jit(solution)/shard_map/ppermute | solution.py:100
  254.3 58.7 %collective-permute-start.10 = (bf16[768,768]{1,0:T(8,128)(2,1)S(1)}, bf16[768,768]{1,0:T(8,128)(2,1)}, u32[]{:S(2)}, u32[]{:S(2)}) collective-permute-start(bf16[768,768]{1,0:T(8,128)(2,1)S(1)} %copy-done.6), channel_id=1, source_target_pairs={{0,8},{8,0},{16,24},{24,16},{1,9},{9,1},{17,25},{25,17},{2,10},{10... | collective-permute-start | bytes 3538952 | tf_op jit(solution)/shard_map/ppermute | solution.py:100
  254.3 58.7 %collective-permute-start.16 = (bf16[768,768]{1,0:T(8,128)(2,1)}, bf16[768,768]{1,0:T(8,128)(2,1)}, u32[]{:S(2)}, u32[]{:S(2)}) collective-permute-start(bf16[768,768]{1,0:T(8,128)(2,1)} %pad_maximum_fusion.3.refs_8_), channel_id=1, source_target_pairs={{0,8},{8,0},{16,24},{24,16},{1,9},{9,1},{17,25},{25,17},{2,10},{10... | collective-permute-start | bytes 3538952 | tf_op jit(solution)/shard_map/ppermute | solution.py:100
  254.8 58.2 %collective-permute-start.11 = (bf16[768,768]{1,0:T(8,128)(2,1)}, bf16[768,768]{1,0:T(8,128)(2,1)}, u32[]{:S(2)}, u32[]{:S(2)}) collective-permute-start(bf16[768,768]{1,0:T(8,128)(2,1)} %collective-permute-done.9.refs_5_), channel_id=1, source_target_pairs={{0,8},{8,0},{16,24},{24,16},{1,9},{9,1},{17,25},{25,17},{2,10},{10... | collective-permute-start | bytes 3538952 | tf_op jit(solution)/shard_map/ppermute | solution.py:100
  254.9 58.2 %collective-permute-start.17 = (bf16[768,768]{1,0:T(8,128)(2,1)}, bf16[768,768]{1,0:T(8,128)(2,1)}, u32[]{:S(2)}, u32[]{:S(2)}) collective-permute-start(bf16[768,768]{1,0:T(8,128)(2,1)} %collective-permute-done.15.refs_9_), channel_id=1, source_target_pairs={{0,8},{8,0},{16,24},{24,16},{1,9},{9,1},{17,25},{25,17},{2,10},{10... | collective-permute-start | bytes 3538952 | tf_op jit(solution)/shard_map/ppermute | solution.py:100
  432.5 50.1 %collective-permute-start.60 = (f32[1536,768]{1,0:T(8,128)}, f32[1536,768]{1,0:T(8,128)}, u32[]{:S(2)}, u32[]{:S(2)}) collective-permute-start(f32[1536,768]{1,0:T(8,128)} %get-tuple-element.111), channel_id=1, source_target_pairs={{0,8},{8,0},{16,24},{24,16},{1,9},{9,1},{17,25},{25,17},{2,10},{10... | collective-permute-start | bytes 14155784 | tf_op jit(solution)/shard_map/ppermute | solution.py:100
  432.6 55.1 %collective-permute-start.45 = (f32[1536,768]{1,0:T(8,128)}, f32[1536,768]{1,0:T(8,128)}, u32[]{:S(2)}, u32[]{:S(2)}) collective-permute-start(f32[1536,768]{1,0:T(8,128)} %get-tuple-element.79), channel_id=1, source_target_pairs={{0,8},{8,0},{16,24},{24,16},{1,9},{9,1},{17,25},{25,17},{2,10},{10... | collective-permute-start | bytes 14155784 | tf_op jit(solution)/shard_map/ppermute | solution.py:100
  433.1 60.5 %collective-permute-start.50 = (f32[1536,768]{1,0:T(8,128)}, f32[1536,768]{1,0:T(8,128)S(1)}, u32[]{:S(2)}, u32[]{:S(2)}) collective-permute-start(f32[1536,768]{1,0:T(8,128)} %get-tuple-element.96), channel_id=1, source_target_pairs={{0,8},{8,0},{16,24},{24,16},{1,9},{9,1},{17,25},{25,17},{2,10},{10... | collective-permute-start | bytes 14155784 | tf_op jit(solution)/shard_map/ppermute | solution.py:100
  487.2 60.7 %collective-permute-start.61 = (f32[768,768]{1,0:T(8,128)}, f32[768,768]{1,0:T(8,128)}, u32[]{:S(2)}, u32[]{:S(2)}) collective-permute-start(f32[768,768]{1,0:T(8,128)} %get-tuple-element.137), channel_id=1, source_target_pairs={{0,1},{1,0},{2,3},{3,2},{4,5},{5,4},{6,7},{7,6},{8,9},{9,8},{10,11... | collective-permute-start | bytes 7077896 | tf_op jit(solution)/shard_map/ppermute | solution.py:100
  492.1 60.3 %collective-permute-start.46 = (f32[768,768]{1,0:T(8,128)}, f32[768,768]{1,0:T(8,128)S(1)}, u32[]{:S(2)}, u32[]{:S(2)}) collective-permute-start(f32[768,768]{1,0:T(8,128)} %get-tuple-element.141), channel_id=1, source_target_pairs={{0,16},{8,24},{16,0},{24,8},{1,17},{9,25},{17,1},{25,9},{2,18},{10... | collective-permute-start | bytes 7077896 | tf_op jit(solution)/shard_map/ppermute | solution.py:100
  494.2 104.1 %collective-permute-start.51 = (f32[768,768]{1,0:T(8,128)S(1)}, f32[768,768]{1,0:T(8,128)S(1)}, u32[]{:S(2)}, u32[]{:S(2)}) collective-permute-start(f32[768,768]{1,0:T(8,128)S(1)} %get-tuple-element.139), channel_id=1, source_target_pairs={{0,1},{1,0},{2,3},{3,2},{4,5},{5,4},{6,7},{7,6},{8,9},{9,8},{10,11... | collective-permute-start | bytes 7077896 | tf_op jit(solution)/shard_map/ppermute | solution.py:100
  523.8 77.8 %collective-permute-start.67 = (f32[1,184,96]{2,1,0:T(8,128)S(1)}, f32[1,184,96]{2,1,0:T(8,128)S(1)}, u32[]{:S(2)}, u32[]{:S(2)}) collective-permute-start(f32[1,184,96]{2,1,0:T(8,128)S(1)} %slice.399), channel_id=1, source_target_pairs={{0,1},{1,0},{2,3},{3,2},{4,5},{5,4},{6,7},{7,6},{8,9},{9,8},{10,11... | collective-permute-start | bytes 211976 | tf_op jit(solution)/shard_map/ppermute | solution.py:100
  525.9 103.4 %collective-permute-start.79 = (f32[96,384]{1,0:T(8,128)}, f32[96,384]{1,0:T(8,128)}, u32[]{:S(2)}, u32[]{:S(2)}) collective-permute-start(f32[96,384]{1,0:T(8,128)} %get-tuple-element.131), channel_id=1, source_target_pairs={{0,16},{8,24},{16,0},{24,8},{1,17},{9,25},{17,1},{25,9},{2,18},{10... | collective-permute-start | bytes 442376 | tf_op jit(solution)/shard_map/ppermute | solution.py:100
  550.9 82.9 %collective-permute-start.62 = (f32[384,768]{1,0:T(8,128)}, f32[384,768]{1,0:T(8,128)}, u32[]{:S(2)}, u32[]{:S(2)}) collective-permute-start(f32[384,768]{1,0:T(8,128)} %get-tuple-element.143), channel_id=1, source_target_pairs={{0,16},{8,24},{16,0},{24,8},{1,17},{9,25},{17,1},{25,9},{2,18},{10... | collective-permute-start | bytes 3538952 | tf_op jit(solution)/shard_map/ppermute | solution.py:100
  554.1 81.2 %collective-permute-start.47 = (f32[384,768]{1,0:T(8,128)}, f32[384,768]{1,0:T(8,128)}, u32[]{:S(2)}, u32[]{:S(2)}) collective-permute-start(f32[384,768]{1,0:T(8,128)} %get-tuple-element.149), channel_id=1, source_target_pairs={{0,1},{1,0},{2,3},{3,2},{4,5},{5,4},{6,7},{7,6},{8,9},{9,8},{10,11... | collective-permute-start | bytes 3538952 | tf_op jit(solution)/shard_map/ppermute | solution.py:100
  640.3 48.3 %collective-permute-start.53 = (f32[192,768]{1,0:T(8,128)S(1)}, f32[192,768]{1,0:T(8,128)S(1)}, u32[]{:S(2)}, u32[]{:S(2)}) collective-permute-start(f32[192,768]{1,0:T(8,128)S(1)} %get-tuple-element.155), channel_id=1, source_target_pairs={{0,2},{1,3},{2,0},{3,1},{4,6},{5,7},{6,4},{7,5},{8,10},{9,11},{10,... | collective-permute-start | bytes 1769480 | tf_op jit(solution)/shard_map/ppermute | solution.py:100
  (106 other events, 2141.9 us)

commit v2 on v1

--- a/solution.py
+++ b/solution.py
@@ -23,6 +23,7 @@
 clip_scale = 1.25
 
 VMEM_LIMIT = 60 * 1024 * 1024
+SMALL = pl.CostEstimate(flops=0, bytes_accessed=1024, transcendentals=0)
 BF16 = jnp.bfloat16
 F32 = jnp.float32
 
@@ -111,46 +112,62 @@
     return stages[:place] + [("rep", 2)] + stages[place:]
 
 
-def gather_unit(mine, kind):
-    arrays, labels = [mine], [[(0, 0)]]
-    stages = stage_order(kind)
-    for number, (axis, bit) in enumerate(stages):
-        got = [swap(a, (axis, bit)) for a in arrays]
-        moved = [
-            [(u ^ bit, e) if axis == "rep" else (u, e ^ bit) for u, e in block] for block in labels
-        ]
-        if number < len(stages) - 1:
-            arrays = [jnp.concatenate([arrays[0], got[0]], axis=0)]
-            labels = [labels[0] + moved[0]]
-        else:
-            arrays, labels = arrays + got, labels + moved
-    got = [swap(a, ("rep", 1)) for a in arrays]
-    moved = [[(u ^ 1, e) for u, e in block] for block in labels]
-    return arrays + got, labels + moved
+def tie(*values):
+    return lax.optimization_barrier(values)
 
 
 class Group:
-    def __init__(self, mine, kind, wide, where):
-        self.arrays, self.labels = gather_unit(mine, kind)
-        self.wide = wide
+    def __init__(self, mine, kind, wide, where, before=None):
+        self.wide, self.where = wide, where
         self.rows, self.width = mine.shape
         count = lax.axis_size("fsdp")
         depth = self.rows * count
         self.shape = (depth, 4 * self.width) if wide else (4, depth, self.width)
-        self.blocks = sum(len(block) for block in self.labels)
+        self.blocks = 4 * count
+        if before is not None:
+            mine, before.arrays[0] = tie(mine, before.arrays[0])
+        self.arrays, self.labels = [mine], [[(0, 0)]]
+        self.stages = stage_order(kind)
+        self.step()
+
+    def step(self):
+        axis, bit = self.stages.pop(0)
+        got = swap(self.arrays[0], (axis, bit))
+        moved = [
+            (u ^ bit, e) if axis == "rep" else (u, e ^ bit) for u, e in self.labels[0]
+        ]
+        if self.stages:
+            self.arrays = [jnp.concatenate([self.arrays[0], got], axis=0)]
+            self.labels = [self.labels[0] + moved]
+        else:
+            self.arrays, self.labels = self.arrays + [got], self.labels + [moved]
+
+    def fabric(self):
+        while self.stages:
+            self.step()
+        return self
+
+    def finish(self):
+        self.arrays = self.arrays + [swap(a, ("rep", 1)) for a in self.arrays]
+        self.labels = self.labels + [[(u ^ 1, e) for u, e in block] for block in self.labels]
         if self.rows % 16:
+            count = lax.axis_size("fsdp")
             flat = jnp.concatenate(self.arrays, axis=0).reshape(-1, self.rows, self.width)
             order = [label for block in self.labels for label in block]
             place = {label: number for number, label in enumerate(order)}
             table = jnp.array(
                 [[place[(u, e)] for e in range(count)] for u in range(4)], jnp.int32
             )
-            units = jnp.arange(4, dtype=jnp.int32)[:, None] ^ where[0]
-            owners = jnp.arange(count, dtype=jnp.int32)[None] ^ where[1]
-            whole = flat[table[units, owners]].reshape(4, depth, self.width)
-            if wide:
-                whole = whole.transpose(1, 0, 2).reshape(depth, 4 * self.width)
-            self.arrays, self.labels, self.blocks = [whole], None, 1
+            units = jnp.arange(4, dtype=jnp.int32)[:, None] ^ self.where[0]
+            owners = jnp.arange(count, dtype=jnp.int32)[None] ^ self.where[1]
+            whole = flat[table[units, owners]].reshape(4, -1, self.width)
+            self.whole(whole)
+        return self
+
+    def whole(self, units):
+        if self.wide:
+            units = units.transpose(1, 0, 2).reshape(self.shape)
+        self.arrays, self.labels, self.blocks = [units], None, 1
 
     def copies(self, where_ref, arrays, out, sems):
         if self.labels is None:
@@ -171,6 +188,36 @@
         return copies
 
 
+class Gathered(Group):
+    def __init__(self, gathered, number, groups, wide, where):
+        count = lax.axis_size("fsdp")
+        self.wide, self.where = wide, where
+        self.rows, self.width = gathered.shape[0] // (4 * count * groups), gathered.shape[1]
+        depth = self.rows * count
+        self.shape = (depth, 4 * self.width) if wide else (4, depth, self.width)
+        self.arrays, self.labels, self.blocks = [gathered], (), 4 * count
+        self.number, self.groups = number, groups
+        if self.rows % 16:
+            blocks = gathered.reshape(count, 4, groups, self.rows, self.width)[:, :, number]
+            self.whole(blocks.transpose(1, 0, 2, 3).reshape(4, depth, self.width))
+
+    def copies(self, where_ref, arrays, out, sems):
+        if self.labels is None:
+            return [pltpu.make_async_copy(arrays[0], out, sems.at[0])]
+        copies = []
+        for place in range(self.blocks):
+            owner, unit = place // 4, place % 4
+            rows = slice(owner * self.rows, (owner + 1) * self.rows)
+            if self.wide:
+                target = out.at[rows, unit * self.width : (unit + 1) * self.width]
+            else:
+                target = out.at[unit, rows, :]
+            first = (place * self.groups + self.number) * self.rows
+            source = arrays[0].at[first : first + self.rows, :]
+            copies.append(pltpu.make_async_copy(source, target, sems.at[place]))
+        return copies
+
+
 class Loading:
     def __init__(self, copies, ref):
         self.pending, self.ref = copies, ref
@@ -184,7 +231,7 @@
         return self.ref
 
 
-def call(body, name, where, groups, ins, outs, scratch=(), flops=0):
+def call(body, name, where, groups, ins, outs, scratch=()):
     sizes = [len(group.arrays) for group in groups]
 
     def kernel(where_ref, *refs):
@@ -209,30 +256,28 @@
         + [pltpu.SemaphoreType.DMA((group.blocks,)) for group in groups]
         + list(scratch),
         compiler_params=pltpu.CompilerParams(vmem_limit_bytes=VMEM_LIMIT),
-        cost_estimate=pl.CostEstimate(flops=flops, bytes_accessed=1 << 20, transcendentals=0),
+        cost_estimate=SMALL,
         name=name,
     )(where, *[array for group in groups for array in group.arrays], *ins)
 
 
-def vector_kernel(where_ref, pieces_ref, out_ref):
+def vector_kernel(pieces_ref, out_ref):
     count, width = pieces_ref.shape[0], pieces_ref.shape[3]
     for k in range(count):
-        out_ref[:, :, k * width : (k + 1) * width] = pieces_ref[jnp.bitwise_xor(where_ref[1], k)]
-
-
-def gather_vectors(mine, where):
-    pieces = mine[None]
-    for bit in reversed(fsdp_bits()):
-        pieces = jnp.concatenate([pieces, swap(pieces, ("fsdp", bit))], axis=0)
+        out_ref[:, :, k * width : (k + 1) * width] = pieces_ref[k]
+
+
+def gather_vectors(mine):
+    pieces = lax.all_gather(mine, "fsdp", axis=0)
     count, two, rows, width = pieces.shape
     return pl.pallas_call(
         vector_kernel,
         out_shape=jax.ShapeDtypeStruct((two, rows, count * width), mine.dtype),
-        in_specs=[smem_spec(), vmem_spec()],
+        in_specs=[vmem_spec()],
         out_specs=vmem_spec(),
         compiler_params=pltpu.CompilerParams(vmem_limit_bytes=VMEM_LIMIT),
         name="gather_vectors",
-    )(where, pieces)
+    )(pieces)
 
 
 def reduce_order(kind):
@@ -273,28 +318,68 @@
     depth = pairs[0][0].shape[1]
     rows = depth // lax.axis_size("fsdp")
     shape = jax.ShapeDtypeStruct((2 * depth, width), F32)
-    flops = sum(2 * left.shape[0] * depth * width * len(units) for (left, _), units in zip(pairs, unit_of))
+    return Summing(
+        *pl.pallas_call(
+            functools.partial(grad_kernel, unit_of, reduce_order(kind), rows, width),
+            out_shape=(shape, shape),
+            in_specs=[smem_spec()] + [vmem_spec()] * (2 * len(pairs)),
+            out_specs=(vmem_spec(), vmem_spec()),
+            compiler_params=pltpu.CompilerParams(vmem_limit_bytes=VMEM_LIMIT),
+            cost_estimate=SMALL,
+            name="unit_grads",
+        )(where, *[left for left, _ in pairs], *[right for _, right in pairs]),
+        kind,
+    )
+
+
+class Summing:
+    def __init__(self, keep, send, kind):
+        self.parts, self.stages = (keep, send), [("rep", 1)] + reduce_order(kind)
+
+    def step(self):
+        keep, send = self.parts
+        got = swap(send, self.stages.pop(0))
+        if self.stages:
+            half = keep.shape[0] // 2
+            self.parts = keep[:half] + got[:half], keep[half:] + got[half:]
+        else:
+            self.parts = (keep + got,)
+
+    def finish(self):
+        while self.stages:
+            self.step()
+        return self.parts[0]
+
+
+def tie_sums(values, *sums):
+    tied = tie(*values, *[part for one in sums for part in one.parts])
+    values, parts = tied[: len(values)], list(tied[len(values) :])
+    for one in sums:
+        one.parts = tuple(parts.pop(0) for _ in one.parts)
+    return values
+
+
+def owner_kernel(count, width, left_ref, right_ref, out_ref):
+    rows = left_ref.shape[1] // count
+    left = left_ref[...]
+    for unit in range(4):
+        product = matmul_tn(left, right_ref[:, unit * width : (unit + 1) * width])
+        for owner in range(count):
+            place = (owner * 4 + unit) * rows
+            out_ref[place : place + rows, :] = product[owner * rows : (owner + 1) * rows, :]
+
+
+def owner_grads(left, right):
+    depth, width = left.shape[1], right.shape[1] // 4
     return pl.pallas_call(
-        functools.partial(grad_kernel, unit_of, reduce_order(kind), rows, width),
-        out_shape=(shape, shape),
-        in_specs=[smem_spec()] + [vmem_spec()] * (2 * len(pairs)),
-        out_specs=(vmem_spec(), vmem_spec()),
+        functools.partial(owner_kernel, lax.axis_size("fsdp"), width),
+        out_shape=jax.ShapeDtypeStruct((4 * depth, width), F32),
+        in_specs=[vmem_spec()] * 2,
+        out_specs=vmem_spec(),
         compiler_params=pltpu.CompilerParams(vmem_limit_bytes=VMEM_LIMIT),
-        cost_estimate=pl.CostEstimate(
-            flops=flops, bytes_accessed=16 * depth * width, transcendentals=0
-        ),
-        name="unit_grads",
-    )(where, *[left for left, _ in pairs], *[right for _, right in pairs])
-
-
-def reduce_units(keep, send, kind):
-    got = swap(send, ("rep", 1))
-    for stage in reduce_order(kind):
-        half = keep.shape[0] // 2
-        send = keep[half:] + got[half:]
-        keep = keep[:half] + got[:half]
-        got = swap(send, stage)
-    return keep + got
+        cost_estimate=SMALL,
+        name="owner_grads",
+    )(left, right)
 
 
 def share_units(own):
@@ -344,11 +429,7 @@
         in_specs=[block] * 3,
         out_specs=(block, small),
         compiler_params=pltpu.CompilerParams(vmem_limit_bytes=VMEM_LIMIT),
-        cost_estimate=pl.CostEstimate(
-            flops=4 * row_count * rows * model_width,
-            bytes_accessed=8 * row_count * model_width,
-            transcendentals=2 * row_count * rows * HEADS,
-        ),
+        cost_estimate=SMALL,
         name="attention",
     )(query, key_rows, value_rows)
 
@@ -397,11 +478,7 @@
         in_specs=[block] * 4 + [small],
         out_specs=(block,) * 3,
         compiler_params=pltpu.CompilerParams(vmem_limit_bytes=VMEM_LIMIT),
-        cost_estimate=pl.CostEstimate(
-            flops=10 * row_count * rows * model_width,
-            bytes_accessed=14 * row_count * model_width,
-            transcendentals=row_count * rows * HEADS,
-        ),
+        cost_estimate=SMALL,
         name="attention_back",
     )(query, key_rows, value_rows, grad, logsum)
 
@@ -717,20 +794,27 @@
         width = array.shape[3] // 4
         return to_low(lax.dynamic_slice_in_dim(array[0, number], rep * width, width, axis=1))
 
-    vector_old_new = gather_vectors(jnp.stack([vector_weights, vector_teacher]), where)
+    vector_old_new = gather_vectors(jnp.stack([vector_weights, vector_teacher]))
     vector_all, vector_old = vector_old_new[0], vector_old_new[1]
-    entry_t = Group(pick(square_teacher, rep), 0, False, where)
-    entry_s = Group(pick(square_weights, rep), 1, False, where)
+    both_s = lax.all_gather(
+        jnp.concatenate([columns_of(feed_weights, 0), columns_of(feed_weights, 1)]),
+        ("fsdp", "rep"),
+        axis=0,
+        tiled=True,
+    )
+    up_s = Gathered(both_s, 0, 2, True, where)
+    down_s = Gathered(both_s, 1, 2, True, where)
     others = jnp.where(
         rep == 0, to_low(square_teacher[4]), pick(square_weights, jnp.clip(rep + 3, 4, 5))
     )
-    outer = Group(others, 0, False, where)
-    up_t = Group(columns_of(feed_teacher, 0), 1, True, where)
-    down_t = Group(columns_of(feed_teacher, 1), 0, True, where)
-    up_s = Group(columns_of(feed_weights, 0), 1, True, where)
-    down_s = Group(columns_of(feed_weights, 1), 0, True, where)
+    entry_t = Group(pick(square_teacher, rep), 0, False, where)
+    entry_s = Group(pick(square_weights, rep), 1, False, where, entry_t)
+    outer = Group(others, 0, False, where, entry_s)
+    up_t = Group(columns_of(feed_teacher, 0), 1, True, where, outer)
+    down_t = Group(columns_of(feed_teacher, 1), 0, True, where, up_t)
+    for group in (entry_t, entry_s, outer, up_t, down_t):
+        group.fabric()
     base = 2 + seq_len
-    wide, square = 2 * row_count * model_width * hidden_units, 2 * row_count * model_width**2
 
     def positions(vector):
         return jnp.pad(vector[2 : 2 + seq_len], ((0, pad_len - seq_len), (0, 0)))
@@ -747,23 +831,29 @@
             [group],
             [patch_rows, vector, positions(vector)] + ([mask_rows] if masked else []),
             [full] + [low_full] * 4,
-            flops=4 * square,
         )
 
-    hidden_t, _, query, key_rows, value_rows = entry(entry_t, vector_old, False, "embed_t")
-    attended, _ = attention_forward(query, key_rows, value_rows, samples, seq_len)
+    hidden_t, _, query, key_rows, value_rows = entry(
+        entry_t.finish(), vector_old, False, "embed_t"
+    )
+    attended_t, _ = attention_forward(query, key_rows, value_rows, samples, seq_len)
+    entry_s.arrays[0], attended_t = tie(entry_s.arrays[0], attended_t)
+    hidden, hidden_low, query, key_rows, value_rows = entry(
+        entry_s.finish(), vector_all, True, "embed_s"
+    )
+    attended, logsum = attention_forward(query, key_rows, value_rows, samples, seq_len)
+    outer.finish(), up_t.finish()
+    down_t.arrays[0], attended = tie(down_t.arrays[0], attended)
+    down_t.finish()
     (target,) = call(
         functools.partial(teacher_body, samples, seq_len, base),
         "layer_t",
         where,
         [outer, up_t, down_t],
-        [attended, hidden_t, vector_old],
+        [attended_t, hidden_t, vector_old],
         [full],
         [pltpu.VMEM(*full), pltpu.VMEM(*low_full), pltpu.VMEM(*low_wide)],
-        flops=square + 2 * wide,
-    )
-    hidden, hidden_low, query, key_rows, value_rows = entry(entry_s, vector_all, True, "embed_s")
-    attended, logsum = attention_forward(query, key_rows, value_rows, samples, seq_len)
+    )
     loss_scale = 1.0 / (total_masked * model_width)
     (
         final_low,
@@ -786,14 +876,13 @@
         [low_full] * 3
         + [full, low_wide, full_wide, low_full, full, column, ((8, model_width), F32), ((1, 1), F32)],
         [pltpu.VMEM(*full)] * 4 + [pltpu.VMEM(*column)] * 2,
-        flops=3 * square + 2 * wide,
     )
     loss_local = loss_sum[0, 0] * loss_scale
 
     unit = model_width
-    quarters = [[(k * unit, k) for k in range(4)]]
-    down_g = unit_grads([(grad_branch_two, activation)], quarters, 0, unit, where)
-    grad_branch_two, *down_g = lax.optimization_barrier((grad_branch_two, *down_g))
+    down_g = owner_grads(grad_branch_two, activation)
+    grad_branch_two, down_g = tie(grad_branch_two, down_g)
+    down_own = lax.psum_scatter(down_g, ("fsdp", "rep"), scatter_dimension=0, tiled=True)
     grad_pre, grad_first, grad_branch, grad_attended, rows_inner, rows_up = call(
         functools.partial(feed_back_body, samples, base),
         "feed_back",
@@ -802,18 +891,29 @@
         [grad_branch_two, grad_second, slope, hat_first, inverse_first, vector_all],
         [low_wide, full, low_full, low_full, ((8, model_width), F32), ((1, hidden_units), F32)],
         [pltpu.VMEM(*full)],
-        flops=square + 2 * wide,
-    )
-    up_g = unit_grads([(normed_low, grad_pre)], quarters, 1, unit, where)
-    halves = [[(0, 0), (unit // 2, 1)], [(0, 2), (unit // 2, 3)]]
+    )
+    half = unit // 2
+
+    def up_half(grad, number):
+        places = [[(k * unit + number * half, k) for k in range(4)]]
+        return unit_grads([(normed_low, grad)], places, number, half, where)
+
+    up_a = up_half(grad_pre, 0)
+    (grad_pre,) = tie_sums([grad_pre], up_a)
+    up_b = up_half(grad_pre, 1)
+    up_a.step()
+    (grad_branch,) = tie_sums([grad_branch], up_a, up_b)
+    halves = [[(0, 0), (half, 1)], [(0, 2), (half, 3)]]
     edge_g = unit_grads(
-        [(final_low, grad_output), (attended, grad_branch)], halves, 0, unit // 2, where
-    )
-    grad_attended, *both = lax.optimization_barrier((grad_attended, *up_g, *edge_g))
-    up_g, edge_g = both[:2], both[2:]
+        [(final_low, grad_output), (attended, grad_branch)], halves, 0, half, where
+    )
+    up_b.step()
+    (grad_attended,) = tie_sums([grad_attended], up_b, edge_g)
     grad_query, grad_key, grad_value = attention_backward(
         query, key_rows, value_rows, logsum, grad_attended, samples, seq_len
     )
+    edge_g.step()
+    grad_query, grad_key, grad_value = tie_sums([grad_query, grad_key, grad_value], edge_g)
     vector_count = vector_all.shape[0]
     count = lax.axis_size("fsdp")
     grad_embed, pieces = call(
@@ -824,24 +924,28 @@
         [grad_query, grad_key, grad_value, grad_first, mask_rows, rows_after, rows_inner, rows_up],
         [low_full, ((count, vector_count, model_width // count), F32)],
         [pltpu.VMEM((vector_count, model_width), F32), pltpu.VMEM((pad_len, model_width), F32)],
-        flops=3 * square,
-    )
-    singles = [[(0, k)] for k in range(4)]
-    qkv_g = unit_grads(
-        [(hidden_low, grad_query), (hidden_low, grad_key), (hidden_low, grad_value), (patch_rows, grad_embed)],
-        singles,
-        1,
-        unit,
-        where,
-    )
-
-    down_own = reduce_units(*down_g, 0)
-    up_own = reduce_units(*up_g, 1)
-    edge_own = reduce_units(*edge_g, 0)
-    qkv_own = reduce_units(*qkv_g, 1)
+    )
+
+    def entry_half(grad, number):
+        pairs = [(hidden_low, grad_query), (hidden_low, grad_key), (hidden_low, grad_value), (patch_rows, grad)]
+        return unit_grads(pairs, [[(number * half, k)] for k in range(4)], number, half, where)
+
+    up_a.step()
+    (grad_embed,) = tie_sums([grad_embed], up_a)
+    qkv_a = entry_half(grad_embed, 0)
+    edge_g.step()
+    (grad_embed,) = tie_sums([grad_embed], edge_g, qkv_a)
+    qkv_b = entry_half(grad_embed, 1)
+    qkv_a.step()
+    up_b.step()
+    tie_sums([], up_b, qkv_a)
+
+    up_own = jnp.concatenate([up_a.finish(), up_b.finish()], axis=1)
+    edge_own = edge_g.finish()
+    qkv_own = jnp.concatenate([qkv_a.finish(), qkv_b.finish()], axis=1)
     for bit in fsdp_bits():
-        half = pieces.shape[0] // 2
-        pieces = pieces[:half] + swap(pieces[half:], ("fsdp", bit))
+        count = pieces.shape[0] // 2
+        pieces = pieces[:count] + swap(pieces[count:], ("fsdp", bit))
     vector_share = pieces[0]
     for bit in (2, 1):
         vector_share = vector_share + swap(vector_share, ("rep", bit))
@@ -863,7 +967,10 @@
         shared = share_units(own_units)
         return [lax.dynamic_index_in_dim(shared, rep ^ k, keepdims=False) for k in range(4)]
 
-    down_u, up_u, edge_u, qkv_u = ordered(down_own), ordered(up_own), ordered(edge_own), ordered(qkv_own)
+    early_u, qkv_u = ordered(jnp.concatenate([down_own, up_own, edge_own], axis=1)), ordered(qkv_own)
+    down_u = [own[:, :unit] for own in early_u]
+    up_u = [own[:, unit : 2 * unit] for own in early_u]
+    edge_u = [own[:, 2 * unit :] for own in early_u]
     feed_grad = jnp.stack([jnp.concatenate(up_u, axis=1), jnp.concatenate(down_u, axis=1)])[None]
     square_grad = jnp.stack(
         [

time: 760 us -> 635 us (0.84)
  waiting for transfers between devices: 399 us -> 250 us
  between operations: 7.83 us -> 20.5 us
  starting transfers between devices: 97.4 us -> 87.6 us
  other arithmetic: 51 us -> 60.4 us
    ppermute x87 -> x71, waiting for transfers between devices: 399 us -> 250 us  [swap(): lax.ppermute(values, axis, [(i, i ^ bit) for i in range(lax.axis_size(axi...]
    add x18 -> x26, other arithmetic: 22.7 us -> 32.7 us  [the longest x20 28.8 us: step(): self.parts = (keep[:half] + got[:half], keep[half:] + got[half:])]
    ppermute x87 -> x71, starting transfers between devices: 97.4 us -> 87.5 us  [swap(): lax.ppermute(values, axis, [(i, i ^ bit) for i in range(lax.axis_size(axi...]
    pallas_call x0 -> x1, Pallas kernels: none -> 8.46 us  [owner_grads(): pl.pallas_call(functools.partial(owner_kernel, lax.axis_size('fsdp'), wid...]
    pallas_call x4 -> x5, Pallas kernels: 39.1 us -> 37.4 us  [unit_grads(): pl.pallas_call(functools.partial(grad_kernel, unit_of, reduce_order(kind)...]
  transfers between devices with their start and end apart: 87 -> 74, of which waited for: 37 -> 35; matrix products, arithmetic and copies ran while one was open for 7% -> 10% of each run, Pallas kernels for 8% -> 18%
where the time goes in v2:
time: 635 us; the launch traced here: 631 us
  waiting for transfers between devices  250 us (39%)
  Pallas kernels  186 us (29%)
  starting transfers between devices  87.6 us (14%)
  other arithmetic  60.4 us (10%)
  local copies, waits for them, and re-layouts  26 us (4%)
  between operations  20.5 us (3%)
    ppermute x71, waiting for transfers between devices, swap(): lax.ppermute(values, axis, [(i, i ^ bit) for i in range(lax.axis_size(axi...  250 us
    pallas_call x6, Pallas kernels, call(): pl.pallas_call(kernel, out_shape=tuple((jax.ShapeDtypeStruct(*out) for ou...  106 us
    ppermute x71, starting transfers between devices, swap(): lax.ppermute(values, axis, [(i, i ^ bit) for i in range(lax.axis_size(axi...  87.5 us
    pallas_call x5, Pallas kernels, unit_grads(): pl.pallas_call(functools.partial(grad_kernel, unit_of, reduce_order(kind)...  37.4 us
    add x20, other arithmetic, step(): self.parts = (keep[:half] + got[:half], keep[half:] + got[half:])  28.8 us
    pallas_call x1, Pallas kernels, attention_backward(): pl.pallas_call(functools.partial(attention_back_kernel, seq_len, head_dim...  16.4 us
    pallas_call x2, Pallas kernels, attention_forward(): pl.pallas_call(functools.partial(attention_kernel, seq_len, head_dim), gr...  14.7 us
  transfers between devices with their start and end apart: 74, of which 35 were waited for; matrix products, arithmetic and copies ran while one was open for 10% of the time, Pallas kernels for 18%

profile of v2, /device:TPU:0, one launch (start us, length us, event | category | flops | bytes accessed | tf_op | source)
XLA Modules:
  0.0 630.8 jit_solution(13453430049429655035)
XLA Ops:
  24.8 11.6 %collective-permute-start.14 = (bf16[192,768]{1,0:T(8,128)(2,1)S(1)}, bf16[192,768]{1,0:T(8,128)(2,1)S(1)}, u32[]{:S(2)}, u32[]{:S(2)}) collective-permute-start(bf16[192,768]{1,0:T(8,128)(2,1)S(1)} %pad_maximum_fusion.8), channel_id=1, source_target_pairs={{0,2},{1,3},{2,0},{3,1},{4,6},{5,7},{6,4},{7,5},{8,10},{9,11},{10,... | collective-permute-start | bytes 884744 | tf_op jit(solution)/shard_map/ppermute | solution.py:101
  58.1 10.5 %collective-permute-done.8 = bf16[96,768]{1,0:T(8,128)(2,1)S(1)} collective-permute-done((bf16[96,768]{1,0:T(8,128)(2,1)}, bf16[96,768]{1,0:T(8,128)(2,1)S(1)}, u32[]{:S(2)}, u32[]{:S(2)}) %collective-permute-start.8) | collective-permute-done | bytes 147488 | tf_op jit(solution)/shard_map/ppermute | solution.py:101
  86.9 8.4 %collective-permute-done.10 = bf16[192,768]{1,0:T(8,128)(2,1)S(1)} collective-permute-done((bf16[192,768]{1,0:T(8,128)(2,1)S(1)}, bf16[192,768]{1,0:T(8,128)(2,1)S(1)}, u32[]{:S(2)}, u32[]{:S(2)}) %collective-permute-start.10) | collective-permute-done | bytes 294944 | tf_op jit(solution)/shard_map/ppermute | solution.py:101
  95.4 30.5 %collective-permute-done.13 = bf16[384,768]{1,0:T(8,128)(2,1)S(1)} collective-permute-done((bf16[384,768]{1,0:T(8,128)(2,1)S(1)}, bf16[384,768]{1,0:T(8,128)(2,1)S(1)}, u32[]{:S(2)}, u32[]{:S(2)}) %collective-permute-start.13) | collective-permute-done | bytes 589856 | tf_op jit(solution)/shard_map/ppermute | solution.py:101
  128.9 11.8 %collective-permute-done.23 = bf16[384,768]{1,0:T(8,128)(2,1)S(1)} collective-permute-done((bf16[384,768]{1,0:T(8,128)(2,1)S(1)}, bf16[384,768]{1,0:T(8,128)(2,1)S(1)}, u32[]{:S(2)}, u32[]{:S(2)}) %collective-permute-start.23) | collective-permute-done | bytes 589856 | tf_op jit(solution)/shard_map/ppermute | solution.py:101
  160.8 23.6 %collective-permute-done.19.refs_1_ = bf16[768,768]{1,0:T(8,128)(2,1)} collective-permute-done((bf16[768,768]{1,0:T(8,128)(2,1)}, bf16[768,768]{1,0:T(8,128)(2,1)}, u32[]{:S(2)}, u32[]{:S(2)}) %collective-permute-start.19) | collective-permute-done | bytes 1179680 | tf_op jit(solution)/shard_map/ppermute | solution.py:101
  184.4 9.6 %embed_t.1 = (f32[504,768]{1,0:T(8,128)}, bf16[504,768]{1,0:T(8,128)(2,1)}, bf16[504,768]{1,0:T(8,128)(2,1)}, bf16[504,768]{1,0:T(8,128)(2,1)}, bf16[504,768]{1,0:T(8,128)(2,1)}) custom-call(s32[2]{0:T(128)} %pad_add_fusion.where_ref, bf16[768,768]{1,0:T(8,128)(2,1)} %copy-done.16, bf16[768,768]{1,0:T(8,128)(2,1)} %collective-permute-done.16.refs_1_, ...), custom_call_target="tpu_custom_call" | custom-call | bytes 1024 | tf_op jit(solution)/shard_map/embed_t/pallas_call | solution.py:250
  194.0 7.4 %attention.2 = (bf16[504,768]{1,0:T(8,128)(2,1)}, f32[504,128]{1,0:T(8,128)}) custom-call(bf16[504,768]{1,0:T(8,128)(2,1)} %get-tuple-element.109.q_ref, bf16[504,768]{1,0:T(8,128)(2,1)} %get-tuple-element.110.k_ref, bf16[504,768]{1,0:T(8,128)(2,1)} %get-tuple-element.111.v_ref), custom_call_target="tpu_custom_call" | custom-call | bytes 1024 | tf_op jit(solution)/shard_map/attention/pallas_call | solution.py:422
  206.6 9.1 %embed_s.1 = (f32[504,768]{1,0:T(8,128)}, bf16[504,768]{1,0:T(8,128)(2,1)}, bf16[504,768]{1,0:T(8,128)(2,1)}, bf16[504,768]{1,0:T(8,128)(2,1)}, bf16[504,768]{1,0:T(8,128)(2,1)}) custom-call(s32[2]{0:T(128)} %pad_add_fusion.where_ref, bf16[768,768]{1,0:T(8,128)(2,1)} %constant_dynamic-update-slice_fusion.7.refs_0_, ...), custom_call_target="tpu_custom_call" | custom-call | bytes 1024 | tf_op jit(solution)/shard_map/embed_s/pallas_call | solution.py:250
  215.7 7.3 %attention.3 = (bf16[504,768]{1,0:T(8,128)(2,1)}, f32[504,128]{1,0:T(8,128)}) custom-call(bf16[504,768]{1,0:T(8,128)(2,1)} %get-tuple-element.114.q_ref, bf16[504,768]{1,0:T(8,128)(2,1)} %get-tuple-element.115.k_ref, bf16[504,768]{1,0:T(8,128)(2,1)} %get-tuple-element.116.v_ref), custom_call_target="tpu_custom_call" | custom-call | bytes 1024 | tf_op jit(solution)/shard_map/attention/pallas_call | solution.py:422
  227.3 23.5 %layer_t.1.refs_9_ = f32[504,768]{1,0:T(8,128)} custom-call(s32[2]{0:T(128)} %pad_add_fusion.where_ref, bf16[768,768]{1,0:T(8,128)(2,1)} %copy-done, bf16[768,768]{1,0:T(8,128)(2,1)} %copy-done.1, bf16[768,768]{1,0:T(8,128)(2,1)} %copy-done.2, bf16[768,768]{1,0:T(8,128)(2,1)} %collective-permute-done.7.refs_3_, ...), custom_call_target="tpu_custom_call" | custom-call | bytes 1024 | tf_op jit(solution)/shard_map/layer_t/pallas_call | solution.py:250
  250.8 32.7 %layer_s.1 = (bf16[504,768]{1,0:T(8,128)(2,1)}, bf16[504,768]{1,0:T(8,128)(2,1)}, bf16[504,768]{1,0:T(8,128)(2,1)}, f32[504,768]{1,0:T(8,128)}, bf16[504,3072]{1...) custom-call(s32[2]{0:T(128)} %pad_add_fusion.where_ref, ...), custom_call_target="tpu_custom_call" | custom-call | bytes 1024 | tf_op jit(solution)/shard_map/layer_s/pallas_call | solution.py:250
  283.5 8.5 %owner_grads.1 = f32[3072,768]{1,0:T(8,128)} custom-call(bf16[504,768]{1,0:T(8,128)(2,1)} %get-tuple-element.127.left_ref.refs_6_, bf16[504,3072]{1,0:T(8,128)(2,1)} %get-tuple-element.125.right_ref), custom_call_target="tpu_custom_call" | custom-call | bytes 1024 | tf_op jit(solution)/shard_map/owner_grads/pallas_call | solution.py:374
  292.0 22.6 %feed_back.1 = (bf16[504,3072]{1,0:T(8,128)(2,1)}, f32[504,768]{1,0:T(8,128)}, bf16[504,768]{1,0:T(8,128)(2,1)}, bf16[504,768]{1,0:T(8,128)(2,1)}, f32[8,768]{1,0:T(8,128)}, /*index=5*/f32[1,3072]{1,0:T(1,128)}) custom-call(s32[2]{0:T(128)} %pad_add_fusion.where_ref, bf16[768,768]{1,0:T(8,128)(2,1)} %copy-done, bf16[768,768]{1,0:T(8,128)(2,1)} %copy-done.1, ...), custom_call_target="tpu_custom_call" | custom-call | bytes 1024 | tf_op jit(solution)/shard_map/feed_back/pallas_call | solution.py:250
  345.0 16.4 %attention_back.1 = (bf16[504,768]{1,0:T(8,128)(2,1)}, bf16[504,768]{1,0:T(8,128)(2,1)}, bf16[504,768]{1,0:T(8,128)(2,1)}) custom-call(bf16[504,768]{1,0:T(8,128)(2,1)} %get-tuple-element.114.q_ref, bf16[504,768]{1,0:T(8,128)(2,1)} %get-tuple-element.115.k_ref, bf16[504,768]{1,0:T(8,128)(2,1)} %get-tuple-element.116.v_ref, ...), custom_call_target="tpu_custom_call" | custom-call | bytes 1024 | tf_op jit(solution)/shard_map/attention_back/pallas_call | solution.py:474
  375.2 9.0 %embed_back.1 = (bf16[504,768]{1,0:T(8,128)(2,1)}, f32[8,184,96]{2,1,0:T(8,128)}) custom-call(s32[2]{0:T(128)} %pad_add_fusion.where_ref, bf16[768,768]{1,0:T(8,128)(2,1)} %constant_dynamic-update-slice_fusion.7.refs_0_, bf16[768,768]{1,0:T(8,128)(2,1)} %collective-permute-done.19.refs_1_, bf16[768,768]{1,0:T(8,128)(2,1)} %collective-permute-done.20.refs_2_, ...), custom_call_target="tpu_custom_call" | custom-call | bytes 1024 | tf_op jit(solution)/shard_map/embed_back/pallas_call | solution.py:250
  384.2 8.6 %unit_grads.8 = (f32[1536,384]{1,0:T(8,128)}, f32[1536,384]{1,0:T(8,128)}) custom-call(s32[2]{0:T(128)} %pad_add_fusion.where_ref, bf16[504,768]{1,0:T(8,128)(2,1)} %get-tuple-element.174.refs_0_.refs_1_.refs_2_, bf16[504,768]{1,0:T(8,128)(2,1)} %get-tuple-element.174.refs_0_.refs_1_.refs_2_, bf16[504,768]{1,0:T(8,128)(2,1)} %get-tuple-element.174.refs_0_.refs_1_.refs_2_, ...), custom_call_target="tpu_custom_call" | custom-call | bytes 1024 | tf_op jit(solution)/shard_map/unit_grads/pallas_call | solution.py:322
  392.7 13.1 %collective-permute-done.38 = f32[768,384]{1,0:T(8,128)} collective-permute-done((f32[768,384]{1,0:T(8,128)}, f32[768,384]{1,0:T(8,128)}, u32[]{:S(2)}, u32[]{:S(2)}) %collective-permute-start.38) | collective-permute-done | bytes 1179680 | tf_op jit(solution)/shard_map/ppermute | solution.py:101
  411.3 8.0 %unit_grads.9 = (f32[1536,384]{1,0:T(8,128)}, f32[1536,384]{1,0:T(8,128)}) custom-call(s32[2]{0:T(128)} %pad_add_fusion.where_ref, bf16[504,768]{1,0:T(8,128)(2,1)} %get-tuple-element.174.refs_0_.refs_1_.refs_2_, bf16[504,768]{1,0:T(8,128)(2,1)} %get-tuple-element.174.refs_0_.refs_1_.refs_2_, bf16[504,768]{1,0:T(8,128)(2,1)} %get-tuple-element.174.refs_0_.refs_1_.refs_2_, ...), custom_call_target="tpu_custom_call" | custom-call | bytes 1024 | tf_op jit(solution)/shard_map/unit_grads/pallas_call | solution.py:322
  421.6 13.5 %collective-permute-done.55 = f32[4,184,96]{2,1,0:T(8,128)S(1)} collective-permute-done((f32[4,184,96]{2,1,0:T(8,128)}, f32[4,184,96]{2,1,0:T(8,128)S(1)}, u32[]{:S(2)}, u32[]{:S(2)}) %collective-permute-start.55) | collective-permute-done | bytes 282656 | tf_op jit(solution)/shard_map/ppermute | solution.py:101
  444.6 31.7 %collective-permute-done.57 = f32[1,184,96]{2,1,0:T(8,128)S(1)} collective-permute-done((f32[1,184,96]{2,1,0:T(8,128)S(1)}, f32[1,184,96]{2,1,0:T(8,128)S(1)}, u32[]{:S(2)}, u32[]{:S(2)}) %collective-permute-start.57) | collective-permute-done | bytes 70688 | tf_op jit(solution)/shard_map/ppermute | solution.py:101
  489.2 9.4 %collective-permute-done.35 = f32[192,384]{1,0:T(8,128)} collective-permute-done((f32[192,384]{1,0:T(8,128)}, f32[192,384]{1,0:T(8,128)}, u32[]{:S(2)}, u32[]{:S(2)}) %collective-permute-start.35) | collective-permute-done | bytes 294944 | tf_op jit(solution)/shard_map/ppermute | solution.py:101
  508.0 8.7 %collective-permute-done.43 = f32[384,384]{1,0:T(8,128)S(1)} collective-permute-done((f32[384,384]{1,0:T(8,128)}, f32[384,384]{1,0:T(8,128)S(1)}, u32[]{:S(2)}, u32[]{:S(2)}) %collective-permute-start.43) | collective-permute-done | bytes 589856 | tf_op jit(solution)/shard_map/ppermute | solution.py:101
  546.8 9.4 %collective-permute-done.52 = f32[384,384]{1,0:T(8,128)S(1)} collective-permute-done((f32[384,384]{1,0:T(8,128)S(1)}, f32[384,384]{1,0:T(8,128)S(1)}, u32[]{:S(2)}, u32[]{:S(2)}) %collective-permute-start.52) | collective-permute-done | bytes 589856 | tf_op jit(solution)/shard_map/ppermute | solution.py:101
  (317 shorter events, 265.5 us)
Async XLA Ops:
  7.2 145.4 %all-gather.6.cloned.1.call-start = ((), (), s32[]{:S(2)}) async-start(), calls=%async_computation.3 | async-start | bytes 1695744 | tf_op jit(solution)/shard_map/all_gather | solution.py:271
  8.9 241.9 %all-gather.4.cloned.1.call-start = ((), (), s32[]{:S(2)}) async-start(), calls=%async_computation.1 | async-start | bytes 9732096 | tf_op jit(solution)/shard_map/all_gather | solution.py:799
  11.5 547.7 %reduce-scatter.2.cloned.1.call-start = ((), (), s32[]{:S(2)}) async-start(), calls=%async_computation.2 | async-start | bytes 9732096 | tf_op jit(solution)/shard_map/reduce_scatter | solution.py:885
  39.0 36.5 %collective-permute-start.12 = (bf16[192,768]{1,0:T(8,128)(2,1)S(1)}, bf16[192,768]{1,0:T(8,128)(2,1)S(1)}, u32[]{:S(2)}, u32[]{:S(2)}) collective-permute-start(bf16[192,768]{1,0:T(8,128)(2,1)S(1)} %pad_maximum_fusion.9), channel_id=1, source_target_pairs={{0,2},{1,3},{2,0},{3,1},{4,6},{5,7},{6,4},{7,5},{8,10},{9,11},{10,... | collective-permute-start | bytes 884744 | tf_op jit(solution)/shard_map/ppermute | solution.py:101
  73.8 69.3 %collective-permute-start.16 = (bf16[768,768]{1,0:T(8,128)(2,1)S(1)}, bf16[768,768]{1,0:T(8,128)(2,1)}, u32[]{:S(2)}, u32[]{:S(2)}) collective-permute-start(bf16[768,768]{1,0:T(8,128)(2,1)S(1)} %constant_dynamic-update-slice_fusion.10.refs_0_), channel_id=1, source_target_pairs={{0,16},{8,24},{16,0},{24,8},{1,17},{9,25},{17,1},{25,9},{2,18},{10... | collective-permute-start | bytes 3538952 | tf_op jit(solution)/shard_map/ppermute | solution.py:101
  76.3 49.6 %collective-permute-start.13 = (bf16[384,768]{1,0:T(8,128)(2,1)S(1)}, bf16[384,768]{1,0:T(8,128)(2,1)S(1)}, u32[]{:S(2)}, u32[]{:S(2)}) collective-permute-start(bf16[384,768]{1,0:T(8,128)(2,1)S(1)} %pad_maximum_fusion.5), channel_id=1, source_target_pairs={{0,16},{8,24},{16,0},{24,8},{1,17},{9,25},{17,1},{25,9},{2,18},{10... | collective-permute-start | bytes 1769480 | tf_op jit(solution)/shard_map/ppermute | solution.py:101
  78.5 50.2 %collective-permute-start.4 = (bf16[384,768]{1,0:T(8,128)(2,1)S(1)}, bf16[384,768]{1,0:T(8,128)(2,1)S(1)}, u32[]{:S(2)}, u32[]{:S(2)}) collective-permute-start(bf16[384,768]{1,0:T(8,128)(2,1)S(1)} %pad_maximum_fusion.3), channel_id=1, source_target_pairs={{0,1},{1,0},{2,3},{3,2},{4,5},{5,4},{6,7},{7,6},{8,9},{9,8},{10,11... | collective-permute-start | bytes 1769480 | tf_op jit(solution)/shard_map/ppermute | solution.py:101
  85.2 55.5 %collective-permute-start.23 = (bf16[384,768]{1,0:T(8,128)(2,1)S(1)}, bf16[384,768]{1,0:T(8,128)(2,1)S(1)}, u32[]{:S(2)}, u32[]{:S(2)}) collective-permute-start(bf16[384,768]{1,0:T(8,128)(2,1)S(1)} %pad_maximum_fusion.7), channel_id=1, source_target_pairs={{0,16},{8,24},{16,0},{24,8},{1,17},{9,25},{17,1},{25,9},{2,18},{10... | collective-permute-start | bytes 1769480 | tf_op jit(solution)/shard_map/ppermute | solution.py:101
  95.4 64.0 %collective-permute-start.17 = (bf16[768,768]{1,0:T(8,128)(2,1)S(1)}, bf16[768,768]{1,0:T(8,128)(2,1)}, u32[]{:S(2)}, u32[]{:S(2)}) collective-permute-start(bf16[768,768]{1,0:T(8,128)(2,1)S(1)} %constant_dynamic-update-slice_fusion.10.refs_0_), channel_id=1, source_target_pairs={{0,8},{8,0},{16,24},{24,16},{1,9},{9,1},{17,25},{25,17},{2,10},{10... | collective-permute-start | bytes 3538952 | tf_op jit(solution)/shard_map/ppermute | solution.py:101
  128.7 55.6 %collective-permute-start.19 = (bf16[768,768]{1,0:T(8,128)(2,1)}, bf16[768,768]{1,0:T(8,128)(2,1)}, u32[]{:S(2)}, u32[]{:S(2)}) collective-permute-start(bf16[768,768]{1,0:T(8,128)(2,1)} %constant_dynamic-update-slice_fusion.7.refs_0_), channel_id=1, source_target_pairs={{0,1},{1,0},{2,3},{3,2},{4,5},{5,4},{6,7},{7,6},{8,9},{9,8},{10,11... | collective-permute-start | bytes 3538952 | tf_op jit(solution)/shard_map/ppermute | solution.py:101
  140.7 61.1 %collective-permute-start.5 = (bf16[768,768]{1,0:T(8,128)(2,1)S(1)}, bf16[768,768]{1,0:T(8,128)(2,1)S(1)}, u32[]{:S(2)}, u32[]{:S(2)}) collective-permute-start(bf16[768,768]{1,0:T(8,128)(2,1)S(1)} %constant_dynamic-update-slice_fusion.refs_0_), channel_id=1, source_target_pairs={{0,16},{8,24},{16,0},{24,8},{1,17},{9,25},{17,1},{25,9},{2,18},{10... | collective-permute-start | bytes 3538952 | tf_op jit(solution)/shard_map/ppermute | solution.py:101
  143.2 41.2 %collective-permute-start.18 = (bf16[768,768]{1,0:T(8,128)(2,1)}, bf16[768,768]{1,0:T(8,128)(2,1)}, u32[]{:S(2)}, u32[]{:S(2)}) collective-permute-start(bf16[768,768]{1,0:T(8,128)(2,1)} %collective-permute-done.16.refs_1_), channel_id=1, source_target_pairs={{0,8},{8,0},{16,24},{24,16},{1,9},{9,1},{17,25},{25,17},{2,10},{10... | collective-permute-start | bytes 3538952 | tf_op jit(solution)/shard_map/ppermute | solution.py:101
  149.3 56.2 %collective-permute-start.24 = (bf16[768,768]{1,0:T(8,128)(2,1)}, bf16[768,768]{1,0:T(8,128)(2,1)}, u32[]{:S(2)}, u32[]{:S(2)}) collective-permute-start(bf16[768,768]{1,0:T(8,128)(2,1)} %constant_dynamic-update-slice_fusion.13.refs_4_), channel_id=1, source_target_pairs={{0,1},{1,0},{2,3},{3,2},{4,5},{5,4},{6,7},{7,6},{8,9},{9,8},{10,11... | collective-permute-start | bytes 3538952 | tf_op jit(solution)/shard_map/ppermute | solution.py:101
  159.4 46.1 %collective-permute-start.27 = (bf16[768,768]{1,0:T(8,128)(2,1)}, bf16[768,768]{1,0:T(8,128)(2,1)}, u32[]{:S(2)}, u32[]{:S(2)}) collective-permute-start(bf16[768,768]{1,0:T(8,128)(2,1)} %constant_dynamic-update-slice_fusion.3.refs_8_), channel_id=1, source_target_pairs={{0,16},{8,24},{16,0},{24,8},{1,17},{9,25},{17,1},{25,9},{2,18},{10... | collective-permute-start | bytes 3538952 | tf_op jit(solution)/shard_map/ppermute | solution.py:101
  343.6 29.2 %collective-permute-start.33 = (f32[768,384]{1,0:T(8,128)}, f32[768,384]{1,0:T(8,128)}, u32[]{:S(2)}, u32[]{:S(2)}) collective-permute-start(f32[768,384]{1,0:T(8,128)} %get-tuple-element.166), channel_id=1, source_target_pairs={{0,16},{8,24},{16,0},{24,8},{1,17},{9,25},{17,1},{25,9},{2,18},{10... | collective-permute-start | bytes 3538952 | tf_op jit(solution)/shard_map/ppermute | solution.py:101
  365.2 40.6 %collective-permute-start.38 = (f32[768,384]{1,0:T(8,128)}, f32[768,384]{1,0:T(8,128)}, u32[]{:S(2)}, u32[]{:S(2)}) collective-permute-start(f32[768,384]{1,0:T(8,128)} %get-tuple-element.173), channel_id=1, source_target_pairs={{0,16},{8,24},{16,0},{24,8},{1,17},{9,25},{17,1},{25,9},{2,18},{10... | collective-permute-start | bytes 3538952 | tf_op jit(solution)/shard_map/ppermute | solution.py:101
  408.3 93.5 %collective-permute-start.39 = (f32[1536,384]{1,0:T(8,128)}, f32[1536,384]{1,0:T(8,128)}, u32[]{:S(2)}, u32[]{:S(2)}) collective-permute-start(f32[1536,384]{1,0:T(8,128)} %get-tuple-element.178), channel_id=1, source_target_pairs={{0,8},{8,0},{16,24},{24,16},{1,9},{9,1},{17,25},{25,17},{2,10},{10... | collective-permute-start | bytes 7077896 | tf_op jit(solution)/shard_map/ppermute | solution.py:101
  419.3 86.1 %collective-permute-start.50 = (f32[1536,384]{1,0:T(8,128)}, f32[1536,384]{1,0:T(8,128)}, u32[]{:S(2)}, u32[]{:S(2)}) collective-permute-start(f32[1536,384]{1,0:T(8,128)} %get-tuple-element.187), channel_id=1, source_target_pairs={{0,8},{8,0},{16,24},{24,16},{1,9},{9,1},{17,25},{25,17},{2,10},{10... | collective-permute-start | bytes 7077896 | tf_op jit(solution)/shard_map/ppermute | solution.py:101
  419.7 65.1 %collective-permute-start.37 = (f32[768,384]{1,0:T(8,128)S(1)}, f32[768,384]{1,0:T(8,128)}, u32[]{:S(2)}, u32[]{:S(2)}) collective-permute-start(f32[768,384]{1,0:T(8,128)S(1)} %copy-done.21), channel_id=1, source_target_pairs={{0,1},{1,0},{2,3},{3,2},{4,5},{5,4},{6,7},{7,6},{8,9},{9,8},{10,11... | collective-permute-start | bytes 3538952 | tf_op jit(solution)/shard_map/ppermute | solution.py:101
  436.3 46.6 %collective-permute-start.34 = (f32[384,384]{1,0:T(8,128)S(1)}, f32[384,384]{1,0:T(8,128)}, u32[]{:S(2)}, u32[]{:S(2)}) collective-permute-start(f32[384,384]{1,0:T(8,128)S(1)} %copy-done.25), channel_id=1, source_target_pairs={{0,1},{1,0},{2,3},{3,2},{4,5},{5,4},{6,7},{7,6},{8,9},{9,8},{10,11... | collective-permute-start | bytes 1769480 | tf_op jit(solution)/shard_map/ppermute | solution.py:101
  443.0 33.3 %collective-permute-start.57 = (f32[1,184,96]{2,1,0:T(8,128)S(1)}, f32[1,184,96]{2,1,0:T(8,128)S(1)}, u32[]{:S(2)}, u32[]{:S(2)}) collective-permute-start(f32[1,184,96]{2,1,0:T(8,128)S(1)} %slice.511), channel_id=1, source_target_pairs={{0,1},{1,0},{2,3},{3,2},{4,5},{5,4},{6,7},{7,6},{8,9},{9,8},{10,11... | collective-permute-start | bytes 211976 | tf_op jit(solution)/shard_map/ppermute | solution.py:101
  507.4 32.9 %collective-permute-start.51 = (f32[768,384]{1,0:T(8,128)S(1)}, f32[768,384]{1,0:T(8,128)S(1)}, u32[]{:S(2)}, u32[]{:S(2)}) collective-permute-start(f32[768,384]{1,0:T(8,128)S(1)} %get-tuple-element.207), channel_id=1, source_target_pairs={{0,1},{1,0},{2,3},{3,2},{4,5},{5,4},{6,7},{7,6},{8,9},{9,8},{10,11... | collective-permute-start | bytes 3538952 | tf_op jit(solution)/shard_map/ppermute | solution.py:101
  560.3 43.7 %collective-permute-start.69 = (f32[96,1920]{1,0:T(8,128)S(1)}, f32[96,1920]{1,0:T(8,128)S(1)}, u32[]{:S(2)}, u32[]{:S(2)}) collective-permute-start(f32[96,1920]{1,0:T(8,128)S(1)} %get-tuple-element.260), channel_id=1, source_target_pairs={{0,16},{8,24},{16,0},{24,8},{1,17},{9,25},{17,1},{25,9},{2,18},{10... | collective-permute-start | bytes 2211848 | tf_op jit(solution)/shard_map/ppermute | solution.py:101
  562.1 45.2 %collective-permute-start.68 = (f32[96,1920]{1,0:T(8,128)S(1)}, f32[96,1920]{1,0:T(8,128)}, u32[]{:S(2)}, u32[]{:S(2)}) collective-permute-start(f32[96,1920]{1,0:T(8,128)S(1)} %get-tuple-element.260), channel_id=1, source_target_pairs={{0,8},{8,0},{16,24},{24,16},{1,9},{9,1},{17,25},{25,17},{2,10},{10... | collective-permute-start | bytes 2211848 | tf_op jit(solution)/shard_map/ppermute | solution.py:101
  (83 other events, 1137.7 us)
Sparse Core Ops, SparseCore 0:
  10.7 57.1 all-gather.5
  70.8 112.5 all-gather.3
  332.9 165.2 reduce-scatter.1

commit v3 on v2

--- a/solution.py
+++ b/solution.py
@@ -23,7 +23,25 @@
 clip_scale = 1.25
 
 VMEM_LIMIT = 60 * 1024 * 1024
-SMALL = pl.CostEstimate(flops=0, bytes_accessed=1024, transcendentals=0)
+SHARE = 0.0
+MICROSECONDS = dict(
+    gather_vectors=3,
+    embed_t=9,
+    embed_s=9,
+    attention=7,
+    layer_t=23,
+    layer_s=33,
+    owner_grads=8,
+    feed_back=23,
+    unit_grads=7,
+    attention_back=16,
+    embed_back=9,
+)
+
+
+def cost(name):
+    flops = int(SHARE * MICROSECONDS[name] * 1.15e9)
+    return pl.CostEstimate(flops=flops, bytes_accessed=1024, transcendentals=0)
 BF16 = jnp.bfloat16
 F32 = jnp.float32
 
@@ -188,6 +206,14 @@
         return copies
 
 
+def tie_groups(values, *groups):
+    tied = tie(*values, *[array for group in groups for array in group.arrays])
+    values, arrays = tied[: len(values)], list(tied[len(values) :])
+    for group in groups:
+        group.arrays = [arrays.pop(0) for _ in group.arrays]
+    return values
+
+
 class Gathered(Group):
     def __init__(self, gathered, number, groups, wide, where):
         count = lax.axis_size("fsdp")
@@ -256,34 +282,54 @@
         + [pltpu.SemaphoreType.DMA((group.blocks,)) for group in groups]
         + list(scratch),
         compiler_params=pltpu.CompilerParams(vmem_limit_bytes=VMEM_LIMIT),
-        cost_estimate=SMALL,
+        cost_estimate=cost(name),
         name=name,
     )(where, *[array for group in groups for array in group.arrays], *ins)
 
 
-def vector_kernel(pieces_ref, out_ref):
-    count, width = pieces_ref.shape[0], pieces_ref.shape[3]
-    for k in range(count):
-        out_ref[:, :, k * width : (k + 1) * width] = pieces_ref[k]
-
-
-def gather_vectors(mine):
-    pieces = lax.all_gather(mine, "fsdp", axis=0)
+def vector_kernel(where_ref, pieces_ref, out_ref):
+    _, two, rows, width = pieces_ref.shape
+    count = pieces_ref.shape[0] // 4
+    for u in range(4):
+        for k in range(count):
+            place = jnp.bitwise_xor(where_ref[0], u) * count + jnp.bitwise_xor(where_ref[1], k)
+            out_ref[:, u * rows : (u + 1) * rows, k * width : (k + 1) * width] = pieces_ref[place]
+
+
+def gather_vectors(both, where):
+    rows = -(-both.shape[1] // 32) * 8
+    both = jnp.pad(both, ((0, 0), (0, 4 * rows - both.shape[1]), (0, 0)))
+    pieces = lax.dynamic_slice_in_dim(both, where[0] * rows, rows, axis=1)[None]
+    for stage in [("fsdp", bit) for bit in reversed(fsdp_bits())] + [("rep", 1), ("rep", 2)]:
+        pieces = jnp.concatenate([pieces, swap(pieces, stage)], axis=0)
+    return pieces
+
+
+def place_vectors(pieces, where):
     count, two, rows, width = pieces.shape
     return pl.pallas_call(
         vector_kernel,
-        out_shape=jax.ShapeDtypeStruct((two, rows, count * width), mine.dtype),
-        in_specs=[vmem_spec()],
+        out_shape=jax.ShapeDtypeStruct((two, 4 * rows, count // 4 * width), pieces.dtype),
+        in_specs=[smem_spec(), vmem_spec()],
         out_specs=vmem_spec(),
         compiler_params=pltpu.CompilerParams(vmem_limit_bytes=VMEM_LIMIT),
+        cost_estimate=cost("gather_vectors"),
         name="gather_vectors",
-    )(pieces)
+    )(where, pieces)
 
 
 def reduce_order(kind):
     stages = [("fsdp", bit) for bit in reversed(fsdp_bits())]
     place = 0 if kind == 0 else 1
     return stages[:place] + [("rep", 2)] + stages[place:]
+
+
+def position(stages, unit, owner):
+    place = 0
+    for axis, bit in stages:
+        value = unit if axis == "rep" else owner
+        place = place * 2 + jnp.where(jnp.bitwise_and(value, bit) != 0, 1, 0)
+    return place
 
 
 def grad_kernel(unit_of, kind_stages, rows, width, where_ref, *refs):
@@ -302,14 +348,8 @@
                 @pl.when(jnp.bitwise_and(shifted, 1) == other)
                 def _():
                     for f in range(owners):
-                        apart = jnp.bitwise_xor(own, f)
-                        position = 0
-                        for axis, bit in kind_stages:
-                            value = shifted if axis == "rep" else apart
-                            position = position * 2 + jnp.where(
-                                jnp.bitwise_and(value, bit) != 0, 1, 0
-                            )
-                        target[pl.ds(pl.multiple_of(position * rows, 8), rows), :] = product[
+                        place = position(kind_stages, shifted, jnp.bitwise_xor(own, f))
+                        target[pl.ds(pl.multiple_of(place * rows, 8), rows), :] = product[
                             f * rows : (f + 1) * rows, :
                         ]
 
@@ -325,7 +365,7 @@
             in_specs=[smem_spec()] + [vmem_spec()] * (2 * len(pairs)),
             out_specs=(vmem_spec(), vmem_spec()),
             compiler_params=pltpu.CompilerParams(vmem_limit_bytes=VMEM_LIMIT),
-            cost_estimate=SMALL,
+            cost_estimate=cost("unit_grads"),
             name="unit_grads",
         )(where, *[left for left, _ in pairs], *[right for _, right in pairs]),
         kind,
@@ -377,7 +417,7 @@
         in_specs=[vmem_spec()] * 2,
         out_specs=vmem_spec(),
         compiler_params=pltpu.CompilerParams(vmem_limit_bytes=VMEM_LIMIT),
-        cost_estimate=SMALL,
+        cost_estimate=cost("owner_grads"),
         name="owner_grads",
     )(left, right)
 
@@ -429,7 +469,7 @@
         in_specs=[block] * 3,
         out_specs=(block, small),
         compiler_params=pltpu.CompilerParams(vmem_limit_bytes=VMEM_LIMIT),
-        cost_estimate=SMALL,
+        cost_estimate=cost("attention"),
         name="attention",
     )(query, key_rows, value_rows)
 
@@ -478,7 +518,7 @@
         in_specs=[block] * 4 + [small],
         out_specs=(block,) * 3,
         compiler_params=pltpu.CompilerParams(vmem_limit_bytes=VMEM_LIMIT),
-        cost_estimate=SMALL,
+        cost_estimate=cost("attention_back"),
         name="attention_back",
     )(query, key_rows, value_rows, grad, logsum)
 
@@ -699,9 +739,9 @@
     tiles(width, project)
 
 
-def embed_back_body(samples, seq_len, base, where_ref, loads, ins, outs, scratch):
+def embed_back_body(samples, seq_len, base, stages, where_ref, loads, ins, outs, scratch):
     gq_ref, gk_ref, gv_ref, gfirst_ref, mask_ref, after_ref, inner_ref, up_ref = ins
-    ge_ref, pieces_ref = outs
+    ge_ref, keep_ref, send_ref = outs
     all_ref, pos_ref = scratch
     weights = loads[0]()
     width = gq_ref.shape[1]
@@ -737,9 +777,20 @@
         all_ref[base + 8 + k : base + 9 + k, :] = up_ref[:, k * width : (k + 1) * width]
     all_ref[base + 12 : base + 14, :] = after_ref[1:3, :]
     all_ref[base + 14 : base + 15, :] = after_ref[0:1, :]
-    count, _, size = pieces_ref.shape
-    for k in range(count):
-        pieces_ref[jnp.bitwise_xor(where_ref[1], k)] = all_ref[:, k * size : (k + 1) * size]
+    quarter, size = keep_ref.shape[1:]
+    used = base + 15
+    all_ref[used:, :] = jnp.zeros_like(all_ref[used:, :])
+    for unit in range(4):
+        shifted = jnp.bitwise_xor(where_ref[0], unit)
+        for other, target in ((0, keep_ref), (1, send_ref)):
+
+            @pl.when(jnp.bitwise_and(shifted, 1) == other)
+            def _():
+                for f in range(width // size):
+                    place = position(stages, shifted, jnp.bitwise_xor(where_ref[1], f))
+                    target[place] = all_ref[
+                        unit * quarter : (unit + 1) * quarter, f * size : (f + 1) * size
+                    ]
 
 
 def adam_step(master, moment_one, moment_two, gradient, factor):
@@ -794,8 +845,7 @@
         width = array.shape[3] // 4
         return to_low(lax.dynamic_slice_in_dim(array[0, number], rep * width, width, axis=1))
 
-    vector_old_new = gather_vectors(jnp.stack([vector_weights, vector_teacher]))
-    vector_all, vector_old = vector_old_new[0], vector_old_new[1]
+    pieces = gather_vectors(jnp.stack([vector_weights, vector_teacher]), where)
     both_s = lax.all_gather(
         jnp.concatenate([columns_of(feed_weights, 0), columns_of(feed_weights, 1)]),
         ("fsdp", "rep"),
@@ -812,8 +862,15 @@
     outer = Group(others, 0, False, where, entry_s)
     up_t = Group(columns_of(feed_teacher, 0), 1, True, where, outer)
     down_t = Group(columns_of(feed_teacher, 1), 0, True, where, up_t)
-    for group in (entry_t, entry_s, outer, up_t, down_t):
+    entry_t.step(), entry_t.step()
+    (pieces,) = tie_groups([pieces], entry_t)
+    vector_old_new = place_vectors(pieces, where)
+    vector_all, vector_old = vector_old_new[0], vector_old_new[1]
+    for group in (entry_t, entry_s, outer):
         group.fabric()
+    for group in (up_t, down_t):
+        group.step(), group.step()
+    (patch_rows_t,) = tie_groups([patch_rows], up_t)
     base = 2 + seq_len
 
     def positions(vector):
@@ -823,7 +880,7 @@
     low_wide, full_wide = ((row_count, hidden_units), BF16), ((row_count, hidden_units), F32)
     column = ((row_count, 1), F32)
 
-    def entry(group, vector, masked, name):
+    def entry(patch_rows, group, vector, masked, name):
         return call(
             functools.partial(embed_body, samples, masked, base),
             name,
@@ -834,17 +891,20 @@
         )
 
     hidden_t, _, query, key_rows, value_rows = entry(
-        entry_t.finish(), vector_old, False, "embed_t"
-    )
+        patch_rows_t, entry_t.finish(), vector_old, False, "embed_t"
+    )
+    up_t.fabric()
+    (query,) = tie_groups([query], down_t)
+    down_t.fabric()
     attended_t, _ = attention_forward(query, key_rows, value_rows, samples, seq_len)
-    entry_s.arrays[0], attended_t = tie(entry_s.arrays[0], attended_t)
+    (attended_t,) = tie_groups([attended_t], entry_s, outer)
     hidden, hidden_low, query, key_rows, value_rows = entry(
-        entry_s.finish(), vector_all, True, "embed_s"
+        patch_rows, entry_s.finish(), vector_all, True, "embed_s"
     )
     attended, logsum = attention_forward(query, key_rows, value_rows, samples, seq_len)
-    outer.finish(), up_t.finish()
-    down_t.arrays[0], attended = tie(down_t.arrays[0], attended)
-    down_t.finish()
+    outer.finish()
+    (attended,) = tie_groups([attended], up_t, down_t)
+    up_t.finish(), down_t.finish()
     (target,) = call(
         functools.partial(teacher_body, samples, seq_len, base),
         "layer_t",
@@ -907,6 +967,7 @@
     edge_g = unit_grads(
         [(final_low, grad_output), (attended, grad_branch)], halves, 0, half, where
     )
+    up_a.step()
     up_b.step()
     (grad_attended,) = tie_sums([grad_attended], up_b, edge_g)
     grad_query, grad_key, grad_value = attention_backward(
@@ -914,47 +975,61 @@
     )
     edge_g.step()
     grad_query, grad_key, grad_value = tie_sums([grad_query, grad_key, grad_value], edge_g)
-    vector_count = vector_all.shape[0]
+    up_b.step()
+    vector_count = vector_weights.shape[0]
     count = lax.axis_size("fsdp")
-    grad_embed, pieces = call(
-        functools.partial(embed_back_body, samples, seq_len, base),
+    quarter = vector_all.shape[0] // 4
+    vector_block = ((2 * count, quarter, model_width // count), F32)
+    grad_embed, *vector_g = call(
+        functools.partial(embed_back_body, samples, seq_len, base, reduce_order(0)),
         "embed_back",
         where,
         [entry_s],
         [grad_query, grad_key, grad_value, grad_first, mask_rows, rows_after, rows_inner, rows_up],
-        [low_full, ((count, vector_count, model_width // count), F32)],
-        [pltpu.VMEM((vector_count, model_width), F32), pltpu.VMEM((pad_len, model_width), F32)],
+        [low_full, vector_block, vector_block],
+        [pltpu.VMEM(vector_all.shape, F32), pltpu.VMEM((pad_len, model_width), F32)],
     )
 
     def entry_half(grad, number):
         pairs = [(hidden_low, grad_query), (hidden_low, grad_key), (hidden_low, grad_value), (patch_rows, grad)]
         return unit_grads(pairs, [[(number * half, k)] for k in range(4)], number, half, where)
 
+    vector_g = Summing(*vector_g, 0)
+    edge_g.step()
+    (grad_embed,) = tie_sums([grad_embed], up_b, up_a)
+    qkv_a = entry_half(grad_embed, 0)
+    up_b.step()
     up_a.step()
-    (grad_embed,) = tie_sums([grad_embed], up_a)
-    qkv_a = entry_half(grad_embed, 0)
+    vector_g.step()
+    (grad_embed,) = tie_sums([grad_embed], up_a, edge_g, vector_g, qkv_a)
+    qkv_b = entry_half(grad_embed, 1)
+    up_a.step()
     edge_g.step()
-    (grad_embed,) = tie_sums([grad_embed], edge_g, qkv_a)
-    qkv_b = entry_half(grad_embed, 1)
     qkv_a.step()
+    vector_g.step()
+    (down_own,) = tie_sums([down_own], qkv_a, qkv_b, up_b, vector_g, up_a)
+    qkv_a.step()
+    qkv_b.step()
     up_b.step()
-    tie_sums([], up_b, qkv_a)
-
+    up_a.step()
+    vector_g.step()
+    tie_sums([], qkv_b, up_b, vector_g)
+    qkv_b.step()
+    up_b.step()
+    vector_g.step()
+    tie_sums([], edge_g, vector_g, up_b, qkv_a, qkv_b)
+    edge_g.step()
+
+    edge_own = edge_g.finish()
+    vector_own = vector_g.finish()
     up_own = jnp.concatenate([up_a.finish(), up_b.finish()], axis=1)
-    edge_own = edge_g.finish()
     qkv_own = jnp.concatenate([qkv_a.finish(), qkv_b.finish()], axis=1)
-    for bit in fsdp_bits():
-        count = pieces.shape[0] // 2
-        pieces = pieces[:count] + swap(pieces[count:], ("fsdp", bit))
-    vector_share = pieces[0]
-    for bit in (2, 1):
-        vector_share = vector_share + swap(vector_share, ("rep", bit))
     squares_own = (
         jnp.sum(down_own * down_own)
         + jnp.sum(up_own * up_own)
         + jnp.sum(edge_own * edge_own)
         + jnp.sum(qkv_own * qkv_own)
-        + 0.25 * jnp.sum(vector_share * vector_share)
+        + jnp.sum(vector_own * vector_own)
     )
     totals = jnp.stack([squares_own, loss_local])
     for bit in fsdp_bits():
@@ -967,7 +1042,14 @@
         shared = share_units(own_units)
         return [lax.dynamic_index_in_dim(shared, rep ^ k, keepdims=False) for k in range(4)]
 
-    early_u, qkv_u = ordered(jnp.concatenate([down_own, up_own, edge_own], axis=1)), ordered(qkv_own)
+    early_u = ordered(jnp.concatenate([down_own, up_own, edge_own], axis=1))
+    late_u = ordered(
+        jnp.concatenate([qkv_own, vector_own.reshape(qkv_own.shape[0], quarter)], axis=1)
+    )
+    qkv_u = [own[:, :unit] for own in late_u]
+    vector_share = jnp.concatenate(
+        [own[:, unit:].reshape(vector_own.shape[1:]) for own in late_u], axis=0
+    )[:vector_count]
     down_u = [own[:, :unit] for own in early_u]
     up_u = [own[:, unit : 2 * unit] for own in early_u]
     edge_u = [own[:, 2 * unit :] for own in early_u]

time: 635 us -> 614 us (0.967)
  waiting for transfers between devices: 250 us -> 236 us
  starting transfers between devices: 87.6 us -> 75.9 us
    ppermute x71 -> x76, waiting for transfers between devices: 250 us -> 236 us  [swap(): lax.ppermute(values, axis, [(i, i ^ bit) for i in range(lax.axis_size(axi...]
    ppermute x71 -> x76, starting transfers between devices: 87.5 us -> 75.8 us  [swap(): lax.ppermute(values, axis, [(i, i ^ bit) for i in range(lax.axis_size(axi...]
    add x20 -> x24, other arithmetic: 28.8 us -> 33.8 us  [step(): self.parts = (keep[:half] + got[:half], keep[half:] + got[half:])]
  transfers between devices with their start and end apart: 74 -> 78, of which waited for: 35 -> 40; matrix products, arithmetic and copies ran while one was open for 10% -> 11% of each run, Pallas kernels for 18% -> 24%
where the time goes in v3:
time: 614 us; the launch traced here: 609 us
  waiting for transfers between devices  236 us (38%)
  Pallas kernels  187 us (30%)
  starting transfers between devices  75.9 us (12%)
  other arithmetic  64.1 us (10%)
  local copies, waits for them, and re-layouts  25.1 us (4%)
  between operations  20.9 us (3%)
    ppermute x76, waiting for transfers between devices, swap(): lax.ppermute(values, axis, [(i, i ^ bit) for i in range(lax.axis_size(axi...  236 us
    pallas_call x6, Pallas kernels, call(): pl.pallas_call(kernel, out_shape=tuple((jax.ShapeDtypeStruct(*out) for ou...  107 us
    ppermute x76, starting transfers between devices, swap(): lax.ppermute(values, axis, [(i, i ^ bit) for i in range(lax.axis_size(axi...  75.8 us
    pallas_call x5, Pallas kernels, unit_grads(): pl.pallas_call(functools.partial(grad_kernel, unit_of, reduce_order(kind)...  37.5 us
    add x24, other arithmetic, step(): self.parts = (keep[:half] + got[:half], keep[half:] + got[half:])  33.8 us
    pallas_call x1, Pallas kernels, attention_backward(): pl.pallas_call(functools.partial(attention_back_kernel, seq_len, head_dim...  16.1 us
    pallas_call x2, Pallas kernels, attention_forward(): pl.pallas_call(functools.partial(attention_kernel, seq_len, head_dim), gr...  14.7 us
  transfers between devices with their start and end apart: 78, of which 40 were waited for; matrix products, arithmetic and copies ran while one was open for 11% of the time, Pallas kernels for 24%

profile of v3, /device:TPU:0, one launch (start us, length us, event | category | flops | bytes accessed | tf_op | source)
XLA Modules:
  0.0 608.9 jit_solution(2388381731584800386)
XLA Ops:
  31.9 8.2 %collective-permute-done.2 = f32[4,2,48,96]{3,2,1,0:T(8,128)S(1)} collective-permute-done((f32[4,2,48,96]{3,2,1,0:T(8,128)S(1)}, f32[4,2,48,96]{3,2,1,0:T(8,128)S(1)}, u32[]{:S(2)}, u32[]{:S(2)}) %collective-permute-start.2) | collective-permute-done | bytes 147488 | tf_op jit(solution)/shard_map/ppermute | solution.py:119
  45.6 11.2 %collective-permute-done.11 = bf16[96,768]{1,0:T(8,128)(2,1)S(1)} collective-permute-done((bf16[96,768]{1,0:T(8,128)(2,1)S(1)}, bf16[96,768]{1,0:T(8,128)(2,1)S(1)}, u32[]{:S(2)}, u32[]{:S(2)}) %collective-permute-start.11) | collective-permute-done | bytes 147488 | tf_op jit(solution)/shard_map/ppermute | solution.py:119
  57.9 8.7 %collective-permute-done.12 = bf16[96,768]{1,0:T(8,128)(2,1)S(1)} collective-permute-done((bf16[96,768]{1,0:T(8,128)(2,1)S(1)}, bf16[96,768]{1,0:T(8,128)(2,1)S(1)}, u32[]{:S(2)}, u32[]{:S(2)}) %collective-permute-start.12) | collective-permute-done | bytes 147488 | tf_op jit(solution)/shard_map/ppermute | solution.py:119
  81.3 15.0 %collective-permute-done.22 = bf16[192,768]{1,0:T(8,128)(2,1)S(1)} collective-permute-done((bf16[192,768]{1,0:T(8,128)(2,1)S(1)}, bf16[192,768]{1,0:T(8,128)(2,1)S(1)}, u32[]{:S(2)}, u32[]{:S(2)}) %collective-permute-start.22) | collective-permute-done | bytes 294944 | tf_op jit(solution)/shard_map/ppermute | solution.py:119
  110.9 18.6 %collective-permute-done.20 = bf16[384,768]{1,0:T(8,128)(2,1)S(1)} collective-permute-done((bf16[384,768]{1,0:T(8,128)(2,1)S(1)}, bf16[384,768]{1,0:T(8,128)(2,1)S(1)}, u32[]{:S(2)}, u32[]{:S(2)}) %collective-permute-start.20) | collective-permute-done | bytes 589856 | tf_op jit(solution)/shard_map/ppermute | solution.py:119
  150.3 21.3 %collective-permute-done.18 = bf16[384,768]{1,0:T(8,128)(2,1)S(1)} collective-permute-done((bf16[384,768]{1,0:T(8,128)(2,1)}, bf16[384,768]{1,0:T(8,128)(2,1)S(1)}, u32[]{:S(2)}, u32[]{:S(2)}) %collective-permute-start.18) | collective-permute-done | bytes 589856 | tf_op jit(solution)/shard_map/ppermute | solution.py:119
  173.7 9.2 %embed_t.1 = (f32[504,768]{1,0:T(8,128)}, bf16[504,768]{1,0:T(8,128)(2,1)}, bf16[504,768]{1,0:T(8,128)(2,1)}, bf16[504,768]{1,0:T(8,128)(2,1)}, bf16[504,768]{1,0:T(8,128)(2,1)}) custom-call(s32[2]{0:T(128)} %pad_add_fusion.where_ref, bf16[768,768]{1,0:T(8,128)(2,1)} %copy-done.7, bf16[768,768]{1,0:T(8,128)(2,1)} %collective-permute-done.8.refs_1_, ...), custom_call_target="tpu_custom_call" | custom-call | bytes 1024 | tf_op jit(solution)/shard_map/embed_t/pallas_call | solution.py:276
  182.9 7.4 %attention.2 = (bf16[504,768]{1,0:T(8,128)(2,1)}, f32[504,128]{1,0:T(8,128)}) custom-call(bf16[504,768]{1,0:T(8,128)(2,1)} %get-tuple-element.153.q_ref, bf16[504,768]{1,0:T(8,128)(2,1)} %get-tuple-element.154.k_ref, bf16[504,768]{1,0:T(8,128)(2,1)} %get-tuple-element.155.v_ref), custom_call_target="tpu_custom_call" | custom-call | bytes 1024 | tf_op jit(solution)/shard_map/attention/pallas_call | solution.py:462
  197.6 9.1 %embed_s.1 = (f32[504,768]{1,0:T(8,128)}, bf16[504,768]{1,0:T(8,128)(2,1)}, bf16[504,768]{1,0:T(8,128)(2,1)}, bf16[504,768]{1,0:T(8,128)(2,1)}, bf16[504,768]{1,0:T(8,128)(2,1)}) custom-call(s32[2]{0:T(128)} %pad_add_fusion.where_ref, bf16[768,768]{1,0:T(8,128)(2,1)} %constant_dynamic-update-slice_fusion.11.refs_0_, ...), custom_call_target="tpu_custom_call" | custom-call | bytes 1024 | tf_op jit(solution)/shard_map/embed_s/pallas_call | solution.py:276
  206.7 7.3 %attention.3 = (bf16[504,768]{1,0:T(8,128)(2,1)}, f32[504,128]{1,0:T(8,128)}) custom-call(bf16[504,768]{1,0:T(8,128)(2,1)} %get-tuple-element.163.q_ref, bf16[504,768]{1,0:T(8,128)(2,1)} %get-tuple-element.164.k_ref, bf16[504,768]{1,0:T(8,128)(2,1)} %get-tuple-element.165.v_ref), custom_call_target="tpu_custom_call" | custom-call | bytes 1024 | tf_op jit(solution)/shard_map/attention/pallas_call | solution.py:462
  229.8 23.5 %layer_t.1.refs_9_ = f32[504,768]{1,0:T(8,128)} custom-call(s32[2]{0:T(128)} %pad_add_fusion.where_ref, bf16[768,768]{1,0:T(8,128)(2,1)} %copy-done, bf16[768,768]{1,0:T(8,128)(2,1)} %copy-done.1, bf16[768,768]{1,0:T(8,128)(2,1)} %copy-done.2, bf16[768,768]{1,0:T(8,128)(2,1)} %collective-permute-done.26.refs_3_, bf16[768,768]{1,0:T(8,128)(2,1)} %pad_maximum_fusion.3.refs_4_, ...), custom_call_target="tpu_custom_call" | custom-call | bytes 1024 | tf_op jit(solution)/shard_map/layer_t/pallas_call | solution.py:276
  253.3 32.7 %layer_s.1 = (bf16[504,768]{1,0:T(8,128)(2,1)}, bf16[504,768]{1,0:T(8,128)(2,1)}, bf16[504,768]{1,0:T(8,128)(2,1)}, f32[504,768]{1,0:T(8,128)}, bf16[504,3072]{1...) custom-call(s32[2]{0:T(128)} %pad_add_fusion.where_ref, ...), custom_call_target="tpu_custom_call" | custom-call | bytes 1024 | tf_op jit(solution)/shard_map/layer_s/pallas_call | solution.py:276
  286.1 8.3 %owner_grads.1 = f32[3072,768]{1,0:T(8,128)} custom-call(bf16[504,768]{1,0:T(8,128)(2,1)} %get-tuple-element.180.left_ref.refs_6_, bf16[504,3072]{1,0:T(8,128)(2,1)} %get-tuple-element.178.right_ref), custom_call_target="tpu_custom_call" | custom-call | bytes 1024 | tf_op jit(solution)/shard_map/owner_grads/pallas_call | solution.py:414
  294.4 23.3 %feed_back.1 = (bf16[504,3072]{1,0:T(8,128)(2,1)}, f32[504,768]{1,0:T(8,128)}, bf16[504,768]{1,0:T(8,128)(2,1)}, bf16[504,768]{1,0:T(8,128)(2,1)}, f32[8,768]{1,0:T(8,128)}, /*index=5*/f32[1,3072]{1,0:T(1,128)}) custom-call(s32[2]{0:T(128)} %pad_add_fusion.where_ref, bf16[768,768]{1,0:T(8,128)(2,1)} %copy-done, bf16[768,768]{1,0:T(8,128)(2,1)} %copy-done.1, ...), custom_call_target="tpu_custom_call" | custom-call | bytes 1024 | tf_op jit(solution)/shard_map/feed_back/pallas_call | solution.py:276
  317.7 7.2 %unit_grads.5 = (f32[1536,384]{1,0:T(8,128)}, f32[1536,384]{1,0:T(8,128)}) custom-call(s32[2]{0:T(128)} %pad_add_fusion.where_ref, bf16[504,768]{1,0:T(8,128)(2,1)} %get-tuple-element.188.refs_0_, bf16[504,3072]{1,0:T(8,128)(2,1)} %get-tuple-element.193.refs_1_), custom_call_target="tpu_custom_call" | custom-call | bytes 1024 | tf_op jit(solution)/shard_map/unit_grads/pallas_call | solution.py:362
  325.1 7.2 %unit_grads.6 = (f32[1536,384]{1,0:T(8,128)}, f32[1536,384]{1,0:T(8,128)}) custom-call(s32[2]{0:T(128)} %pad_add_fusion.where_ref, bf16[504,768]{1,0:T(8,128)(2,1)} %get-tuple-element.188.refs_0_, bf16[504,3072]{1,0:T(8,128)(2,1)} %get-tuple-element.193.refs_1_), custom_call_target="tpu_custom_call" | custom-call | bytes 1024 | tf_op jit(solution)/shard_map/unit_grads/pallas_call | solution.py:362
  348.7 16.1 %attention_back.1 = (bf16[504,768]{1,0:T(8,128)(2,1)}, bf16[504,768]{1,0:T(8,128)(2,1)}, bf16[504,768]{1,0:T(8,128)(2,1)}) custom-call(bf16[504,768]{1,0:T(8,128)(2,1)} %get-tuple-element.163.q_ref, bf16[504,768]{1,0:T(8,128)(2,1)} %get-tuple-element.164.k_ref, bf16[504,768]{1,0:T(8,128)(2,1)} %get-tuple-element.165.v_ref, ...), custom_call_target="tpu_custom_call" | custom-call | bytes 1024 | tf_op jit(solution)/shard_map/attention_back/pallas_call | solution.py:514
  369.0 23.0 %collective-permute-done.39 = f32[768,384]{1,0:T(8,128)} collective-permute-done((f32[768,384]{1,0:T(8,128)}, f32[768,384]{1,0:T(8,128)}, u32[]{:S(2)}, u32[]{:S(2)}) %collective-permute-start.39) | collective-permute-done | bytes 1179680 | tf_op jit(solution)/shard_map/ppermute | solution.py:119
  395.6 9.4 %embed_back.1 = (bf16[504,768]{1,0:T(8,128)(2,1)}, f32[16,48,96]{2,1,0:T(8,128)}, f32[16,48,96]{2,1,0:T(8,128)}) custom-call(s32[2]{0:T(128)} %pad_add_fusion.where_ref, bf16[768,768]{1,0:T(8,128)(2,1)} %constant_dynamic-update-slice_fusion.11.refs_0_, bf16[768,768]{1,0:T(8,128)(2,1)} %collective-permute-done.21.refs_1_, ...), custom_call_target="tpu_custom_call" | custom-call | bytes 1024 | tf_op jit(solution)/shard_map/embed_back/pallas_call | solution.py:276
  406.0 8.0 %unit_grads.8 = (f32[1536,384]{1,0:T(8,128)}, f32[1536,384]{1,0:T(8,128)}) custom-call(s32[2]{0:T(128)} %pad_add_fusion.where_ref, bf16[504,768]{1,0:T(8,128)(2,1)} %get-tuple-element.229.refs_0_.refs_1_.refs_2_, bf16[504,768]{1,0:T(8,128)(2,1)} %get-tuple-element.229.refs_0_.refs_1_.refs_2_, bf16[504,768]{1,0:T(8,128)(2,1)} %get-tuple-element.229.refs_0_.refs_1_.refs_2_, ...), custom_call_target="tpu_custom_call" | custom-call | bytes 1024 | tf_op jit(solution)/shard_map/unit_grads/pallas_call | solution.py:362
  416.0 11.8 %collective-permute-done.40 = f32[384,384]{1,0:T(8,128)S(1)} collective-permute-done((f32[384,384]{1,0:T(8,128)S(1)}, f32[384,384]{1,0:T(8,128)S(1)}, u32[]{:S(2)}, u32[]{:S(2)}) %collective-permute-start.40) | collective-permute-done | bytes 589856 | tf_op jit(solution)/shard_map/ppermute | solution.py:119
  434.6 14.8 %collective-permute-done.44 = f32[384,384]{1,0:T(8,128)S(1)} collective-permute-done((f32[384,384]{1,0:T(8,128)S(1)}, f32[384,384]{1,0:T(8,128)S(1)}, u32[]{:S(2)}, u32[]{:S(2)}) %collective-permute-start.44) | collective-permute-done | bytes 589856 | tf_op jit(solution)/shard_map/ppermute | solution.py:119
  450.3 8.2 %unit_grads.9 = (f32[1536,384]{1,0:T(8,128)}, f32[1536,384]{1,0:T(8,128)}) custom-call(s32[2]{0:T(128)} %pad_add_fusion.where_ref, bf16[504,768]{1,0:T(8,128)(2,1)} %get-tuple-element.229.refs_0_.refs_1_.refs_2_, bf16[504,768]{1,0:T(8,128)(2,1)} %get-tuple-element.229.refs_0_.refs_1_.refs_2_, bf16[504,768]{1,0:T(8,128)(2,1)} %get-tuple-element.229.refs_0_.refs_1_.refs_2_, ...), custom_call_target="tpu_custom_call" | custom-call | bytes 1024 | tf_op jit(solution)/shard_map/unit_grads/pallas_call | solution.py:362
  483.7 10.5 %collective-permute-done.54 = f32[768,384]{1,0:T(8,128)S(1)} collective-permute-done((f32[768,384]{1,0:T(8,128)}, f32[768,384]{1,0:T(8,128)S(1)}, u32[]{:S(2)}, u32[]{:S(2)}) %collective-permute-start.54) | collective-permute-done | bytes 1179680 | tf_op jit(solution)/shard_map/ppermute | solution.py:119
  (342 shorter events, 267.8 us)
Async XLA Ops:
  7.2 246.2 %all-gather.2.cloned.1.call-start = ((), (), s32[]{:S(2)}) async-start(), calls=%async_computation.1 | async-start | bytes 9732096 | tf_op jit(solution)/shard_map/all_gather | solution.py:849
  9.8 453.0 %reduce-scatter.2.cloned.1.call-start = ((), (), s32[]{:S(2)}) async-start(), calls=%async_computation.2 | async-start | bytes 9732096 | tf_op jit(solution)/shard_map/reduce_scatter | solution.py:945
  71.2 61.0 %collective-permute-start.8 = (bf16[768,768]{1,0:T(8,128)(2,1)S(1)}, bf16[768,768]{1,0:T(8,128)(2,1)}, u32[]{:S(2)}, u32[]{:S(2)}) collective-permute-start(bf16[768,768]{1,0:T(8,128)(2,1)S(1)} %pad_maximum_fusion.2.refs_0_), channel_id=1, source_target_pairs={{0,16},{8,24},{16,0},{24,8},{1,17},{9,25},{17,1},{25,9},{2,18},{10... | collective-permute-start | bytes 3538952 | tf_op jit(solution)/shard_map/ppermute | solution.py:119
  77.9 30.5 %collective-permute-start.14 = (bf16[192,768]{1,0:T(8,128)(2,1)S(1)}, bf16[192,768]{1,0:T(8,128)(2,1)S(1)}, u32[]{:S(2)}, u32[]{:S(2)}) collective-permute-start(bf16[192,768]{1,0:T(8,128)(2,1)S(1)} %pad_maximum_fusion.16), channel_id=1, source_target_pairs={{0,2},{1,3},{2,0},{3,1},{4,6},{5,7},{6,4},{7,5},{8,10},{9,11},{10,... | collective-permute-start | bytes 884744 | tf_op jit(solution)/shard_map/ppermute | solution.py:119
  81.0 48.6 %collective-permute-start.20 = (bf16[384,768]{1,0:T(8,128)(2,1)S(1)}, bf16[384,768]{1,0:T(8,128)(2,1)S(1)}, u32[]{:S(2)}, u32[]{:S(2)}) collective-permute-start(bf16[384,768]{1,0:T(8,128)(2,1)S(1)} %pad_maximum_fusion.9), channel_id=1, source_target_pairs={{0,16},{8,24},{16,0},{24,8},{1,17},{9,25},{17,1},{25,9},{2,18},{10... | collective-permute-start | bytes 1769480 | tf_op jit(solution)/shard_map/ppermute | solution.py:119
  96.4 34.0 %collective-permute-start.23 = (bf16[384,768]{1,0:T(8,128)(2,1)S(1)}, bf16[384,768]{1,0:T(8,128)(2,1)S(1)}, u32[]{:S(2)}, u32[]{:S(2)}) collective-permute-start(bf16[384,768]{1,0:T(8,128)(2,1)S(1)} %pad_maximum_fusion.10), channel_id=1, source_target_pairs={{0,1},{1,0},{2,3},{3,2},{4,5},{5,4},{6,7},{7,6},{8,9},{9,8},{10,11... | collective-permute-start | bytes 1769480 | tf_op jit(solution)/shard_map/ppermute | solution.py:119
  104.8 27.6 %collective-permute-start.17 = (bf16[192,768]{1,0:T(8,128)(2,1)S(1)}, bf16[192,768]{1,0:T(8,128)(2,1)}, u32[]{:S(2)}, u32[]{:S(2)}) collective-permute-start(bf16[192,768]{1,0:T(8,128)(2,1)S(1)} %pad_maximum_fusion.17), channel_id=1, source_target_pairs={{0,2},{1,3},{2,0},{3,1},{4,6},{5,7},{6,4},{7,5},{8,10},{9,11},{10,... | collective-permute-start | bytes 884744 | tf_op jit(solution)/shard_map/ppermute | solution.py:119
  109.3 33.0 %collective-permute-start.15 = (bf16[384,768]{1,0:T(8,128)(2,1)}, bf16[384,768]{1,0:T(8,128)(2,1)}, u32[]{:S(2)}, u32[]{:S(2)}) collective-permute-start(bf16[384,768]{1,0:T(8,128)(2,1)} %pad_maximum_fusion.7), channel_id=1, source_target_pairs={{0,16},{8,24},{16,0},{24,8},{1,17},{9,25},{17,1},{25,9},{2,18},{10... | collective-permute-start | bytes 1769480 | tf_op jit(solution)/shard_map/ppermute | solution.py:119
  129.6 44.2 %collective-permute-start.9 = (bf16[768,768]{1,0:T(8,128)(2,1)S(1)}, bf16[768,768]{1,0:T(8,128)(2,1)}, u32[]{:S(2)}, u32[]{:S(2)}) collective-permute-start(bf16[768,768]{1,0:T(8,128)(2,1)S(1)} %pad_maximum_fusion.2.refs_0_), channel_id=1, source_target_pairs={{0,8},{8,0},{16,24},{24,16},{1,9},{9,1},{17,25},{25,17},{2,10},{10... | collective-permute-start | bytes 3538952 | tf_op jit(solution)/shard_map/ppermute | solution.py:119
  130.4 59.9 %collective-permute-start.21 = (bf16[768,768]{1,0:T(8,128)(2,1)}, bf16[768,768]{1,0:T(8,128)(2,1)}, u32[]{:S(2)}, u32[]{:S(2)}) collective-permute-start(bf16[768,768]{1,0:T(8,128)(2,1)} %constant_dynamic-update-slice_fusion.11.refs_0_), channel_id=1, source_target_pairs={{0,1},{1,0},{2,3},{3,2},{4,5},{5,4},{6,7},{7,6},{8,9},{9,8},{10,11... | collective-permute-start | bytes 3538952 | tf_op jit(solution)/shard_map/ppermute | solution.py:119
  132.2 41.6 %collective-permute-start.10 = (bf16[768,768]{1,0:T(8,128)(2,1)}, bf16[768,768]{1,0:T(8,128)(2,1)}, u32[]{:S(2)}, u32[]{:S(2)}) collective-permute-start(bf16[768,768]{1,0:T(8,128)(2,1)} %collective-permute-done.8.refs_1_), channel_id=1, source_target_pairs={{0,8},{8,0},{16,24},{24,16},{1,9},{9,1},{17,25},{25,17},{2,10},{10... | collective-permute-start | bytes 3538952 | tf_op jit(solution)/shard_map/ppermute | solution.py:119
  132.5 57.8 %collective-permute-start.24 = (bf16[768,768]{1,0:T(8,128)(2,1)S(1)}, bf16[768,768]{1,0:T(8,128)(2,1)S(1)}, u32[]{:S(2)}, u32[]{:S(2)}) collective-permute-start(bf16[768,768]{1,0:T(8,128)(2,1)S(1)} %constant_dynamic-update-slice_fusion.14.refs_0_), channel_id=1, source_target_pairs={{0,16},{8,24},{16,0},{24,8},{1,17},{9,25},{17,1},{25,9},{2,18},{10... | collective-permute-start | bytes 3538952 | tf_op jit(solution)/shard_map/ppermute | solution.py:119
  142.3 29.4 %collective-permute-start.18 = (bf16[384,768]{1,0:T(8,128)(2,1)}, bf16[384,768]{1,0:T(8,128)(2,1)S(1)}, u32[]{:S(2)}, u32[]{:S(2)}) collective-permute-start(bf16[384,768]{1,0:T(8,128)(2,1)} %pad_maximum_fusion.8), channel_id=1, source_target_pairs={{0,1},{1,0},{2,3},{3,2},{4,5},{5,4},{6,7},{7,6},{8,9},{9,8},{10,11... | collective-permute-start | bytes 1769480 | tf_op jit(solution)/shard_map/ppermute | solution.py:119
  190.9 28.3 %collective-permute-start.29 = (bf16[768,768]{1,0:T(8,128)(2,1)}, bf16[768,768]{1,0:T(8,128)(2,1)}, u32[]{:S(2)}, u32[]{:S(2)}) collective-permute-start(bf16[768,768]{1,0:T(8,128)(2,1)} %pad_maximum_fusion.3.refs_4_), channel_id=1, source_target_pairs={{0,1},{1,0},{2,3},{3,2},{4,5},{5,4},{6,7},{7,6},{8,9},{9,8},{10,11... | collective-permute-start | bytes 3538952 | tf_op jit(solution)/shard_map/ppermute | solution.py:119
  192.6 28.0 %collective-permute-start.30 = (bf16[768,768]{1,0:T(8,128)(2,1)}, bf16[768,768]{1,0:T(8,128)(2,1)}, u32[]{:S(2)}, u32[]{:S(2)}) collective-permute-start(bf16[768,768]{1,0:T(8,128)(2,1)} %pad_maximum_fusion.4.refs_8_), channel_id=1, source_target_pairs={{0,16},{8,24},{16,0},{24,8},{1,17},{9,25},{17,1},{25,9},{2,18},{10... | collective-permute-start | bytes 3538952 | tf_op jit(solution)/shard_map/ppermute | solution.py:119
  194.1 27.0 %collective-permute-start.25 = (bf16[768,768]{1,0:T(8,128)(2,1)S(1)}, bf16[768,768]{1,0:T(8,128)(2,1)S(1)}, u32[]{:S(2)}, u32[]{:S(2)}) collective-permute-start(bf16[768,768]{1,0:T(8,128)(2,1)S(1)} %constant_dynamic-update-slice_fusion.14.refs_0_), channel_id=1, source_target_pairs={{0,8},{8,0},{16,24},{24,16},{1,9},{9,1},{17,25},{25,17},{2,10},{10... | collective-permute-start | bytes 3538952 | tf_op jit(solution)/shard_map/ppermute | solution.py:119
  347.1 45.0 %collective-permute-start.39 = (f32[768,384]{1,0:T(8,128)}, f32[768,384]{1,0:T(8,128)}, u32[]{:S(2)}, u32[]{:S(2)}) collective-permute-start(f32[768,384]{1,0:T(8,128)} %get-tuple-element.221), channel_id=1, source_target_pairs={{0,16},{8,24},{16,0},{24,8},{1,17},{9,25},{17,1},{25,9},{2,18},{10... | collective-permute-start | bytes 3538952 | tf_op jit(solution)/shard_map/ppermute | solution.py:119
  348.5 45.7 %collective-permute-start.38 = (f32[768,384]{1,0:T(8,128)}, f32[768,384]{1,0:T(8,128)}, u32[]{:S(2)}, u32[]{:S(2)}) collective-permute-start(f32[768,384]{1,0:T(8,128)} %get-tuple-element.219), channel_id=1, source_target_pairs={{0,1},{1,0},{2,3},{3,2},{4,5},{5,4},{6,7},{7,6},{8,9},{9,8},{10,11... | collective-permute-start | bytes 3538952 | tf_op jit(solution)/shard_map/ppermute | solution.py:119
  368.4 60.3 %collective-permute-start.41 = (f32[768,384]{1,0:T(8,128)}, f32[768,384]{1,0:T(8,128)}, u32[]{:S(2)}, u32[]{:S(2)}) collective-permute-start(f32[768,384]{1,0:T(8,128)} %get-tuple-element.226), channel_id=1, source_target_pairs={{0,16},{8,24},{16,0},{24,8},{1,17},{9,25},{17,1},{25,9},{2,18},{10... | collective-permute-start | bytes 3538952 | tf_op jit(solution)/shard_map/ppermute | solution.py:119
  431.1 28.9 %collective-permute-start.43 = (f32[1536,384]{1,0:T(8,128)}, f32[1536,384]{1,0:T(8,128)}, u32[]{:S(2)}, u32[]{:S(2)}) collective-permute-start(f32[1536,384]{1,0:T(8,128)} %get-tuple-element.233), channel_id=1, source_target_pairs={{0,8},{8,0},{16,24},{24,16},{1,9},{9,1},{17,25},{25,17},{2,10},{10... | collective-permute-start | bytes 7077896 | tf_op jit(solution)/shard_map/ppermute | solution.py:119
  466.4 27.8 %collective-permute-start.54 = (f32[768,384]{1,0:T(8,128)}, f32[768,384]{1,0:T(8,128)S(1)}, u32[]{:S(2)}, u32[]{:S(2)}) collective-permute-start(f32[768,384]{1,0:T(8,128)} %get-tuple-element.259), channel_id=1, source_target_pairs={{0,16},{8,24},{16,0},{24,8},{1,17},{9,25},{17,1},{25,9},{2,18},{10... | collective-permute-start | bytes 3538952 | tf_op jit(solution)/shard_map/ppermute | solution.py:119
  475.6 30.6 %collective-permute-start.55 = (f32[768,384]{1,0:T(8,128)S(1)}, f32[768,384]{1,0:T(8,128)S(1)}, u32[]{:S(2)}, u32[]{:S(2)}) collective-permute-start(f32[768,384]{1,0:T(8,128)S(1)} %get-tuple-element.261), channel_id=1, source_target_pairs={{0,1},{1,0},{2,3},{3,2},{4,5},{5,4},{6,7},{7,6},{8,9},{9,8},{10,11... | collective-permute-start | bytes 3538952 | tf_op jit(solution)/shard_map/ppermute | solution.py:119
  539.9 41.5 %collective-permute-start.74 = (f32[96,1920]{1,0:T(8,128)}, f32[96,1920]{1,0:T(8,128)}, u32[]{:S(2)}, u32[]{:S(2)}) collective-permute-start(f32[96,1920]{1,0:T(8,128)} %get-tuple-element.350), channel_id=1, source_target_pairs={{0,16},{8,24},{16,0},{24,8},{1,17},{9,25},{17,1},{25,9},{2,18},{10... | collective-permute-start | bytes 2211848 | tf_op jit(solution)/shard_map/ppermute | solution.py:119
  540.9 43.6 %collective-permute-start.73 = (f32[96,1920]{1,0:T(8,128)}, f32[96,1920]{1,0:T(8,128)}, u32[]{:S(2)}, u32[]{:S(2)}) collective-permute-start(f32[96,1920]{1,0:T(8,128)} %get-tuple-element.350), channel_id=1, source_target_pairs={{0,8},{8,0},{16,24},{24,16},{1,9},{9,1},{17,25},{25,17},{2,10},{10... | collective-permute-start | bytes 2211848 | tf_op jit(solution)/shard_map/ppermute | solution.py:119
  (91 other events, 1138.3 us)
Sparse Core Ops, SparseCore 0:
  10.9 119.1 all-gather.1
  294.5 159.1 reduce-scatter.1

commit v4 on v3

--- a/solution.py
+++ b/solution.py
@@ -524,6 +524,7 @@
 
 
 TILE = 256
+UNROLL = 3
 
 
 def tiles(width, body):
@@ -531,7 +532,7 @@
         body(pl.ds(pl.multiple_of(number * TILE, TILE), TILE))
         return carry
 
-    lax.fori_loop(0, width // TILE, step, 0)
+    lax.fori_loop(0, width // TILE, step, 0, unroll=min(UNROLL, width // TILE))
 
 
 def embed_body(samples, masked, base, where_ref, loads, ins, outs, scratch):
@@ -606,7 +607,7 @@
             widen(outer, vec_ref[base + 8 + quarter : base + 9 + quarter, inner])
             return carry
 
-        lax.fori_loop(0, size // TILE, step, 0)
+        lax.fori_loop(0, size // TILE, step, 0, unroll=min(UNROLL, size // TILE))
     down = loads[2]()
 
     def narrow(columns, target_ref, residual):

time: 614 us -> 608 us (level)
  starting transfers between devices: 75.9 us -> 89.1 us
  waiting for transfers between devices: 236 us -> 225 us
  Pallas kernels: 187 us -> 177 us
    ppermute x76, starting transfers between devices: 75.8 us -> 89 us  [swap(): lax.ppermute(values, axis, [(i, i ^ bit) for i in range(lax.axis_size(axi...]
    ppermute x76, waiting for transfers between devices: 236 us -> 224 us  [swap(): lax.ppermute(values, axis, [(i, i ^ bit) for i in range(lax.axis_size(axi...]
    pallas_call x6, Pallas kernels: 107 us -> 96.8 us  [call(): pl.pallas_call(kernel, out_shape=tuple((jax.ShapeDtypeStruct(*out) for ou...]
  transfers between devices with their start and end apart: 78 -> 78, of which waited for: 40 -> 40; matrix products, arithmetic and copies ran while one was open for 11% -> 11% of each run, Pallas kernels for 24% -> 23%
where the time goes in v4:
time: 608 us; the launch traced here: 602 us
  waiting for transfers between devices  225 us (37%)
  Pallas kernels  177 us (29%)
  starting transfers between devices  89.1 us (15%)
  other arithmetic  64 us (11%)
  local copies, waits for them, and re-layouts  25.1 us (4%)
  between operations  21 us (3%)
    ppermute x76, waiting for transfers between devices, swap(): lax.ppermute(values, axis, [(i, i ^ bit) for i in range(lax.axis_size(axi...  224 us
    pallas_call x6, Pallas kernels, call(): pl.pallas_call(kernel, out_shape=tuple((jax.ShapeDtypeStruct(*out) for ou...  96.8 us
    ppermute x76, starting transfers between devices, swap(): lax.ppermute(values, axis, [(i, i ^ bit) for i in range(lax.axis_size(axi...  89 us
    pallas_call x5, Pallas kernels, unit_grads(): pl.pallas_call(functools.partial(grad_kernel, unit_of, reduce_order(kind)...  37.8 us
    add x24, other arithmetic, step(): self.parts = (keep[:half] + got[:half], keep[half:] + got[half:])  33.8 us
    pallas_call x1, Pallas kernels, attention_backward(): pl.pallas_call(functools.partial(attention_back_kernel, seq_len, head_dim...  16 us
    pallas_call x2, Pallas kernels, attention_forward(): pl.pallas_call(functools.partial(attention_kernel, seq_len, head_dim), gr...  15.5 us
  transfers between devices with their start and end apart: 78, of which 40 were waited for; matrix products, arithmetic and copies ran while one was open for 11% of the time, Pallas kernels for 23%

profile of v4, /device:TPU:0, one launch (start us, length us, event | category | flops | bytes accessed | tf_op | source)
XLA Modules:
  0.0 601.6 jit_solution(14878272964904793341)
XLA Ops:
  31.9 8.2 %collective-permute-done.2 = f32[4,2,48,96]{3,2,1,0:T(8,128)S(1)} collective-permute-done((f32[4,2,48,96]{3,2,1,0:T(8,128)S(1)}, f32[4,2,48,96]{3,2,1,0:T(8,128)S(1)}, u32[]{:S(2)}, u32[]{:S(2)}) %collective-permute-start.2) | collective-permute-done | bytes 147488 | tf_op jit(solution)/shard_map/ppermute | solution.py:119
  45.6 11.2 %collective-permute-done.11 = bf16[96,768]{1,0:T(8,128)(2,1)S(1)} collective-permute-done((bf16[96,768]{1,0:T(8,128)(2,1)S(1)}, bf16[96,768]{1,0:T(8,128)(2,1)S(1)}, u32[]{:S(2)}, u32[]{:S(2)}) %collective-permute-start.11) | collective-permute-done | bytes 147488 | tf_op jit(solution)/shard_map/ppermute | solution.py:119
  57.9 8.7 %collective-permute-done.12 = bf16[96,768]{1,0:T(8,128)(2,1)S(1)} collective-permute-done((bf16[96,768]{1,0:T(8,128)(2,1)S(1)}, bf16[96,768]{1,0:T(8,128)(2,1)S(1)}, u32[]{:S(2)}, u32[]{:S(2)}) %collective-permute-start.12) | collective-permute-done | bytes 147488 | tf_op jit(solution)/shard_map/ppermute | solution.py:119
  81.3 15.0 %collective-permute-done.22 = bf16[192,768]{1,0:T(8,128)(2,1)S(1)} collective-permute-done((bf16[192,768]{1,0:T(8,128)(2,1)S(1)}, bf16[192,768]{1,0:T(8,128)(2,1)S(1)}, u32[]{:S(2)}, u32[]{:S(2)}) %collective-permute-start.22) | collective-permute-done | bytes 294944 | tf_op jit(solution)/shard_map/ppermute | solution.py:119
  110.9 18.6 %collective-permute-done.20 = bf16[384,768]{1,0:T(8,128)(2,1)S(1)} collective-permute-done((bf16[384,768]{1,0:T(8,128)(2,1)S(1)}, bf16[384,768]{1,0:T(8,128)(2,1)S(1)}, u32[]{:S(2)}, u32[]{:S(2)}) %collective-permute-start.20) | collective-permute-done | bytes 589856 | tf_op jit(solution)/shard_map/ppermute | solution.py:119
  150.3 21.3 %collective-permute-done.18 = bf16[384,768]{1,0:T(8,128)(2,1)S(1)} collective-permute-done((bf16[384,768]{1,0:T(8,128)(2,1)}, bf16[384,768]{1,0:T(8,128)(2,1)S(1)}, u32[]{:S(2)}, u32[]{:S(2)}) %collective-permute-start.18) | collective-permute-done | bytes 589856 | tf_op jit(solution)/shard_map/ppermute | solution.py:119
  173.7 8.4 %embed_t.1 = (f32[504,768]{1,0:T(8,128)}, bf16[504,768]{1,0:T(8,128)(2,1)}, bf16[504,768]{1,0:T(8,128)(2,1)}, bf16[504,768]{1,0:T(8,128)(2,1)}, bf16[504,768]{1,0:T(8,128)(2,1)}) custom-call(s32[2]{0:T(128)} %pad_add_fusion.where_ref, bf16[768,768]{1,0:T(8,128)(2,1)} %copy-done.7, bf16[768,768]{1,0:T(8,128)(2,1)} %collective-permute-done.8.refs_1_, ...), custom_call_target="tpu_custom_call" | custom-call | bytes 1024 | tf_op jit(solution)/shard_map/embed_t/pallas_call | solution.py:276
  182.2 7.7 %attention.2 = (bf16[504,768]{1,0:T(8,128)(2,1)}, f32[504,128]{1,0:T(8,128)}) custom-call(bf16[504,768]{1,0:T(8,128)(2,1)} %get-tuple-element.153.q_ref, bf16[504,768]{1,0:T(8,128)(2,1)} %get-tuple-element.154.k_ref, bf16[504,768]{1,0:T(8,128)(2,1)} %get-tuple-element.155.v_ref), custom_call_target="tpu_custom_call" | custom-call | bytes 1024 | tf_op jit(solution)/shard_map/attention/pallas_call | solution.py:462
  197.1 8.0 %embed_s.1 = (f32[504,768]{1,0:T(8,128)}, bf16[504,768]{1,0:T(8,128)(2,1)}, bf16[504,768]{1,0:T(8,128)(2,1)}, bf16[504,768]{1,0:T(8,128)(2,1)}, bf16[504,768]{1,0:T(8,128)(2,1)}) custom-call(s32[2]{0:T(128)} %pad_add_fusion.where_ref, bf16[768,768]{1,0:T(8,128)(2,1)} %constant_dynamic-update-slice_fusion.11.refs_0_, ...), custom_call_target="tpu_custom_call" | custom-call | bytes 1024 | tf_op jit(solution)/shard_map/embed_s/pallas_call | solution.py:276
  205.1 7.8 %attention.3 = (bf16[504,768]{1,0:T(8,128)(2,1)}, f32[504,128]{1,0:T(8,128)}) custom-call(bf16[504,768]{1,0:T(8,128)(2,1)} %get-tuple-element.163.q_ref, bf16[504,768]{1,0:T(8,128)(2,1)} %get-tuple-element.164.k_ref, bf16[504,768]{1,0:T(8,128)(2,1)} %get-tuple-element.165.v_ref), custom_call_target="tpu_custom_call" | custom-call | bytes 1024 | tf_op jit(solution)/shard_map/attention/pallas_call | solution.py:462
  229.3 21.7 %layer_t.1.refs_9_ = f32[504,768]{1,0:T(8,128)} custom-call(s32[2]{0:T(128)} %pad_add_fusion.where_ref, bf16[768,768]{1,0:T(8,128)(2,1)} %copy-done, bf16[768,768]{1,0:T(8,128)(2,1)} %copy-done.1, bf16[768,768]{1,0:T(8,128)(2,1)} %copy-done.2, bf16[768,768]{1,0:T(8,128)(2,1)} %collective-permute-done.26.refs_3_, bf16[768,768]{1,0:T(8,128)(2,1)} %pad_maximum_fusion.3.refs_4_, ...), custom_call_target="tpu_custom_call" | custom-call | bytes 1024 | tf_op jit(solution)/shard_map/layer_t/pallas_call | solution.py:276
  251.1 29.2 %layer_s.1 = (bf16[504,768]{1,0:T(8,128)(2,1)}, bf16[504,768]{1,0:T(8,128)(2,1)}, bf16[504,768]{1,0:T(8,128)(2,1)}, f32[504,768]{1,0:T(8,128)}, bf16[504,3072]{1...) custom-call(s32[2]{0:T(128)} %pad_add_fusion.where_ref, ...), custom_call_target="tpu_custom_call" | custom-call | bytes 1024 | tf_op jit(solution)/shard_map/layer_s/pallas_call | solution.py:276
  280.3 8.3 %owner_grads.1 = f32[3072,768]{1,0:T(8,128)} custom-call(bf16[504,768]{1,0:T(8,128)(2,1)} %get-tuple-element.180.left_ref.refs_6_, bf16[504,3072]{1,0:T(8,128)(2,1)} %get-tuple-element.178.right_ref), custom_call_target="tpu_custom_call" | custom-call | bytes 1024 | tf_op jit(solution)/shard_map/owner_grads/pallas_call | solution.py:414
  288.6 20.6 %feed_back.1 = (bf16[504,3072]{1,0:T(8,128)(2,1)}, f32[504,768]{1,0:T(8,128)}, bf16[504,768]{1,0:T(8,128)(2,1)}, bf16[504,768]{1,0:T(8,128)(2,1)}, f32[8,768]{1,0:T(8,128)}, /*index=5*/f32[1,3072]{1,0:T(1,128)}) custom-call(s32[2]{0:T(128)} %pad_add_fusion.where_ref, bf16[768,768]{1,0:T(8,128)(2,1)} %copy-done, bf16[768,768]{1,0:T(8,128)(2,1)} %copy-done.1, ...), custom_call_target="tpu_custom_call" | custom-call | bytes 1024 | tf_op jit(solution)/shard_map/feed_back/pallas_call | solution.py:276
  309.2 7.2 %unit_grads.5 = (f32[1536,384]{1,0:T(8,128)}, f32[1536,384]{1,0:T(8,128)}) custom-call(s32[2]{0:T(128)} %pad_add_fusion.where_ref, bf16[504,768]{1,0:T(8,128)(2,1)} %get-tuple-element.188.refs_0_, bf16[504,3072]{1,0:T(8,128)(2,1)} %get-tuple-element.193.refs_1_), custom_call_target="tpu_custom_call" | custom-call | bytes 1024 | tf_op jit(solution)/shard_map/unit_grads/pallas_call | solution.py:362
  316.5 7.2 %unit_grads.6 = (f32[1536,384]{1,0:T(8,128)}, f32[1536,384]{1,0:T(8,128)}) custom-call(s32[2]{0:T(128)} %pad_add_fusion.where_ref, bf16[504,768]{1,0:T(8,128)(2,1)} %get-tuple-element.188.refs_0_, bf16[504,3072]{1,0:T(8,128)(2,1)} %get-tuple-element.193.refs_1_), custom_call_target="tpu_custom_call" | custom-call | bytes 1024 | tf_op jit(solution)/shard_map/unit_grads/pallas_call | solution.py:362
  340.3 16.0 %attention_back.1 = (bf16[504,768]{1,0:T(8,128)(2,1)}, bf16[504,768]{1,0:T(8,128)(2,1)}, bf16[504,768]{1,0:T(8,128)(2,1)}) custom-call(bf16[504,768]{1,0:T(8,128)(2,1)} %get-tuple-element.163.q_ref, bf16[504,768]{1,0:T(8,128)(2,1)} %get-tuple-element.164.k_ref, bf16[504,768]{1,0:T(8,128)(2,1)} %get-tuple-element.165.v_ref, ...), custom_call_target="tpu_custom_call" | custom-call | bytes 1024 | tf_op jit(solution)/shard_map/attention_back/pallas_call | solution.py:514
  360.4 21.8 %collective-permute-done.39 = f32[768,384]{1,0:T(8,128)} collective-permute-done((f32[768,384]{1,0:T(8,128)}, f32[768,384]{1,0:T(8,128)}, u32[]{:S(2)}, u32[]{:S(2)}) %collective-permute-start.39) | collective-permute-done | bytes 1179680 | tf_op jit(solution)/shard_map/ppermute | solution.py:119
  385.7 8.8 %embed_back.1 = (bf16[504,768]{1,0:T(8,128)(2,1)}, f32[16,48,96]{2,1,0:T(8,128)}, f32[16,48,96]{2,1,0:T(8,128)}) custom-call(s32[2]{0:T(128)} %pad_add_fusion.where_ref, bf16[768,768]{1,0:T(8,128)(2,1)} %constant_dynamic-update-slice_fusion.11.refs_0_, bf16[768,768]{1,0:T(8,128)(2,1)} %collective-permute-done.21.refs_1_, ...), custom_call_target="tpu_custom_call" | custom-call | bytes 1024 | tf_op jit(solution)/shard_map/embed_back/pallas_call | solution.py:276
  394.7 8.0 %unit_grads.8 = (f32[1536,384]{1,0:T(8,128)}, f32[1536,384]{1,0:T(8,128)}) custom-call(s32[2]{0:T(128)} %pad_add_fusion.where_ref, bf16[504,768]{1,0:T(8,128)(2,1)} %get-tuple-element.229.refs_0_.refs_1_.refs_2_, bf16[504,768]{1,0:T(8,128)(2,1)} %get-tuple-element.229.refs_0_.refs_1_.refs_2_, bf16[504,768]{1,0:T(8,128)(2,1)} %get-tuple-element.229.refs_0_.refs_1_.refs_2_, ...), custom_call_target="tpu_custom_call" | custom-call | bytes 1024 | tf_op jit(solution)/shard_map/unit_grads/pallas_call | solution.py:362
  404.7 10.8 %collective-permute-done.40 = f32[384,384]{1,0:T(8,128)S(1)} collective-permute-done((f32[384,384]{1,0:T(8,128)S(1)}, f32[384,384]{1,0:T(8,128)S(1)}, u32[]{:S(2)}, u32[]{:S(2)}) %collective-permute-start.40) | collective-permute-done | bytes 589856 | tf_op jit(solution)/shard_map/ppermute | solution.py:119
  427.4 7.5 %collective-permute-done.44 = f32[384,384]{1,0:T(8,128)S(1)} collective-permute-done((f32[384,384]{1,0:T(8,128)S(1)}, f32[384,384]{1,0:T(8,128)S(1)}, u32[]{:S(2)}, u32[]{:S(2)}) %collective-permute-start.44) | collective-permute-done | bytes 589856 | tf_op jit(solution)/shard_map/ppermute | solution.py:119
  435.9 8.2 %unit_grads.9 = (f32[1536,384]{1,0:T(8,128)}, f32[1536,384]{1,0:T(8,128)}) custom-call(s32[2]{0:T(128)} %pad_add_fusion.where_ref, bf16[504,768]{1,0:T(8,128)(2,1)} %get-tuple-element.229.refs_0_.refs_1_.refs_2_, bf16[504,768]{1,0:T(8,128)(2,1)} %get-tuple-element.229.refs_0_.refs_1_.refs_2_, bf16[504,768]{1,0:T(8,128)(2,1)} %get-tuple-element.229.refs_0_.refs_1_.refs_2_, ...), custom_call_target="tpu_custom_call" | custom-call | bytes 1024 | tf_op jit(solution)/shard_map/unit_grads/pallas_call | solution.py:362
  476.5 10.5 %collective-permute-done.54 = f32[768,384]{1,0:T(8,128)S(1)} collective-permute-done((f32[768,384]{1,0:T(8,128)}, f32[768,384]{1,0:T(8,128)S(1)}, u32[]{:S(2)}, u32[]{:S(2)}) %collective-permute-start.54) | collective-permute-done | bytes 1179680 | tf_op jit(solution)/shard_map/ppermute | solution.py:119
  (342 shorter events, 279.9 us)
Async XLA Ops:
  7.2 243.9 %all-gather.2.cloned.1.call-start = ((), (), s32[]{:S(2)}) async-start(), calls=%async_computation.1 | async-start | bytes 9732096 | tf_op jit(solution)/shard_map/all_gather | solution.py:850
  9.8 440.1 %reduce-scatter.2.cloned.1.call-start = ((), (), s32[]{:S(2)}) async-start(), calls=%async_computation.2 | async-start | bytes 9732096 | tf_op jit(solution)/shard_map/reduce_scatter | solution.py:946
  71.2 61.0 %collective-permute-start.8 = (bf16[768,768]{1,0:T(8,128)(2,1)S(1)}, bf16[768,768]{1,0:T(8,128)(2,1)}, u32[]{:S(2)}, u32[]{:S(2)}) collective-permute-start(bf16[768,768]{1,0:T(8,128)(2,1)S(1)} %pad_maximum_fusion.2.refs_0_), channel_id=1, source_target_pairs={{0,16},{8,24},{16,0},{24,8},{1,17},{9,25},{17,1},{25,9},{2,18},{10... | collective-permute-start | bytes 3538952 | tf_op jit(solution)/shard_map/ppermute | solution.py:119
  77.9 30.5 %collective-permute-start.14 = (bf16[192,768]{1,0:T(8,128)(2,1)S(1)}, bf16[192,768]{1,0:T(8,128)(2,1)S(1)}, u32[]{:S(2)}, u32[]{:S(2)}) collective-permute-start(bf16[192,768]{1,0:T(8,128)(2,1)S(1)} %pad_maximum_fusion.16), channel_id=1, source_target_pairs={{0,2},{1,3},{2,0},{3,1},{4,6},{5,7},{6,4},{7,5},{8,10},{9,11},{10,... | collective-permute-start | bytes 884744 | tf_op jit(solution)/shard_map/ppermute | solution.py:119
  81.0 48.6 %collective-permute-start.20 = (bf16[384,768]{1,0:T(8,128)(2,1)S(1)}, bf16[384,768]{1,0:T(8,128)(2,1)S(1)}, u32[]{:S(2)}, u32[]{:S(2)}) collective-permute-start(bf16[384,768]{1,0:T(8,128)(2,1)S(1)} %pad_maximum_fusion.9), channel_id=1, source_target_pairs={{0,16},{8,24},{16,0},{24,8},{1,17},{9,25},{17,1},{25,9},{2,18},{10... | collective-permute-start | bytes 1769480 | tf_op jit(solution)/shard_map/ppermute | solution.py:119
  96.4 34.0 %collective-permute-start.23 = (bf16[384,768]{1,0:T(8,128)(2,1)S(1)}, bf16[384,768]{1,0:T(8,128)(2,1)S(1)}, u32[]{:S(2)}, u32[]{:S(2)}) collective-permute-start(bf16[384,768]{1,0:T(8,128)(2,1)S(1)} %pad_maximum_fusion.10), channel_id=1, source_target_pairs={{0,1},{1,0},{2,3},{3,2},{4,5},{5,4},{6,7},{7,6},{8,9},{9,8},{10,11... | collective-permute-start | bytes 1769480 | tf_op jit(solution)/shard_map/ppermute | solution.py:119
  104.8 27.6 %collective-permute-start.17 = (bf16[192,768]{1,0:T(8,128)(2,1)S(1)}, bf16[192,768]{1,0:T(8,128)(2,1)}, u32[]{:S(2)}, u32[]{:S(2)}) collective-permute-start(bf16[192,768]{1,0:T(8,128)(2,1)S(1)} %pad_maximum_fusion.17), channel_id=1, source_target_pairs={{0,2},{1,3},{2,0},{3,1},{4,6},{5,7},{6,4},{7,5},{8,10},{9,11},{10,... | collective-permute-start | bytes 884744 | tf_op jit(solution)/shard_map/ppermute | solution.py:119
  109.3 33.0 %collective-permute-start.15 = (bf16[384,768]{1,0:T(8,128)(2,1)}, bf16[384,768]{1,0:T(8,128)(2,1)}, u32[]{:S(2)}, u32[]{:S(2)}) collective-permute-start(bf16[384,768]{1,0:T(8,128)(2,1)} %pad_maximum_fusion.7), channel_id=1, source_target_pairs={{0,16},{8,24},{16,0},{24,8},{1,17},{9,25},{17,1},{25,9},{2,18},{10... | collective-permute-start | bytes 1769480 | tf_op jit(solution)/shard_map/ppermute | solution.py:119
  129.6 44.2 %collective-permute-start.9 = (bf16[768,768]{1,0:T(8,128)(2,1)S(1)}, bf16[768,768]{1,0:T(8,128)(2,1)}, u32[]{:S(2)}, u32[]{:S(2)}) collective-permute-start(bf16[768,768]{1,0:T(8,128)(2,1)S(1)} %pad_maximum_fusion.2.refs_0_), channel_id=1, source_target_pairs={{0,8},{8,0},{16,24},{24,16},{1,9},{9,1},{17,25},{25,17},{2,10},{10... | collective-permute-start | bytes 3538952 | tf_op jit(solution)/shard_map/ppermute | solution.py:119
  130.4 59.4 %collective-permute-start.21 = (bf16[768,768]{1,0:T(8,128)(2,1)}, bf16[768,768]{1,0:T(8,128)(2,1)}, u32[]{:S(2)}, u32[]{:S(2)}) collective-permute-start(bf16[768,768]{1,0:T(8,128)(2,1)} %constant_dynamic-update-slice_fusion.11.refs_0_), channel_id=1, source_target_pairs={{0,1},{1,0},{2,3},{3,2},{4,5},{5,4},{6,7},{7,6},{8,9},{9,8},{10,11... | collective-permute-start | bytes 3538952 | tf_op jit(solution)/shard_map/ppermute | solution.py:119
  132.2 41.6 %collective-permute-start.10 = (bf16[768,768]{1,0:T(8,128)(2,1)}, bf16[768,768]{1,0:T(8,128)(2,1)}, u32[]{:S(2)}, u32[]{:S(2)}) collective-permute-start(bf16[768,768]{1,0:T(8,128)(2,1)} %collective-permute-done.8.refs_1_), channel_id=1, source_target_pairs={{0,8},{8,0},{16,24},{24,16},{1,9},{9,1},{17,25},{25,17},{2,10},{10... | collective-permute-start | bytes 3538952 | tf_op jit(solution)/shard_map/ppermute | solution.py:119
  132.5 57.4 %collective-permute-start.24 = (bf16[768,768]{1,0:T(8,128)(2,1)S(1)}, bf16[768,768]{1,0:T(8,128)(2,1)S(1)}, u32[]{:S(2)}, u32[]{:S(2)}) collective-permute-start(bf16[768,768]{1,0:T(8,128)(2,1)S(1)} %constant_dynamic-update-slice_fusion.14.refs_0_), channel_id=1, source_target_pairs={{0,16},{8,24},{16,0},{24,8},{1,17},{9,25},{17,1},{25,9},{2,18},{10... | collective-permute-start | bytes 3538952 | tf_op jit(solution)/shard_map/ppermute | solution.py:119
  142.3 29.4 %collective-permute-start.18 = (bf16[384,768]{1,0:T(8,128)(2,1)}, bf16[384,768]{1,0:T(8,128)(2,1)S(1)}, u32[]{:S(2)}, u32[]{:S(2)}) collective-permute-start(bf16[384,768]{1,0:T(8,128)(2,1)} %pad_maximum_fusion.8), channel_id=1, source_target_pairs={{0,1},{1,0},{2,3},{3,2},{4,5},{5,4},{6,7},{7,6},{8,9},{9,8},{10,11... | collective-permute-start | bytes 1769480 | tf_op jit(solution)/shard_map/ppermute | solution.py:119
  190.4 28.3 %collective-permute-start.29 = (bf16[768,768]{1,0:T(8,128)(2,1)}, bf16[768,768]{1,0:T(8,128)(2,1)}, u32[]{:S(2)}, u32[]{:S(2)}) collective-permute-start(bf16[768,768]{1,0:T(8,128)(2,1)} %pad_maximum_fusion.3.refs_4_), channel_id=1, source_target_pairs={{0,1},{1,0},{2,3},{3,2},{4,5},{5,4},{6,7},{7,6},{8,9},{9,8},{10,11... | collective-permute-start | bytes 3538952 | tf_op jit(solution)/shard_map/ppermute | solution.py:119
  192.2 28.0 %collective-permute-start.30 = (bf16[768,768]{1,0:T(8,128)(2,1)}, bf16[768,768]{1,0:T(8,128)(2,1)}, u32[]{:S(2)}, u32[]{:S(2)}) collective-permute-start(bf16[768,768]{1,0:T(8,128)(2,1)} %pad_maximum_fusion.4.refs_8_), channel_id=1, source_target_pairs={{0,16},{8,24},{16,0},{24,8},{1,17},{9,25},{17,1},{25,9},{2,18},{10... | collective-permute-start | bytes 3538952 | tf_op jit(solution)/shard_map/ppermute | solution.py:119
  193.7 27.0 %collective-permute-start.25 = (bf16[768,768]{1,0:T(8,128)(2,1)S(1)}, bf16[768,768]{1,0:T(8,128)(2,1)S(1)}, u32[]{:S(2)}, u32[]{:S(2)}) collective-permute-start(bf16[768,768]{1,0:T(8,128)(2,1)S(1)} %constant_dynamic-update-slice_fusion.14.refs_0_), channel_id=1, source_target_pairs={{0,8},{8,0},{16,24},{24,16},{1,9},{9,1},{17,25},{25,17},{2,10},{10... | collective-permute-start | bytes 3538952 | tf_op jit(solution)/shard_map/ppermute | solution.py:119
  338.8 43.4 %collective-permute-start.39 = (f32[768,384]{1,0:T(8,128)}, f32[768,384]{1,0:T(8,128)}, u32[]{:S(2)}, u32[]{:S(2)}) collective-permute-start(f32[768,384]{1,0:T(8,128)} %get-tuple-element.221), channel_id=1, source_target_pairs={{0,16},{8,24},{16,0},{24,8},{1,17},{9,25},{17,1},{25,9},{2,18},{10... | collective-permute-start | bytes 3538952 | tf_op jit(solution)/shard_map/ppermute | solution.py:119
  340.1 44.2 %collective-permute-start.38 = (f32[768,384]{1,0:T(8,128)}, f32[768,384]{1,0:T(8,128)}, u32[]{:S(2)}, u32[]{:S(2)}) collective-permute-start(f32[768,384]{1,0:T(8,128)} %get-tuple-element.219), channel_id=1, source_target_pairs={{0,1},{1,0},{2,3},{3,2},{4,5},{5,4},{6,7},{7,6},{8,9},{9,8},{10,11... | collective-permute-start | bytes 3538952 | tf_op jit(solution)/shard_map/ppermute | solution.py:119
  359.9 56.5 %collective-permute-start.41 = (f32[768,384]{1,0:T(8,128)}, f32[768,384]{1,0:T(8,128)}, u32[]{:S(2)}, u32[]{:S(2)}) collective-permute-start(f32[768,384]{1,0:T(8,128)} %get-tuple-element.226), channel_id=1, source_target_pairs={{0,16},{8,24},{16,0},{24,8},{1,17},{9,25},{17,1},{25,9},{2,18},{10... | collective-permute-start | bytes 3538952 | tf_op jit(solution)/shard_map/ppermute | solution.py:119
  418.8 26.8 %collective-permute-start.43 = (f32[1536,384]{1,0:T(8,128)}, f32[1536,384]{1,0:T(8,128)}, u32[]{:S(2)}, u32[]{:S(2)}) collective-permute-start(f32[1536,384]{1,0:T(8,128)} %get-tuple-element.233), channel_id=1, source_target_pairs={{0,8},{8,0},{16,24},{24,16},{1,9},{9,1},{17,25},{25,17},{2,10},{10... | collective-permute-start | bytes 7077896 | tf_op jit(solution)/shard_map/ppermute | solution.py:119
  459.2 27.8 %collective-permute-start.54 = (f32[768,384]{1,0:T(8,128)}, f32[768,384]{1,0:T(8,128)S(1)}, u32[]{:S(2)}, u32[]{:S(2)}) collective-permute-start(f32[768,384]{1,0:T(8,128)} %get-tuple-element.259), channel_id=1, source_target_pairs={{0,16},{8,24},{16,0},{24,8},{1,17},{9,25},{17,1},{25,9},{2,18},{10... | collective-permute-start | bytes 3538952 | tf_op jit(solution)/shard_map/ppermute | solution.py:119
  468.1 30.0 %collective-permute-start.55 = (f32[768,384]{1,0:T(8,128)S(1)}, f32[768,384]{1,0:T(8,128)S(1)}, u32[]{:S(2)}, u32[]{:S(2)}) collective-permute-start(f32[768,384]{1,0:T(8,128)S(1)} %get-tuple-element.261), channel_id=1, source_target_pairs={{0,1},{1,0},{2,3},{3,2},{4,5},{5,4},{6,7},{7,6},{8,9},{9,8},{10,11... | collective-permute-start | bytes 3538952 | tf_op jit(solution)/shard_map/ppermute | solution.py:119
  532.6 41.5 %collective-permute-start.74 = (f32[96,1920]{1,0:T(8,128)}, f32[96,1920]{1,0:T(8,128)}, u32[]{:S(2)}, u32[]{:S(2)}) collective-permute-start(f32[96,1920]{1,0:T(8,128)} %get-tuple-element.350), channel_id=1, source_target_pairs={{0,16},{8,24},{16,0},{24,8},{1,17},{9,25},{17,1},{25,9},{2,18},{10... | collective-permute-start | bytes 2211848 | tf_op jit(solution)/shard_map/ppermute | solution.py:119
  534.1 43.2 %collective-permute-start.73 = (f32[96,1920]{1,0:T(8,128)}, f32[96,1920]{1,0:T(8,128)}, u32[]{:S(2)}, u32[]{:S(2)}) collective-permute-start(f32[96,1920]{1,0:T(8,128)} %get-tuple-element.350), channel_id=1, source_target_pairs={{0,8},{8,0},{16,24},{24,16},{1,9},{9,1},{17,25},{25,17},{2,10},{10... | collective-permute-start | bytes 2211848 | tf_op jit(solution)/shard_map/ppermute | solution.py:119
  (91 other events, 1142.6 us)
Sparse Core Ops, SparseCore 0:
  10.9 119.1 all-gather.1
  288.7 161.1 reduce-scatter.1

commit v5 on v4

--- a/solution.py
+++ b/solution.py
@@ -869,9 +869,7 @@
     vector_all, vector_old = vector_old_new[0], vector_old_new[1]
     for group in (entry_t, entry_s, outer):
         group.fabric()
-    for group in (up_t, down_t):
-        group.step(), group.step()
-    (patch_rows_t,) = tie_groups([patch_rows], up_t)
+    up_t.fabric(), down_t.fabric()
     base = 2 + seq_len
 
     def positions(vector):
@@ -892,11 +890,8 @@
         )
 
     hidden_t, _, query, key_rows, value_rows = entry(
-        patch_rows_t, entry_t.finish(), vector_old, False, "embed_t"
-    )
-    up_t.fabric()
-    (query,) = tie_groups([query], down_t)
-    down_t.fabric()
+        patch_rows, entry_t.finish(), vector_old, False, "embed_t"
+    )
     attended_t, _ = attention_forward(query, key_rows, value_rows, samples, seq_len)
     (attended_t,) = tie_groups([attended_t], entry_s, outer)
     hidden, hidden_low, query, key_rows, value_rows = entry(
@@ -997,20 +992,21 @@
 
     vector_g = Summing(*vector_g, 0)
     edge_g.step()
-    (grad_embed,) = tie_sums([grad_embed], up_b, up_a)
+    (grad_embed,) = tie_sums([grad_embed], up_a)
     qkv_a = entry_half(grad_embed, 0)
-    up_b.step()
     up_a.step()
     vector_g.step()
-    (grad_embed,) = tie_sums([grad_embed], up_a, edge_g, vector_g, qkv_a)
+    (grad_embed,) = tie_sums([grad_embed], up_b, vector_g, qkv_a)
     qkv_b = entry_half(grad_embed, 1)
+    up_b.step()
+    qkv_a.step()
+    tie_sums([], qkv_a, qkv_b, up_a, edge_g)
+    qkv_a.step()
+    qkv_b.step()
     up_a.step()
     edge_g.step()
-    qkv_a.step()
     vector_g.step()
-    (down_own,) = tie_sums([down_own], qkv_a, qkv_b, up_b, vector_g, up_a)
-    qkv_a.step()
-    qkv_b.step()
+    tie_sums([], qkv_b, up_b, vector_g, up_a)
     up_b.step()
     up_a.step()
     vector_g.step()
@@ -1018,7 +1014,7 @@
     qkv_b.step()
     up_b.step()
     vector_g.step()
-    tie_sums([], edge_g, vector_g, up_b, qkv_a, qkv_b)
+    (down_own,) = tie_sums([down_own], edge_g, vector_g, up_b, qkv_a, qkv_b)
     edge_g.step()
 
     edge_own = edge_g.finish()

time: 608 us -> 590 us (0.970)
  starting transfers between devices: 89.1 us -> 76.3 us
  local copies, waits for them, and re-layouts: 25.1 us -> 32.8 us
  other arithmetic: 64 us -> 56.9 us
    ppermute x76, starting transfers between devices: 89 us -> 76.3 us  [swap(): lax.ppermute(values, axis, [(i, i ^ bit) for i in range(lax.axis_size(axi...]
    add x24, other arithmetic: 33.8 us -> 27.6 us  [step(): self.parts = (keep[:half] + got[:half], keep[half:] + got[half:])]
    unnamed x86 -> x93, local copies, waits for them, and re-layouts: 10.2 us -> 14.1 us
  transfers between devices with their start and end apart: 78 -> 78, of which waited for: 40 -> 41; matrix products, arithmetic and copies ran while one was open for 11% -> 11% of each run, Pallas kernels for 23% -> 19%
where the time goes in v5:
time: 590 us; the launch traced here: 583 us
  waiting for transfers between devices  220 us (37%)
  Pallas kernels  176 us (30%)
  starting transfers between devices  76.3 us (13%)
  other arithmetic  56.9 us (10%)
  local copies, waits for them, and re-layouts  32.8 us (6%)
  between operations  21 us (4%)
    ppermute x76, waiting for transfers between devices, swap(): lax.ppermute(values, axis, [(i, i ^ bit) for i in range(lax.axis_size(axi...  220 us
    pallas_call x6, Pallas kernels, call(): pl.pallas_call(kernel, out_shape=tuple((jax.ShapeDtypeStruct(*out) for ou...  96.9 us
    ppermute x76, starting transfers between devices, swap(): lax.ppermute(values, axis, [(i, i ^ bit) for i in range(lax.axis_size(axi...  76.3 us
    pallas_call x5, Pallas kernels, unit_grads(): pl.pallas_call(functools.partial(grad_kernel, unit_of, reduce_order(kind)...  37.1 us
    add x24, other arithmetic, step(): self.parts = (keep[:half] + got[:half], keep[half:] + got[half:])  27.6 us
    pallas_call x1, Pallas kernels, attention_backward(): pl.pallas_call(functools.partial(attention_back_kernel, seq_len, head_dim...  16 us
    pallas_call x2, Pallas kernels, attention_forward(): pl.pallas_call(functools.partial(attention_kernel, seq_len, head_dim), gr...  15.3 us
    unnamed x93, local copies, waits for them, and re-layouts  14.1 us
  transfers between devices with their start and end apart: 78, of which 41 were waited for; matrix products, arithmetic and copies ran while one was open for 11% of the time, Pallas kernels for 19%

profile of v5, /device:TPU:0, one launch (start us, length us, event | category | flops | bytes accessed | tf_op | source)
XLA Modules:
  0.0 583.3 jit_solution(10669263836192202161)
XLA Ops:
  88.8 6.6 %collective-permute-done.16 = bf16[192,768]{1,0:T(8,128)(2,1)S(1)} collective-permute-done((bf16[192,768]{1,0:T(8,128)(2,1)S(1)}, bf16[192,768]{1,0:T(8,128)(2,1)S(1)}, u32[]{:S(2)}, u32[]{:S(2)}) %collective-permute-start.16) | collective-permute-done | bytes 294944 | tf_op jit(solution)/shard_map/ppermute | solution.py:119
  96.2 8.0 %collective-permute-done.27 = bf16[96,768]{1,0:T(8,128)(2,1)S(1)} collective-permute-done((bf16[96,768]{1,0:T(8,128)(2,1)S(1)}, bf16[96,768]{1,0:T(8,128)(2,1)S(1)}, u32[]{:S(2)}, u32[]{:S(2)}) %collective-permute-start.27) | collective-permute-done | bytes 147488 | tf_op jit(solution)/shard_map/ppermute | solution.py:119
  110.9 20.2 %collective-permute-done.13 = bf16[384,768]{1,0:T(8,128)(2,1)S(1)} collective-permute-done((bf16[384,768]{1,0:T(8,128)(2,1)S(1)}, bf16[384,768]{1,0:T(8,128)(2,1)S(1)}, u32[]{:S(2)}, u32[]{:S(2)}) %collective-permute-start.13) | collective-permute-done | bytes 589856 | tf_op jit(solution)/shard_map/ppermute | solution.py:119
  151.8 8.4 %embed_t.1 = (f32[504,768]{1,0:T(8,128)}, bf16[504,768]{1,0:T(8,128)(2,1)}, bf16[504,768]{1,0:T(8,128)(2,1)}, bf16[504,768]{1,0:T(8,128)(2,1)}, bf16[504,768]{1,0:T(8,128)(2,1)}) custom-call(s32[2]{0:T(128)} %pad_add_fusion.where_ref, bf16[768,768]{1,0:T(8,128)(2,1)} %copy-done.7, bf16[768,768]{1,0:T(8,128)(2,1)} %collective-permute-done.8.refs_1_, ...), custom_call_target="tpu_custom_call" | custom-call | bytes 1024 | tf_op jit(solution)/shard_map/embed_t/pallas_call | solution.py:276
  160.3 7.8 %attention.2 = (bf16[504,768]{1,0:T(8,128)(2,1)}, f32[504,128]{1,0:T(8,128)}) custom-call(bf16[504,768]{1,0:T(8,128)(2,1)} %get-tuple-element.144.q_ref, bf16[504,768]{1,0:T(8,128)(2,1)} %get-tuple-element.145.k_ref, bf16[504,768]{1,0:T(8,128)(2,1)} %get-tuple-element.146.v_ref), custom_call_target="tpu_custom_call" | custom-call | bytes 1024 | tf_op jit(solution)/shard_map/attention/pallas_call | solution.py:462
  179.4 8.0 %embed_s.1 = (f32[504,768]{1,0:T(8,128)}, bf16[504,768]{1,0:T(8,128)(2,1)}, bf16[504,768]{1,0:T(8,128)(2,1)}, bf16[504,768]{1,0:T(8,128)(2,1)}, bf16[504,768]{1,0:T(8,128)(2,1)}) custom-call(s32[2]{0:T(128)} %pad_add_fusion.where_ref, bf16[768,768]{1,0:T(8,128)(2,1)} %constant_dynamic-update-slice_fusion.11.refs_0_, ...), custom_call_target="tpu_custom_call" | custom-call | bytes 1024 | tf_op jit(solution)/shard_map/embed_s/pallas_call | solution.py:276
  187.5 7.5 %attention.3 = (bf16[504,768]{1,0:T(8,128)(2,1)}, f32[504,128]{1,0:T(8,128)}) custom-call(bf16[504,768]{1,0:T(8,128)(2,1)} %get-tuple-element.156.q_ref, bf16[504,768]{1,0:T(8,128)(2,1)} %get-tuple-element.157.k_ref, bf16[504,768]{1,0:T(8,128)(2,1)} %get-tuple-element.158.v_ref), custom_call_target="tpu_custom_call" | custom-call | bytes 1024 | tf_op jit(solution)/shard_map/attention/pallas_call | solution.py:462
  212.3 21.7 %layer_t.1.refs_9_ = f32[504,768]{1,0:T(8,128)} custom-call(s32[2]{0:T(128)} %pad_add_fusion.where_ref, bf16[768,768]{1,0:T(8,128)(2,1)} %copy-done, bf16[768,768]{1,0:T(8,128)(2,1)} %copy-done.1, bf16[768,768]{1,0:T(8,128)(2,1)} %copy-done.2, bf16[768,768]{1,0:T(8,128)(2,1)} %collective-permute-done.20.refs_3_, ...), custom_call_target="tpu_custom_call" | custom-call | bytes 1024 | tf_op jit(solution)/shard_map/layer_t/pallas_call | solution.py:276
  234.0 29.2 %layer_s.1 = (bf16[504,768]{1,0:T(8,128)(2,1)}, bf16[504,768]{1,0:T(8,128)(2,1)}, bf16[504,768]{1,0:T(8,128)(2,1)}, f32[504,768]{1,0:T(8,128)}, bf16[504,3072]{1...) custom-call(s32[2]{0:T(128)} %pad_add_fusion.where_ref, ...), custom_call_target="tpu_custom_call" | custom-call | bytes 1024 | tf_op jit(solution)/shard_map/layer_s/pallas_call | solution.py:276
  263.2 8.3 %owner_grads.1 = f32[3072,768]{1,0:T(8,128)} custom-call(bf16[504,768]{1,0:T(8,128)(2,1)} %get-tuple-element.174.left_ref.refs_6_, bf16[504,3072]{1,0:T(8,128)(2,1)} %get-tuple-element.172.right_ref), custom_call_target="tpu_custom_call" | custom-call | bytes 1024 | tf_op jit(solution)/shard_map/owner_grads/pallas_call | solution.py:414
  271.5 20.1 %feed_back.1 = (bf16[504,3072]{1,0:T(8,128)(2,1)}, f32[504,768]{1,0:T(8,128)}, bf16[504,768]{1,0:T(8,128)(2,1)}, bf16[504,768]{1,0:T(8,128)(2,1)}, f32[8,768]{1,0:T(8,128)}, /*index=5*/f32[1,3072]{1,0:T(1,128)}) custom-call(s32[2]{0:T(128)} %pad_add_fusion.where_ref, bf16[768,768]{1,0:T(8,128)(2,1)} %copy-done, bf16[768,768]{1,0:T(8,128)(2,1)} %copy-done.1, ...), custom_call_target="tpu_custom_call" | custom-call | bytes 1024 | tf_op jit(solution)/shard_map/feed_back/pallas_call | solution.py:276
  291.6 7.4 %unit_grads.5 = (f32[1536,384]{1,0:T(8,128)}, f32[1536,384]{1,0:T(8,128)}) custom-call(s32[2]{0:T(128)} %pad_add_fusion.where_ref, bf16[504,768]{1,0:T(8,128)(2,1)} %get-tuple-element.182.refs_0_, bf16[504,3072]{1,0:T(8,128)(2,1)} %get-tuple-element.187.refs_1_), custom_call_target="tpu_custom_call" | custom-call | bytes 1024 | tf_op jit(solution)/shard_map/unit_grads/pallas_call | solution.py:362
  299.2 7.2 %unit_grads.6 = (f32[1536,384]{1,0:T(8,128)}, f32[1536,384]{1,0:T(8,128)}) custom-call(s32[2]{0:T(128)} %pad_add_fusion.where_ref, bf16[504,768]{1,0:T(8,128)(2,1)} %get-tuple-element.182.refs_0_, bf16[504,3072]{1,0:T(8,128)(2,1)} %get-tuple-element.187.refs_1_), custom_call_target="tpu_custom_call" | custom-call | bytes 1024 | tf_op jit(solution)/shard_map/unit_grads/pallas_call | solution.py:362
  309.7 6.8 %unit_grads.7 = (f32[1536,384]{1,0:T(8,128)}, f32[1536,384]{1,0:T(8,128)}) custom-call(s32[2]{0:T(128)} %pad_add_fusion.where_ref, bf16[504,768]{1,0:T(8,128)(2,1)} %get-tuple-element.192.refs_0_, bf16[504,768]{1,0:T(8,128)(2,1)} %get-tuple-element.163.refs_6_.refs_1_, bf16[504,768]{1,0:T(8,128)(2,1)} %get-tuple-element.193.refs_2_, ...), custom_call_target="tpu_custom_call" | custom-call | bytes 1024 | tf_op jit(solution)/shard_map/unit_grads/pallas_call | solution.py:362
  322.1 16.0 %attention_back.1 = (bf16[504,768]{1,0:T(8,128)(2,1)}, bf16[504,768]{1,0:T(8,128)(2,1)}, bf16[504,768]{1,0:T(8,128)(2,1)}) custom-call(bf16[504,768]{1,0:T(8,128)(2,1)} %get-tuple-element.156.q_ref, bf16[504,768]{1,0:T(8,128)(2,1)} %get-tuple-element.157.k_ref, bf16[504,768]{1,0:T(8,128)(2,1)} %get-tuple-element.158.v_ref, ...), custom_call_target="tpu_custom_call" | custom-call | bytes 1024 | tf_op jit(solution)/shard_map/attention_back/pallas_call | solution.py:514
  341.9 9.4 %embed_back.1 = (bf16[504,768]{1,0:T(8,128)(2,1)}, f32[16,48,96]{2,1,0:T(8,128)}, f32[16,48,96]{2,1,0:T(8,128)}) custom-call(s32[2]{0:T(128)} %pad_add_fusion.where_ref, bf16[768,768]{1,0:T(8,128)(2,1)} %constant_dynamic-update-slice_fusion.11.refs_0_, bf16[768,768]{1,0:T(8,128)(2,1)} %collective-permute-done.14.refs_1_, ...), custom_call_target="tpu_custom_call" | custom-call | bytes 1024 | tf_op jit(solution)/shard_map/embed_back/pallas_call | solution.py:276
  356.1 7.9 %unit_grads.8 = (f32[1536,384]{1,0:T(8,128)}, f32[1536,384]{1,0:T(8,128)}) custom-call(s32[2]{0:T(128)} %pad_add_fusion.where_ref, bf16[504,768]{1,0:T(8,128)(2,1)} %get-tuple-element.219.refs_0_.refs_1_.refs_2_, bf16[504,768]{1,0:T(8,128)(2,1)} %get-tuple-element.219.refs_0_.refs_1_.refs_2_, bf16[504,768]{1,0:T(8,128)(2,1)} %get-tuple-element.219.refs_0_.refs_1_.refs_2_, ...), custom_call_target="tpu_custom_call" | custom-call | bytes 1024 | tf_op jit(solution)/shard_map/unit_grads/pallas_call | solution.py:362
  368.5 7.8 %unit_grads.9 = (f32[1536,384]{1,0:T(8,128)}, f32[1536,384]{1,0:T(8,128)}) custom-call(s32[2]{0:T(128)} %pad_add_fusion.where_ref, bf16[504,768]{1,0:T(8,128)(2,1)} %get-tuple-element.219.refs_0_.refs_1_.refs_2_, bf16[504,768]{1,0:T(8,128)(2,1)} %get-tuple-element.219.refs_0_.refs_1_.refs_2_, bf16[504,768]{1,0:T(8,128)(2,1)} %get-tuple-element.219.refs_0_.refs_1_.refs_2_, ...), custom_call_target="tpu_custom_call" | custom-call | bytes 1024 | tf_op jit(solution)/shard_map/unit_grads/pallas_call | solution.py:362
  376.3 11.2 %collective-permute-done.42 = f32[384,384]{1,0:T(8,128)} collective-permute-done((f32[384,384]{1,0:T(8,128)}, f32[384,384]{1,0:T(8,128)}, u32[]{:S(2)}, u32[]{:S(2)}) %collective-permute-start.42) | collective-permute-done | bytes 589856 | tf_op jit(solution)/shard_map/ppermute | solution.py:119
  388.6 19.9 %collective-permute-done.43 = f32[768,384]{1,0:T(8,128)} collective-permute-done((f32[768,384]{1,0:T(8,128)S(1)}, f32[768,384]{1,0:T(8,128)}, u32[]{:S(2)}, u32[]{:S(2)}) %collective-permute-start.43) | collective-permute-done | bytes 1179680 | tf_op jit(solution)/shard_map/ppermute | solution.py:119
  416.0 20.6 %collective-permute-done.47 = f32[8,48,96]{2,1,0:T(8,128)S(1)} collective-permute-done((f32[8,48,96]{2,1,0:T(8,128)S(1)}, f32[8,48,96]{2,1,0:T(8,128)S(1)}, u32[]{:S(2)}, u32[]{:S(2)}) %collective-permute-start.47) | collective-permute-done | bytes 147488 | tf_op jit(solution)/shard_map/ppermute | solution.py:119
  448.0 10.9 %collective-permute-done.44 = f32[384,384]{1,0:T(8,128)S(1)} collective-permute-done((f32[384,384]{1,0:T(8,128)S(1)}, f32[384,384]{1,0:T(8,128)S(1)}, u32[]{:S(2)}, u32[]{:S(2)}) %collective-permute-start.44) | collective-permute-done | bytes 589856 | tf_op jit(solution)/shard_map/ppermute | solution.py:119
  460.2 8.9 %collective-permute-done.53 = f32[768,384]{1,0:T(8,128)S(1)} collective-permute-done((f32[768,384]{1,0:T(8,128)S(1)}, f32[768,384]{1,0:T(8,128)S(1)}, u32[]{:S(2)}, u32[]{:S(2)}) %collective-permute-start.53) | collective-permute-done | bytes 1179680 | tf_op jit(solution)/shard_map/ppermute | solution.py:119
  525.3 7.8 %collective-permute-done.63 = f32[96,384]{1,0:T(8,128)S(1)} collective-permute-done((f32[96,384]{1,0:T(8,128)S(1)}, f32[96,384]{1,0:T(8,128)S(1)}, u32[]{:S(2)}, u32[]{:S(2)}) %collective-permute-start.63) | collective-permute-done | bytes 147488 | tf_op jit(solution)/shard_map/ppermute | solution.py:119
  (349 shorter events, 274.8 us)
Async XLA Ops:
  7.2 226.8 %all-gather.2.cloned.1.call-start = ((), (), s32[]{:S(2)}) async-start(), calls=%async_computation.1 | async-start | bytes 9732096 | tf_op jit(solution)/shard_map/all_gather | solution.py:850
  9.8 472.3 %reduce-scatter.2.cloned.1.call-start = ((), (), s32[]{:S(2)}) async-start(), calls=%async_computation.2 | async-start | bytes 9732096 | tf_op jit(solution)/shard_map/reduce_scatter | solution.py:941
  64.6 30.7 %collective-permute-start.16 = (bf16[192,768]{1,0:T(8,128)(2,1)S(1)}, bf16[192,768]{1,0:T(8,128)(2,1)S(1)}, u32[]{:S(2)}, u32[]{:S(2)}) collective-permute-start(bf16[192,768]{1,0:T(8,128)(2,1)S(1)} %pad_maximum_fusion.13), channel_id=1, source_target_pairs={{0,2},{1,3},{2,0},{3,1},{4,6},{5,7},{6,4},{7,5},{8,10},{9,11},{10,... | collective-permute-start | bytes 884744 | tf_op jit(solution)/shard_map/ppermute | solution.py:119
  72.7 61.5 %collective-permute-start.8 = (bf16[768,768]{1,0:T(8,128)(2,1)S(1)}, bf16[768,768]{1,0:T(8,128)(2,1)}, u32[]{:S(2)}, u32[]{:S(2)}) collective-permute-start(bf16[768,768]{1,0:T(8,128)(2,1)S(1)} %pad_maximum_fusion.2.refs_0_), channel_id=1, source_target_pairs={{0,16},{8,24},{16,0},{24,8},{1,17},{9,25},{17,1},{25,9},{2,18},{10... | collective-permute-start | bytes 3538952 | tf_op jit(solution)/shard_map/ppermute | solution.py:119
  76.8 54.2 %collective-permute-start.13 = (bf16[384,768]{1,0:T(8,128)(2,1)S(1)}, bf16[384,768]{1,0:T(8,128)(2,1)S(1)}, u32[]{:S(2)}, u32[]{:S(2)}) collective-permute-start(bf16[384,768]{1,0:T(8,128)(2,1)S(1)} %pad_maximum_fusion.5), channel_id=1, source_target_pairs={{0,16},{8,24},{16,0},{24,8},{1,17},{9,25},{17,1},{25,9},{2,18},{10... | collective-permute-start | bytes 1769480 | tf_op jit(solution)/shard_map/ppermute | solution.py:119
  95.4 36.6 %collective-permute-start.17 = (bf16[384,768]{1,0:T(8,128)(2,1)S(1)}, bf16[384,768]{1,0:T(8,128)(2,1)S(1)}, u32[]{:S(2)}, u32[]{:S(2)}) collective-permute-start(bf16[384,768]{1,0:T(8,128)(2,1)S(1)} %pad_maximum_fusion.6), channel_id=1, source_target_pairs={{0,1},{1,0},{2,3},{3,2},{4,5},{5,4},{6,7},{7,6},{8,9},{9,8},{10,11... | collective-permute-start | bytes 1769480 | tf_op jit(solution)/shard_map/ppermute | solution.py:119
  104.2 29.6 %collective-permute-start.28 = (bf16[192,768]{1,0:T(8,128)(2,1)S(1)}, bf16[192,768]{1,0:T(8,128)(2,1)S(1)}, u32[]{:S(2)}, u32[]{:S(2)}) collective-permute-start(bf16[192,768]{1,0:T(8,128)(2,1)S(1)} %pad_maximum_fusion.16), channel_id=1, source_target_pairs={{0,2},{1,3},{2,0},{3,1},{4,6},{5,7},{6,4},{7,5},{8,10},{9,11},{10,... | collective-permute-start | bytes 884744 | tf_op jit(solution)/shard_map/ppermute | solution.py:119
  108.2 35.6 %collective-permute-start.25 = (bf16[384,768]{1,0:T(8,128)(2,1)}, bf16[384,768]{1,0:T(8,128)(2,1)}, u32[]{:S(2)}, u32[]{:S(2)}) collective-permute-start(bf16[384,768]{1,0:T(8,128)(2,1)} %pad_maximum_fusion.7), channel_id=1, source_target_pairs={{0,16},{8,24},{16,0},{24,8},{1,17},{9,25},{17,1},{25,9},{2,18},{10... | collective-permute-start | bytes 1769480 | tf_op jit(solution)/shard_map/ppermute | solution.py:119
  131.9 36.2 %collective-permute-start.14 = (bf16[768,768]{1,0:T(8,128)(2,1)}, bf16[768,768]{1,0:T(8,128)(2,1)}, u32[]{:S(2)}, u32[]{:S(2)}) collective-permute-start(bf16[768,768]{1,0:T(8,128)(2,1)} %constant_dynamic-update-slice_fusion.11.refs_0_), channel_id=1, source_target_pairs={{0,1},{1,0},{2,3},{3,2},{4,5},{5,4},{6,7},{7,6},{8,9},{9,8},{10,11... | collective-permute-start | bytes 3538952 | tf_op jit(solution)/shard_map/ppermute | solution.py:119
  133.8 34.3 %collective-permute-start.18 = (bf16[768,768]{1,0:T(8,128)(2,1)S(1)}, bf16[768,768]{1,0:T(8,128)(2,1)S(1)}, u32[]{:S(2)}, u32[]{:S(2)}) collective-permute-start(bf16[768,768]{1,0:T(8,128)(2,1)S(1)} %constant_dynamic-update-slice_fusion.14.refs_0_), channel_id=1, source_target_pairs={{0,16},{8,24},{16,0},{24,8},{1,17},{9,25},{17,1},{25,9},{2,18},{10... | collective-permute-start | bytes 3538952 | tf_op jit(solution)/shard_map/ppermute | solution.py:119
  143.8 29.9 %collective-permute-start.29 = (bf16[384,768]{1,0:T(8,128)(2,1)}, bf16[384,768]{1,0:T(8,128)(2,1)}, u32[]{:S(2)}, u32[]{:S(2)}) collective-permute-start(bf16[384,768]{1,0:T(8,128)(2,1)} %pad_maximum_fusion.8), channel_id=1, source_target_pairs={{0,1},{1,0},{2,3},{3,2},{4,5},{5,4},{6,7},{7,6},{8,9},{9,8},{10,11... | collective-permute-start | bytes 1769480 | tf_op jit(solution)/shard_map/ppermute | solution.py:119
  151.5 47.0 %collective-permute-start.26 = (bf16[768,768]{1,0:T(8,128)(2,1)}, bf16[768,768]{1,0:T(8,128)(2,1)}, u32[]{:S(2)}, u32[]{:S(2)}) collective-permute-start(bf16[768,768]{1,0:T(8,128)(2,1)} %constant_dynamic-update-slice_fusion.17.refs_4_), channel_id=1, source_target_pairs={{0,1},{1,0},{2,3},{3,2},{4,5},{5,4},{6,7},{7,6},{8,9},{9,8},{10,11... | collective-permute-start | bytes 3538952 | tf_op jit(solution)/shard_map/ppermute | solution.py:119
  175.7 27.4 %collective-permute-start.30 = (bf16[768,768]{1,0:T(8,128)(2,1)}, bf16[768,768]{1,0:T(8,128)(2,1)}, u32[]{:S(2)}, u32[]{:S(2)}) collective-permute-start(bf16[768,768]{1,0:T(8,128)(2,1)} %constant_dynamic-update-slice_fusion.20.refs_8_), channel_id=1, source_target_pairs={{0,16},{8,24},{16,0},{24,8},{1,17},{9,25},{17,1},{25,9},{2,18},{10... | collective-permute-start | bytes 3538952 | tf_op jit(solution)/shard_map/ppermute | solution.py:119
  176.0 27.6 %collective-permute-start.19 = (bf16[768,768]{1,0:T(8,128)(2,1)S(1)}, bf16[768,768]{1,0:T(8,128)(2,1)S(1)}, u32[]{:S(2)}, u32[]{:S(2)}) collective-permute-start(bf16[768,768]{1,0:T(8,128)(2,1)S(1)} %constant_dynamic-update-slice_fusion.14.refs_0_), channel_id=1, source_target_pairs={{0,8},{8,0},{16,24},{24,16},{1,9},{9,1},{17,25},{25,17},{2,10},{10... | collective-permute-start | bytes 3538952 | tf_op jit(solution)/shard_map/ppermute | solution.py:119
  178.9 25.2 %collective-permute-start.20 = (bf16[768,768]{1,0:T(8,128)(2,1)S(1)}, bf16[768,768]{1,0:T(8,128)(2,1)}, u32[]{:S(2)}, u32[]{:S(2)}) collective-permute-start(bf16[768,768]{1,0:T(8,128)(2,1)S(1)} %collective-permute-done.18.refs_1_), channel_id=1, source_target_pairs={{0,8},{8,0},{16,24},{24,16},{1,9},{9,1},{17,25},{25,17},{2,10},{10... | collective-permute-start | bytes 3538952 | tf_op jit(solution)/shard_map/ppermute | solution.py:119
  320.3 31.1 %collective-permute-start.38 = (f32[768,384]{1,0:T(8,128)}, f32[768,384]{1,0:T(8,128)}, u32[]{:S(2)}, u32[]{:S(2)}) collective-permute-start(f32[768,384]{1,0:T(8,128)} %get-tuple-element.213), channel_id=1, source_target_pairs={{0,16},{8,24},{16,0},{24,8},{1,17},{9,25},{17,1},{25,9},{2,18},{10... | collective-permute-start | bytes 3538952 | tf_op jit(solution)/shard_map/ppermute | solution.py:119
  320.4 33.4 %collective-permute-start.39 = (f32[768,384]{1,0:T(8,128)}, f32[768,384]{1,0:T(8,128)}, u32[]{:S(2)}, u32[]{:S(2)}) collective-permute-start(f32[768,384]{1,0:T(8,128)} %get-tuple-element.216), channel_id=1, source_target_pairs={{0,1},{1,0},{2,3},{3,2},{4,5},{5,4},{6,7},{7,6},{8,9},{9,8},{10,11... | collective-permute-start | bytes 3538952 | tf_op jit(solution)/shard_map/ppermute | solution.py:119
  365.9 44.1 %collective-permute-start.41 = (f32[1536,384]{1,0:T(8,128)}, f32[1536,384]{1,0:T(8,128)}, u32[]{:S(2)}, u32[]{:S(2)}) collective-permute-start(f32[1536,384]{1,0:T(8,128)} %get-tuple-element.223), channel_id=1, source_target_pairs={{0,8},{8,0},{16,24},{24,16},{1,9},{9,1},{17,25},{25,17},{2,10},{10... | collective-permute-start | bytes 7077896 | tf_op jit(solution)/shard_map/ppermute | solution.py:119
  366.3 42.2 %collective-permute-start.43 = (f32[768,384]{1,0:T(8,128)S(1)}, f32[768,384]{1,0:T(8,128)}, u32[]{:S(2)}, u32[]{:S(2)}) collective-permute-start(f32[768,384]{1,0:T(8,128)S(1)} %copy-done.24), channel_id=1, source_target_pairs={{0,16},{8,24},{16,0},{24,8},{1,17},{9,25},{17,1},{25,9},{2,18},{10... | collective-permute-start | bytes 3538952 | tf_op jit(solution)/shard_map/ppermute | solution.py:119
  412.4 24.3 %collective-permute-start.45 = (f32[1536,384]{1,0:T(8,128)S(1)}, f32[1536,384]{1,0:T(8,128)S(1)}, u32[]{:S(2)}, u32[]{:S(2)}) collective-permute-start(f32[1536,384]{1,0:T(8,128)S(1)} %copy-done.37), channel_id=1, source_target_pairs={{0,8},{8,0},{16,24},{24,16},{1,9},{9,1},{17,25},{25,17},{2,10},{10... | collective-permute-start | bytes 7077896 | tf_op jit(solution)/shard_map/ppermute | solution.py:119
  440.0 29.1 %collective-permute-start.53 = (f32[768,384]{1,0:T(8,128)S(1)}, f32[768,384]{1,0:T(8,128)S(1)}, u32[]{:S(2)}, u32[]{:S(2)}) collective-permute-start(f32[768,384]{1,0:T(8,128)S(1)} %get-tuple-element.252), channel_id=1, source_target_pairs={{0,16},{8,24},{16,0},{24,8},{1,17},{9,25},{17,1},{25,9},{2,18},{10... | collective-permute-start | bytes 3538952 | tf_op jit(solution)/shard_map/ppermute | solution.py:119
  447.9 34.1 %collective-permute-start.54 = (f32[768,384]{1,0:T(8,128)S(1)}, f32[768,384]{1,0:T(8,128)S(1)}, u32[]{:S(2)}, u32[]{:S(2)}) collective-permute-start(f32[768,384]{1,0:T(8,128)S(1)} %get-tuple-element.254), channel_id=1, source_target_pairs={{0,1},{1,0},{2,3},{3,2},{4,5},{5,4},{6,7},{7,6},{8,9},{9,8},{10,11... | collective-permute-start | bytes 3538952 | tf_op jit(solution)/shard_map/ppermute | solution.py:119
  515.8 40.1 %collective-permute-start.74 = (f32[96,1920]{1,0:T(8,128)}, f32[96,1920]{1,0:T(8,128)}, u32[]{:S(2)}, u32[]{:S(2)}) collective-permute-start(f32[96,1920]{1,0:T(8,128)} %get-tuple-element.346), channel_id=1, source_target_pairs={{0,16},{8,24},{16,0},{24,8},{1,17},{9,25},{17,1},{25,9},{2,18},{10... | collective-permute-start | bytes 2211848 | tf_op jit(solution)/shard_map/ppermute | solution.py:119
  517.3 41.7 %collective-permute-start.73 = (f32[96,1920]{1,0:T(8,128)}, f32[96,1920]{1,0:T(8,128)}, u32[]{:S(2)}, u32[]{:S(2)}) collective-permute-start(f32[96,1920]{1,0:T(8,128)} %get-tuple-element.346), channel_id=1, source_target_pairs={{0,8},{8,0},{16,24},{24,16},{1,9},{9,1},{17,25},{25,17},{2,10},{10... | collective-permute-start | bytes 2211848 | tf_op jit(solution)/shard_map/ppermute | solution.py:119
  (92 other events, 1110.7 us)
Sparse Core Ops, SparseCore 0:
  10.9 115.9 all-gather.1
  309.8 150.5 reduce-scatter.1
